TPU v7x, 32 devices: a whole 2x2x4 slice. The times are simulated.
32 devices in a mesh: head: 4 (over x, core), row: 8 (over z, y).
Axes of the slice: x: 2, y: 2, z: 4, core: 2. Of those that a mesh axis runs over, the one named last changes fastest.
Arguments:
- inputs: bfloat16 [8, 8192, 512], P('row', 'head'), may hold values from -6 to 6
- cotangent: bfloat16 [8, 8192, 512], P('row', 'head'), may hold values from -6 to 6
- segments: int32 [8, 8192], P('row'), may hold values from 0 to 31, never falling along the last dimension, each value on 1 to 1024 neighbouring positions
- feature_matrix: bfloat16 [256, 64], replicated, may hold values from -6 to 6
- w_qkv: float32 [512, 3, 512], P(('head', 'row')), may hold values from -0.25 to 0.25
- w_out: float32 [512, 512], P(('head', 'row')), may hold values from -1 to 1
- w_up: float32 [512, 2048], P(('head', 'row')), may hold values from -0.25 to 0.25
- w_down: float32 [2048, 512], P(('head', 'row')), may hold values from -0.125 to 0.125
- gains: float32 [512, 2], P(('head', 'row')), may hold values from 0.3 to 2.7
- first_qkv: float32 [512, 3, 512], P(('head', 'row')), may hold values from -0.0004272461 to 0.0004272461
- second_qkv: float32 [512, 3, 512], P(('head', 'row')), may hold values from 2.9802324e-11 to 4.768372e-10
- first_out: float32 [512, 512], P(('head', 'row')), may hold values from -0.00021362305 to 0.00021362305
- second_out: float32 [512, 512], P(('head', 'row')), may hold values from 7.6293945e-12 to 1.2207031e-10
- first_up: float32 [512, 2048], P(('head', 'row')), may hold values from -0.00021362305 to 0.00021362305
- second_up: float32 [512, 2048], P(('head', 'row')), may hold values from 7.6293945e-12 to 1.2207031e-10
- first_down: float32 [2048, 512], P(('head', 'row')), may hold values from -0.00030517578 to 0.00030517578
- second_down: float32 [2048, 512], P(('head', 'row')), may hold values from 1.9073486e-11 to 3.0517577e-10
- first_gains: float32 [512, 2], P(('head', 'row')), may hold values from -0.0012207031 to 0.0012207031
- second_gains: float32 [512, 2], P(('head', 'row')), may hold values from 3.0517577e-10 to 4.8828124e-09
- step_count: int32 [], replicated, may hold values from 1 to 20
Outputs:
- out_act: bfloat16 [8, 8192, 512], P('row', 'head')
- input_grad: float32 [8, 8192, 512], P('row', 'head')
- grad_norm: float32 [], replicated
- clipped_qkv: float32 [512, 3, 512], P(('head', 'row'))
- moment_qkv: float32 [512, 3, 512], P(('head', 'row'))
- square_qkv: float32 [512, 3, 512], P(('head', 'row'))
- updated_qkv: float32 [512, 3, 512], P(('head', 'row'))
- clipped_out: float32 [512, 512], P(('head', 'row'))
- moment_out: float32 [512, 512], P(('head', 'row'))
- square_out: float32 [512, 512], P(('head', 'row'))
- updated_out: float32 [512, 512], P(('head', 'row'))
- clipped_up: float32 [512, 2048], P(('head', 'row'))
- moment_up: float32 [512, 2048], P(('head', 'row'))
- square_up: float32 [512, 2048], P(('head', 'row'))
- updated_up: float32 [512, 2048], P(('head', 'row'))
- clipped_down: float32 [2048, 512], P(('head', 'row'))
- moment_down: float32 [2048, 512], P(('head', 'row'))
- square_down: float32 [2048, 512], P(('head', 'row'))
- updated_down: float32 [2048, 512], P(('head', 'row'))
- clipped_gains: float32 [512, 2], P(('head', 'row'))
- moment_gains: float32 [512, 2], P(('head', 'row'))
- square_gains: float32 [512, 2], P(('head', 'row'))
- updated_gains: float32 [512, 2], P(('head', 'row'))
Inputs may be any that keep to these rules, and one draw needn't show every extreme that they name: `segments`: within a packed row segment numbers never fall; each segment spans 1 to 1024 positions and one spans exactly 1024.
All inputs are finite; a program needn't handle non-finite values.
Results may differ from a plain program's by a relative error of at most 0.028.
The roundings to bfloat16 on the way count: a program that leaves them out, or rounds other values in their place, can miss the bound.
Values may be sent and summed in bfloat16 or wider, within the bound.
No kernel may reach another device: no remote copies, remote signals or barrier semaphores. Data moves between devices by JAX's collectives and lax.ppermute only.
A program may use at most 320 MiB of HBM per device.

v0:
```python
from functools import partial

import jax
import jax.numpy as jnp
from jax import lax
from jax.sharding import PartitionSpec as P

D = 512
HD = 64
FEATS = 256
BLOCK = 512


finest_matmul_accuracy = lax.Precision.HIGHEST
norm_eps = 1e-06
beta_first = 0.9
beta_second = 0.999
adam_eps = 1e-08
max_norm = 1.0
matrix_rate = 0.08
output_rate = 0.3
gain_rate = 1.5
matrix_decay = 0.1
contract_last = (((1,), (1,)), ((), ()))
contract_first = (((0,), (0,)), ((), ()))


def rms_scale(values):
    return lax.rsqrt(jnp.mean(values * values, axis=-1, keepdims=True) + norm_eps)


def norm_backward(grad_normed, normed, scale_values):
    return scale_values * (
        grad_normed - normed * jnp.mean(grad_normed * normed, axis=-1, keepdims=True)
    )


def feature_map(projected, feature_matrix):
    feature_scale = HD ** (-0.25)
    logits = (
        jnp.einsum("lhd,md->lhm", projected, feature_matrix, preferred_element_type=jnp.float32)
        * feature_scale
    )
    wide_proj = projected.astype(jnp.float32)
    squares = (
        0.5 * feature_scale * feature_scale * jnp.sum(wide_proj * wide_proj, axis=-1, keepdims=True)
    )
    return jnp.exp(logits - squares) / jnp.sqrt(jnp.float32(FEATS))


def feature_backward(projected, feature_matrix, features, grad_features):
    feature_scale = HD ** (-0.25)
    grad_logits = grad_features.astype(jnp.bfloat16).astype(jnp.float32) * features
    rounded = grad_logits.astype(jnp.bfloat16)
    through = (
        jnp.einsum("lhm,md->lhd", rounded, feature_matrix, preferred_element_type=jnp.float32)
        * feature_scale
    )
    totals = jnp.sum(grad_logits, axis=-1, keepdims=True)
    result = through - feature_scale * feature_scale * projected.astype(jnp.float32) * totals
    return result.astype(jnp.bfloat16)


def block_scores(asking_slice, key_portion, segment_part):
    raw_scores = jnp.einsum(
        "qhm,khm->hqk", asking_slice, key_portion, preferred_element_type=jnp.float32
    )
    position = lax.broadcasted_iota(jnp.int32, (BLOCK, BLOCK), 0)
    column = lax.broadcasted_iota(jnp.int32, (BLOCK, BLOCK), 1)
    allowed = ((position >= column) & (segment_part[:, None] == segment_part[None, :])).astype(
        jnp.float32
    )
    scores = raw_scores.astype(jnp.bfloat16) * allowed.astype(jnp.bfloat16)[None]
    return (scores, allowed)


def state_flags(segment_part, before):
    last_segment = segment_part[BLOCK - 1]
    carry_on = (last_segment == before).astype(jnp.float32)
    chosen = (segment_part == last_segment)[:, None, None]
    return (carry_on, chosen)


def split_blocks(phi_query, phi_key, values, segments):
    length, head_count = (values.shape[0], values.shape[1])
    block_count = length // BLOCK
    previous = jnp.concatenate(
        [jnp.full((1,), -1, jnp.int32), segments[BLOCK - 1 : length - 1 : BLOCK]]
    )
    return (
        phi_query.reshape(block_count, BLOCK, head_count, FEATS),
        phi_key.reshape(block_count, BLOCK, head_count, FEATS),
        values.reshape(block_count, BLOCK, head_count, HD),
        segments.reshape(block_count, BLOCK),
        previous,
    )


def attend_forward(phi_query, phi_key, values, segments):
    length, head_count = (values.shape[0], values.shape[1])
    blocked = split_blocks(phi_query, phi_key, values, segments)

    def one_block(carried, inputs):
        state_matrix, state_sum = carried
        asking_slice, key_portion, value_portion, segment_part, before = inputs
        scores, allowed = block_scores(asking_slice, key_portion, segment_part)
        following_marker_mask = (segment_part == before).astype(jnp.float32)
        memory_matrix_narrow = state_matrix.astype(jnp.bfloat16)
        upper_accrued_whole = jnp.einsum(
            "hqk,khd->qhd", scores, value_portion, preferred_element_type=jnp.float32
        )
        upper_accrued_whole = upper_accrued_whole + following_marker_mask[
            :, None, None
        ] * jnp.einsum(
            "ewx,wxt->ewt", asking_slice, memory_matrix_narrow, preferred_element_type=jnp.float32
        )
        denominator = jnp.sum(scores.astype(jnp.float32), axis=-1).T
        denominator = denominator + following_marker_mask[:, None] * jnp.einsum(
            "qhm,hm->qh",
            asking_slice.astype(jnp.float32),
            state_sum,
            precision=finest_matmul_accuracy,
        )
        result = upper_accrued_whole / denominator[:, :, None]
        carry_on, chosen = state_flags(segment_part, before)
        weighted_values = jnp.where(chosen, key_portion, jnp.zeros_like(key_portion))
        appended_sum = jnp.einsum(
            "gqx,gqr->qxr", weighted_values, value_portion, preferred_element_type=jnp.float32
        )
        next_matrix = carry_on * state_matrix + appended_sum.astype(jnp.bfloat16).astype(
            jnp.float32
        )
        next_sum = carry_on * state_sum + jnp.sum(weighted_values.astype(jnp.float32), axis=0)
        return ((next_matrix, next_sum), (result, denominator, memory_matrix_narrow, state_sum))

    initial = (
        jnp.zeros((head_count, FEATS, HD), jnp.float32),
        jnp.zeros((head_count, FEATS), jnp.float32),
    )
    finals, (results, denominators, matrices, sums) = lax.scan(one_block, initial, blocked)
    return (
        results.reshape(length, head_count, HD),
        denominators.reshape(length, head_count),
        matrices,
        sums,
    )


def attend_backward(
    phi_query, phi_key, values, segments, results, denominators, matrices, sums, grad_results
):
    length, head_count = (values.shape[0], values.shape[1])
    block_count = length // BLOCK
    blocked = split_blocks(phi_query, phi_key, values, segments) + (
        results.reshape(block_count, BLOCK, head_count, HD),
        denominators.reshape(block_count, BLOCK, head_count),
        matrices,
        sums,
        grad_results.reshape(block_count, BLOCK, head_count, HD),
    )

    def one_block(carried, inputs):
        grad_matrix, grad_sum = carried
        (
            asking_slice,
            key_portion,
            value_portion,
            segment_part,
            before,
            result,
            denominator,
            memory_matrix_narrow,
            state_sum,
            grad_result,
        ) = inputs
        scores, allowed = block_scores(asking_slice, key_portion, segment_part)
        following_marker_mask = (segment_part == before).astype(jnp.float32)
        grad_numerator = (grad_result / denominator[:, :, None]).astype(jnp.bfloat16)
        grad_denominator = -jnp.sum(grad_result * result, axis=-1) / denominator
        grad_scores = jnp.einsum(
            "qhd,khd->hqk", grad_numerator, value_portion, preferred_element_type=jnp.float32
        )
        grad_scores = ((grad_scores + grad_denominator.T[:, :, None]) * allowed[None]).astype(
            jnp.bfloat16
        )
        grad_query = jnp.einsum(
            "hqk,khm->qhm", grad_scores, key_portion, preferred_element_type=jnp.float32
        )
        grad_key = jnp.einsum(
            "hqk,qhm->khm", grad_scores, asking_slice, preferred_element_type=jnp.float32
        )
        grad_value = jnp.einsum(
            "hqk,qhd->khd", scores, grad_numerator, preferred_element_type=jnp.float32
        )
        upper_kept_running = (
            grad_numerator * following_marker_mask.astype(jnp.bfloat16)[:, None, None]
        )
        denominator_part = grad_denominator * following_marker_mask[:, None]
        grad_query = grad_query + jnp.einsum(
            "owf,wrf->owr",
            upper_kept_running,
            memory_matrix_narrow,
            preferred_element_type=jnp.float32,
        )
        grad_query = grad_query + denominator_part[:, :, None] * state_sum[None]
        carry_on, chosen = state_flags(segment_part, before)
        chosen_wide = chosen.astype(jnp.float32)
        gradient_lowered = grad_matrix.astype(jnp.bfloat16)
        grad_key = grad_key + chosen_wide * (
            jnp.einsum(
                "gfa,fxa->gfx", value_portion, gradient_lowered, preferred_element_type=jnp.float32
            )
            + grad_sum[None]
        )
        grad_value = grad_value + chosen_wide * jnp.einsum(
            "wjy,jyf->wjf", key_portion, gradient_lowered, preferred_element_type=jnp.float32
        )
        prior_matrix = carry_on * grad_matrix + jnp.einsum(
            "mrc,mry->rcy", asking_slice, upper_kept_running, preferred_element_type=jnp.float32
        )
        prior_sum = carry_on * grad_sum + jnp.einsum(
            "qhm,qh->hm",
            asking_slice.astype(jnp.float32),
            denominator_part,
            precision=finest_matmul_accuracy,
        )
        return ((prior_matrix, prior_sum), (grad_query, grad_key, grad_value))

    initial = (
        jnp.zeros((head_count, FEATS, HD), jnp.float32),
        jnp.zeros((head_count, FEATS), jnp.float32),
    )
    finals, (grad_query, grad_key, grad_value) = lax.scan(one_block, initial, blocked, reverse=True)
    return (
        grad_query.reshape(length, head_count, FEATS),
        grad_key.reshape(length, head_count, FEATS),
        grad_value.reshape(length, head_count, HD),
    )


def adam_update(
    weight, gradient, first_moment, second_moment, clip_factor, step_value, step_rate, decay_rate
):
    clipped = gradient * clip_factor
    next_first = beta_first * first_moment + (1.0 - beta_first) * clipped
    next_second = beta_second * second_moment + (1.0 - beta_second) * clipped * clipped
    first_hat = next_first / (1.0 - beta_first**step_value)
    second_hat = next_second / (1.0 - beta_second**step_value)
    updated = weight - step_rate * (
        first_hat / (jnp.sqrt(second_hat) + adam_eps) + decay_rate * weight
    )
    return (clipped, next_first, next_second, updated)


def per_device(
    inputs,
    cotangent,
    segments,
    feature_matrix,
    w_qkv,
    w_out,
    w_up,
    w_down,
    gains,
    first_qkv,
    second_qkv,
    first_out,
    second_out,
    first_up,
    second_up,
    first_down,
    second_down,
    first_gains,
    second_gains,
    step_count,
):
    columns = D // lax.axis_size("head")
    head_count = columns // HD
    head_start = lax.axis_index("head") * columns
    gathered = (
        lax.all_gather(w_qkv.astype(jnp.bfloat16), ("head", "row"), axis=0, tiled=True),
        lax.all_gather(w_out.astype(jnp.bfloat16), ("head", "row"), axis=0, tiled=True),
        lax.all_gather(w_up.astype(jnp.bfloat16), ("head", "row"), axis=0, tiled=True),
        lax.all_gather(w_down.astype(jnp.bfloat16), ("head", "row"), axis=0, tiled=True),
        lax.all_gather(gains.astype(jnp.bfloat16), ("head", "row"), axis=0, tiled=True),
    )
    qkv_full, out_full, up_full, down_full, gains_full = gathered
    gain_first = gains_full[:, 0].astype(jnp.float32)
    gain_second = gains_full[:, 1].astype(jnp.float32)
    row_segments = segments[0]
    values_in = inputs[0].astype(jnp.float32)
    scale_first = rms_scale(values_in)
    normed_first = values_in * scale_first
    hidden_first = (normed_first * gain_first).astype(jnp.bfloat16)
    hidden_rows = lax.all_gather(hidden_first, "head", axis=0, tiled=True)
    qkv_own = lax.dynamic_slice_in_dim(qkv_full, head_start, columns, 2)
    projected = jnp.einsum(
        "ld,dcf->lcf", hidden_rows, qkv_own, preferred_element_type=jnp.float32
    ).astype(jnp.bfloat16)
    length = projected.shape[0]
    query_proj = projected[:, 0].reshape(length, head_count, HD)
    key_proj = projected[:, 1].reshape(length, head_count, HD)
    value_proj = projected[:, 2].reshape(length, head_count, HD)
    features_query = feature_map(query_proj, feature_matrix)
    features_key = feature_map(key_proj, feature_matrix)
    phi_query = features_query.astype(jnp.bfloat16)
    phi_key = features_key.astype(jnp.bfloat16)
    results, denominators, matrices, sums = attend_forward(
        phi_query, phi_key, value_proj, row_segments
    )
    attended = results.astype(jnp.bfloat16).reshape(length, columns)
    out_own = lax.dynamic_slice_in_dim(out_full, head_start, columns, 1)
    partial_branch = lax.dot_general(
        attended, out_own, contract_last, preferred_element_type=jnp.float32
    )
    branch = lax.psum_scatter(partial_branch, "head", scatter_dimension=0, tiled=True)
    middle = values_in + branch
    later_norm_factor = rms_scale(middle)
    normed_second = middle * later_norm_factor
    hidden_second = (normed_second * gain_second).astype(jnp.bfloat16)
    upward = jnp.dot(hidden_second, up_full, preferred_element_type=jnp.float32)
    activated_wide, gelu_pull = jax.vjp(partial(jax.nn.gelu, approximate=False), upward)
    activated = activated_wide.astype(jnp.bfloat16)
    output = (middle + jnp.dot(activated, down_full, preferred_element_type=jnp.float32)).astype(
        jnp.bfloat16
    )
    grad_output = cotangent[0]
    grad_activated = lax.dot_general(
        grad_output, down_full, contract_last, preferred_element_type=jnp.float32
    )
    grad_down = lax.dot_general(
        activated, grad_output, contract_first, preferred_element_type=jnp.float32
    )
    grad_upward = gelu_pull(grad_activated)[0].astype(jnp.bfloat16)
    grad_up = lax.dot_general(
        hidden_second, grad_upward, contract_first, preferred_element_type=jnp.float32
    )
    grad_hidden_second = lax.dot_general(
        grad_upward, up_full, contract_last, preferred_element_type=jnp.float32
    )
    gain_grad_second = jnp.sum(grad_hidden_second * normed_second, axis=0)
    grad_middle = grad_output.astype(jnp.float32) + norm_backward(
        grad_hidden_second * gain_second, normed_second, later_norm_factor
    )
    grad_branch = grad_middle.astype(jnp.bfloat16)
    grad_rows = lax.all_gather(grad_branch, "head", axis=0, tiled=True)
    grad_attended = jnp.dot(grad_rows, out_own, preferred_element_type=jnp.float32)
    grad_out_own = lax.dot_general(
        grad_rows, attended, contract_first, preferred_element_type=jnp.float32
    )
    grad_out = lax.dynamic_update_slice_in_dim(
        jnp.zeros((D, D), jnp.float32), grad_out_own, head_start, 1
    )
    grad_phi_query, grad_phi_key, grad_value = attend_backward(
        phi_query,
        phi_key,
        value_proj,
        row_segments,
        results,
        denominators,
        matrices,
        sums,
        grad_attended.reshape(length, head_count, HD),
    )
    grad_query = feature_backward(
        query_proj, feature_matrix, features_query, grad_phi_query
    ).reshape(length, columns)
    grad_key = feature_backward(key_proj, feature_matrix, features_key, grad_phi_key).reshape(
        length, columns
    )
    grad_projected = jnp.stack(
        [grad_query, grad_key, grad_value.astype(jnp.bfloat16).reshape(length, columns)], axis=1
    )
    grad_qkv_own = jnp.einsum(
        "ld,lcf->dcf", hidden_rows, grad_projected, preferred_element_type=jnp.float32
    )
    grad_qkv = lax.dynamic_update_slice_in_dim(
        jnp.zeros((D, 3, D), jnp.float32), grad_qkv_own, head_start, 2
    )
    partial_input = jnp.einsum(
        "lcf,dcf->ld", grad_projected, qkv_own, preferred_element_type=jnp.float32
    )
    grad_hidden_first = lax.psum_scatter(
        partial_input.astype(jnp.bfloat16), "head", scatter_dimension=0, tiled=True
    ).astype(jnp.float32)
    gain_grad_first = jnp.sum(grad_hidden_first * normed_first, axis=0)
    grad_inputs = grad_middle + norm_backward(
        grad_hidden_first * gain_first, normed_first, scale_first
    )
    grad_gains = jnp.stack([gain_grad_first, gain_grad_second], axis=1)
    reduced = (
        lax.psum_scatter(grad_qkv, ("head", "row"), scatter_dimension=0, tiled=True),
        lax.psum_scatter(grad_out, ("head", "row"), scatter_dimension=0, tiled=True),
        lax.psum_scatter(grad_up, ("head", "row"), scatter_dimension=0, tiled=True),
        lax.psum_scatter(grad_down, ("head", "row"), scatter_dimension=0, tiled=True),
        lax.psum_scatter(grad_gains, ("head", "row"), scatter_dimension=0, tiled=True),
    )
    local_squares = jnp.float32(0.0)
    for gradient in reduced:
        local_squares = local_squares + jnp.sum(gradient * gradient)
    total_squares = lax.psum(local_squares, ("head", "row"))
    grad_norm = jnp.sqrt(total_squares)
    clip_factor = jnp.minimum(1.0, max_norm / (grad_norm + 1e-06))
    step_value = step_count.astype(jnp.float32)
    qkv_parts = adam_update(
        w_qkv, reduced[0], first_qkv, second_qkv, clip_factor, step_value, matrix_rate, matrix_decay
    )
    out_parts = adam_update(
        w_out, reduced[1], first_out, second_out, clip_factor, step_value, output_rate, matrix_decay
    )
    up_parts = adam_update(
        w_up, reduced[2], first_up, second_up, clip_factor, step_value, matrix_rate, matrix_decay
    )
    down_parts = adam_update(
        w_down,
        reduced[3],
        first_down,
        second_down,
        clip_factor,
        step_value,
        matrix_rate,
        matrix_decay,
    )
    gain_parts = adam_update(
        gains, reduced[4], first_gains, second_gains, clip_factor, step_value, gain_rate, 0.0
    )
    return (
        output[None],
        grad_inputs[None],
        grad_norm,
        qkv_parts[0],
        qkv_parts[1],
        qkv_parts[2],
        qkv_parts[3],
        out_parts[0],
        out_parts[1],
        out_parts[2],
        out_parts[3],
        up_parts[0],
        up_parts[1],
        up_parts[2],
        up_parts[3],
        down_parts[0],
        down_parts[1],
        down_parts[2],
        down_parts[3],
        gain_parts[0],
        gain_parts[1],
        gain_parts[2],
        gain_parts[3],
    )


def solution(mesh):
    placed = (
        P("row", "head", None),
        P("row", "head", None),
        P("row", None),
        P(),
        P(("head", "row"), None, None),
        P(("head", "row"), None),
        P(("head", "row"), None),
        P(("head", "row"), None),
        P(("head", "row"), None),
        P(("head", "row"), None, None),
        P(("head", "row"), None, None),
        P(("head", "row"), None),
        P(("head", "row"), None),
        P(("head", "row"), None),
        P(("head", "row"), None),
        P(("head", "row"), None),
        P(("head", "row"), None),
        P(("head", "row"), None),
        P(("head", "row"), None),
        P(),
    )
    return jax.shard_map(
        per_device,
        mesh=mesh,
        in_specs=placed,
        out_specs=(
            P("row", "head", None),
            P("row", "head", None),
            P(),
            P(("head", "row"), None, None),
            P(("head", "row"), None, None),
            P(("head", "row"), None, None),
            P(("head", "row"), None, None),
            P(("head", "row"), None),
            P(("head", "row"), None),
            P(("head", "row"), None),
            P(("head", "row"), None),
            P(("head", "row"), None),
            P(("head", "row"), None),
            P(("head", "row"), None),
            P(("head", "row"), None),
            P(("head", "row"), None),
            P(("head", "row"), None),
            P(("head", "row"), None),
            P(("head", "row"), None),
            P(("head", "row"), None),
            P(("head", "row"), None),
            P(("head", "row"), None),
            P(("head", "row"), None),
        ),
        check_vma=False,
    )
```

profile of v0, /device:TPU:0, one launch (start us, length us, event | category | flops | bytes accessed | tf_op | source)
XLA Modules:
  0.0 1833.7 jit_solution(17276187479510351741)
XLA Ops:
  9.6 69.3 %all-gather = bf16[32,16,2]{1,2,0:T(2,128)(2,1)S(1)} all-gather(bf16[1,16,2]{1,2,0:T(2,128)(2,1)S(1)} %convert_bitcast_fusion), channel_id=1, replica_groups=mesh['head'=4,'row'=8] {'head','row'}, dimensions={0}, use_global_device_ids=true | all-gather | bytes 2112 | tf_op jit(solution)/shard_map/all_gather | solution.py:285
  86.7 67.8 %all_gather.24 = bf16[512,512]{1,0:T(8,128)(2,1)S(1)} all-gather(bf16[16,512]{1,0:T(8,128)(2,1)S(1)} %convert_element_type.334), channel_id=1, replica_groups=mesh['head'=4,'row'=8] {'head','row'}, dimensions={0}, use_global_device_ids=true | all-gather | bytes 540672 | tf_op jit(solution)/shard_map/all_gather | solution.py:282
  156.0 11.7 fusion.165
  167.7 8.1 convert_element_type.327
  179.7 9.9 fusion.164
  197.7 9.9 fusion.163
  209.7 224.3 %while.46 = (s32[]{:T(128)}, f32[2,256,64]{1,2,0:T(8,128)S(1)}, f32[2,256]{1,0:T(2,128)S(1)}, f32[16,512,2,64]{1,3,2,0:T(8,128)}, f32[16,512,2]{1,2,0:T(2,128)},...) while((s32[]{:T(128)}, f32[2,256,64]{1,2,0:T(8,128)S(1)}, ...), condition=%wide.region_6.7_spmd.clone.clone, body=%wide.region_3.6_spmd.clone.sunk.clone | while | flops 410687488 | bytes 8006353 | solution.py:140
  441.2 8.1 fusion.139
  451.6 122.0 %reduce-scatter.10.cloned.1.call-done = f32[2048,512]{1,0:T(8,128)} async-done(((f32[8192,512]{1,0:T(8,128)}), f32[2048,512]{1,0:T(8,128)}) %reduce-scatter.10.cloned.1.call-update) | async-done | bytes 4194320 | tf_op jit(solution)/shard_map/reduce_scatter | solution.py:316
  578.3 55.7 %all-gather.11.cloned.1.call-done = bf16[512,2048]{1,0:T(8,128)(2,1)} async-done(((bf16[16,2048]{1,0:T(8,128)(2,1)}), bf16[512,2048]{1,0:T(8,128)(2,1)}) %all-gather.11.cloned.1.call-update) | async-done | bytes 2097168 | tf_op jit(solution)/shard_map/all_gather | solution.py:283
  634.1 44.6 %multiply_convert_fusion.1 = (bf16[2048,2048]{1,0:T(8,128)(2,1)}, f32[2048,2048]{1,0:T(8,128)}, f32[2048,2048]{1,0:T(8,128)}) fusion(bf16[512,2048]{1,0:T(8,128)(2,1)} %all-gather.11.cloned.1.call-done, f32[2048,512]{1,0:T(8,128)} %get-tuple-element.673, f32[512]{0:T(512)S(1)} %bitcast.454, f32[2048]{0:T(1024)S(1)} %add_rsqrt_fusion), kind=kOutput, calls=%fused_computation.140 | convolution fusion | flops 4570742784 | bytes 48244736 | tf_op jit(solution)/shard_map/dot_general | solution.py:321
  678.6 14.6 all-gather.13.cloned.1.call-done
  693.3 18.8 %add_convert_fusion = bf16[2048,2048]{1,0:T(8,128)(2,1)} fusion(f32[2048,2048]{1,0:T(8,128)} %get-tuple-element.671, f32[2048,2048]{1,0:T(8,128)} %get-tuple-element.692, bf16[2048,512]{1,0:T(8,128)(2,1)} %all-gather.13.cloned.1.call-done, bf16[1,2048,512]{2,1,0:T(8,128)(2,1)S(1)} %copy-done.13), kind=kOutput, calls=%fused_computation.139 | convolution fusion | flops 4353687552 | bytes 46137344 | tf_op jit(solution)/shard_map/dot_general | solution.py:328
  712.1 11.6 multiply_reduce_fusion
  728.0 11.5 fusion.152
  741.1 9.9 fusion.129
  751.1 34.1 %all-gather.15.cloned.1.call-done = bf16[8192,512]{1,0:T(8,128)(2,1)} async-done(((bf16[2048,512]{1,0:T(8,128)(2,1)}), bf16[8192,512]{1,0:T(8,128)(2,1)}) %all-gather.15.cloned.1.call-update) | async-done | bytes 8388624 | tf_op jit(solution)/shard_map/all_gather | solution.py:346
  805.2 396.5 %while.47 = (s32[]{:T(128)}, f32[2,256,64]{1,2,0:T(8,128)S(1)}, f32[2,256]{1,0:T(2,128)S(1)}, bf16[16,512,2,256]{1,3,2,0:T(8,128)(2,1)}, bf16[16,512,2,256]{1,3,...) while((s32[]{:T(128)}, f32[2,256,64]{1,2,0:T(8,128)S(1)}, ...), condition=%wide.region_12.13_spmd.clone.clone, body=%wide.region_10.12_spmd.clone.sunk.clone | while | flops 1083283456 | bytes 19943700 | solution.py:233
  1201.7 13.0 copy.101
  1214.7 13.2 fusion.112
  1242.4 13.2 copy.102
  1261.5 11.9 fusion.113
  1273.4 15.1 bitcast_multiply_fusion.2
  1300.2 10.8 copy.121
  1319.1 9.8 fusion.132
  1330.6 9.4 bitcast_convert_fusion
  1341.0 11.2 fusion.128
  1355.4 68.4 %reduce-scatter.16.cloned.1.call-done = f32[16,512]{1,0:T(8,128)} async-done(((f32[512,512]{1,0:T(8,128)}), f32[16,512]{1,0:T(8,128)}) %reduce-scatter.16.cloned.1.call-update) | async-done | bytes 32784 | tf_op jit(solution)/shard_map/reduce_scatter | solution.py:393
  1425.1 138.6 %reduce-scatter.14.cloned.1.call-done = f32[16,3,512]{2,0,1:T(8,128)} async-done(((f32[512,3,512]{2,0,1:T(8,128)}), f32[16,3,512]{2,0,1:T(8,128)}) %reduce-scatter.14.cloned.1.call-update) | async-done | bytes 98320 | tf_op jit(solution)/shard_map/reduce_scatter | solution.py:392
  1567.8 67.1 %reduce-scatter.12.cloned.1.call-done = bf16[2048,512]{1,0:T(8,128)(2,1)} async-done(((bf16[8192,512]{1,0:T(8,128)(2,1)}), bf16[2048,512]{1,0:T(8,128)(2,1)}) %reduce-scatter.12.cloned.1.call-update) | async-done | bytes 2097168 | tf_op jit(solution)/shard_map/reduce_scatter | solution.py:383
  1639.3 133.0 %reduce-scatter.22.cloned.1.call-done = f32[16,2]{1,0:T(8,128)} async-done(((f32[512,2]{1,0:T(8,128)}), f32[16,2]{1,0:T(8,128)}) %reduce-scatter.22.cloned.1.call-update) | async-done | bytes 144
  1781.8 36.8 %psum.7 = f32[]{:T(128)} all-reduce(f32[]{:T(128)S(6)} %add.282), channel_id=1, replica_groups=mesh['head'=4,'row'=8] {'head','row'}, use_global_device_ids=true, to_apply=%region_29.30 | all-reduce | flops 1 | bytes 8 | tf_op jit(solution)/shard_map/psum | solution.py:401
  (773 shorter events, 708.5 us)
Async XLA Ops:
  7.2 172.5 %copy-start = (bf16[256,64]{0,1:T(8,128)(2,1)S(1)}, bf16[256,64]{0,1:T(8,128)(2,1)}, u32[]{:S(2)}) copy-start(bf16[256,64]{0,1:T(8,128)(2,1)} %param.27) | copy-start | bytes 98308
  7.2 78.6 %copy-start.40 = (s32[1,8192]{1,0:T(1,128)S(1)}, s32[1,8192]{1,0:T(1,128)}, u32[]{:S(2)}) copy-start(s32[1,8192]{1,0:T(1,128)} %param.26) | copy-start | bytes 98308
  7.2 79.4 %copy-start.32 = (f32[16,512]{1,0:T(8,128)S(1)}, f32[16,512]{1,0:T(8,128)}, u32[]{:S(2)}) copy-start(f32[16,512]{1,0:T(8,128)} %param.29) | copy-start | bytes 98308
  7.2 147.3 %all-gather.9.cloned.1.call-start = ((), (), s32[]{:S(2)}) async-start(), calls=%async_computation.8 | async-start | bytes 1622016 | tf_op jit(solution)/shard_map/all_gather | solution.py:281
  8.8 147.2 %all-gather.7.cloned.1.call-start = ((), (), s32[]{:S(2)}) async-start(), calls=%async_computation.7 | async-start | bytes 10485760 | tf_op jit(solution)/shard_map/all_gather | solution.py:295
  79.0 649.0 %copy-start.43 = (f32[512,1]{0,1:T(1,128)}, f32[512,1]{0,1:T(1,128)S(1)}, u32[]{:S(2)}) copy-start(f32[512,1]{0,1:T(1,128)S(1)} %get-tuple-element.686) | copy-start | bytes 6148
  85.1 488.5 %reduce-scatter.10.cloned.1.call-start = ((), (), s32[]{:S(2)}) async-start(), calls=%async_computation.9 | async-start | bytes 20971520 | tf_op jit(solution)/shard_map/reduce_scatter | solution.py:316
  154.5 285.3 %copy-start.17 = (bf16[512,512]{1,0:T(8,128)(2,1)}, bf16[512,512]{1,0:T(8,128)(2,1)S(1)}, u32[]{:S(2)}) copy-start(bf16[512,512]{1,0:T(8,128)(2,1)S(1)} %all_gather.24) | copy-start | bytes 1572868
  449.3 124.3 %copy-start.6 = (bf16[1,2048,512]{2,1,0:T(8,128)(2,1)S(1)}, bf16[1,2048,512]{2,1,0:T(8,128)(2,1)}, u32[]{:S(2)}) copy-start(bf16[1,2048,512]{2,1,0:T(8,128)(2,1)} %param.24) | copy-start | bytes 6291460
  449.3 184.7 %all-gather.11.cloned.1.call-start = ((), (), s32[]{:S(2)}) async-start(), calls=%async_computation.10 | async-start | bytes 2162688 | tf_op jit(solution)/shard_map/all_gather | solution.py:283
  450.9 242.4 %all-gather.13.cloned.1.call-start = ((), (), s32[]{:S(2)}) async-start(), calls=%async_computation.11 | async-start | bytes 2162688 | tf_op jit(solution)/shard_map/all_gather | solution.py:284
  451.6 333.6 %all-gather.15.cloned.1.call-start = ((), (), s32[]{:S(2)}) async-start(), calls=%async_computation.12 | async-start | bytes 10485760 | tf_op jit(solution)/shard_map/all_gather | solution.py:346
  578.3 149.7 %copy-start.37 = (f32[2048]{0:T(1024)}, f32[2048]{0:T(1024)S(1)}, u32[]{:S(2)}) copy-start(f32[2048]{0:T(1024)S(1)} %add_rsqrt_fusion) | copy-start | bytes 24580
  634.1 59.2 %copy-start.13 = (bf16[1,2048,512]{2,1,0:T(8,128)(2,1)S(1)}, bf16[1,2048,512]{2,1,0:T(8,128)(2,1)}, u32[]{:S(2)}) copy-start(bf16[1,2048,512]{2,1,0:T(8,128)(2,1)} %param.25) | copy-start | bytes 6291460
  727.9 624.4 %reduce-scatter.18.cloned.1.call-start = ((), (), s32[]{:S(2)}) async-start(), calls=%async_computation.16 | async-start | bytes 4325376 | tf_op jit(solution)/shard_map/reduce_scatter | solution.py:394
  739.5 614.3 %reduce-scatter.20.cloned.1.call-start = ((), (), s32[]{:S(2)}) async-start(), calls=%async_computation.17 | async-start | bytes 4325376 | tf_op jit(solution)/shard_map/reduce_scatter | solution.py:395
  751.1 672.7 %reduce-scatter.16.cloned.1.call-start = ((), (), s32[]{:S(2)}) async-start(), calls=%async_computation.15 | async-start | bytes 1081344 | tf_op jit(solution)/shard_map/reduce_scatter | solution.py:393
  1288.5 275.2 %reduce-scatter.14.cloned.1.call-start = ((), (), s32[]{:S(2)}) async-start(), calls=%async_computation.14 | async-start | bytes 3244032 | tf_op jit(solution)/shard_map/reduce_scatter | solution.py:392
  1330.5 304.4 %reduce-scatter.12.cloned.1.call-start = ((), (), s32[]{:S(2)}) async-start(), calls=%async_computation.13 | async-start | bytes 10485760 | tf_op jit(solution)/shard_map/reduce_scatter | solution.py:383
  1340.0 432.3 %reduce-scatter.22.cloned.1.call-start = ((), (), s32[]{:S(2)}) async-start(), calls=%async_computation.18 | async-start | bytes 270336
  1341.0 294.0 %copy-start.7 = (bf16[1,2048,512]{2,1,0:T(8,128)(2,1)S(1)}, bf16[1,2048,512]{2,1,0:T(8,128)(2,1)}, u32[]{:S(2)}) copy-start(bf16[1,2048,512]{2,1,0:T(8,128)(2,1)} %param.24) | copy-start | bytes 6291460
  1341.0 293.9 %copy-start.27 = (f32[2048]{0:T(1024)S(1)}, f32[2048]{0:T(1024)}, u32[]{:S(2)}) copy-start(f32[2048]{0:T(1024)} %copy-done.26) | copy-start | bytes 24580
  1341.0 293.9 %copy-start.42 = (f32[512,1]{0,1:T(1,128)S(1)}, f32[512,1]{0,1:T(1,128)}, u32[]{:S(2)}) copy-start(f32[512,1]{0,1:T(1,128)} %copy-done.41) | copy-start | bytes 6148
  1341.0 296.8 %copy-start.45 = (f32[512]{0:T(512)S(1)}, f32[512]{0:T(512)}, u32[]{:S(2)}) copy-start(f32[512]{0:T(512)} %get-tuple-element.583) | copy-start | bytes 6148
  1341.0 433.3 %copy-start.38 = (f32[2048]{0:T(1024)S(1)}, f32[2048]{0:T(1024)}, u32[]{:S(2)}) copy-start(f32[2048]{0:T(1024)} %copy-done.37) | copy-start | bytes 24580
  1774.4 47.1 %copy-start.21 = (f32[16,2048]{1,0:T(8,128)S(1)}, f32[16,2048]{1,0:T(8,128)}, u32[]{:S(2)}) copy-start(f32[16,2048]{1,0:T(8,128)} %param.30) | copy-start | bytes 393220
  1774.4 47.1 %copy-start.22 = (f32[16,2048]{1,0:T(8,128)S(1)}, f32[16,2048]{1,0:T(8,128)}, u32[]{:S(2)}) copy-start(f32[16,2048]{1,0:T(8,128)} %reduce-scatter.18.cloned.1.call-done) | copy-start | bytes 393220
  1774.5 47.9 %copy-start.33 = (f32[16,512]{1,0:T(8,128)S(1)}, f32[16,512]{1,0:T(8,128)}, u32[]{:S(2)}) copy-start(f32[16,512]{1,0:T(8,128)} %param.29) | copy-start | bytes 98308
  1774.5 47.9 %copy-start.34 = (f32[16,512]{1,0:T(8,128)S(1)}, f32[16,512]{1,0:T(8,128)}, u32[]{:S(2)}) copy-start(f32[16,512]{1,0:T(8,128)} %reduce-scatter.16.cloned.1.call-done) | copy-start | bytes 98308
  1774.5 49.3 %copy-start.24 = (f32[16,3,512]{2,0,1:T(8,128)S(1)}, f32[16,3,512]{2,0,1:T(8,128)}, u32[]{:S(2)}) copy-start(f32[16,3,512]{2,0,1:T(8,128)} %param.28) | copy-start | bytes 294916
  1774.5 49.3 %copy-start.25 = (f32[16,3,512]{2,0,1:T(8,128)S(1)}, f32[16,3,512]{2,0,1:T(8,128)}, u32[]{:S(2)}) copy-start(f32[16,3,512]{2,0,1:T(8,128)} %reduce-scatter.14.cloned.1.call-done) | copy-start | bytes 294916
  1774.5 49.3 %copy-start.36 = (f32[16,3,512]{2,0,1:T(8,128)S(1)}, f32[16,3,512]{2,0,1:T(8,128)}, u32[]{:S(2)}) copy-start(f32[16,3,512]{2,0,1:T(8,128)} %param.34) | copy-start | bytes 294916
  (28 other events, 433.8 us)
Sparse Core Ops, SparseCore 0:
  11.7 57.6 all-gather.8
  85.3 54.6 all-gather.6
  449.5 124.1 reduce-scatter.9
  577.5 56.5 all-gather.10
  637.9 55.3 all-gather.12
  728.0 57.1 all-gather.14
  787.6 143.9 reduce-scatter.17
  934.0 140.9 reduce-scatter.19
  1288.6 135.0 reduce-scatter.15
  1426.4 137.1 reduce-scatter.13
  1566.4 68.4 reduce-scatter.11
  1638.8 133.4 reduce-scatter.21
where the time goes:
time: 1860 us; the launch traced here: 1830 us
  waiting for transfers between devices  634 us (34%)
  matrix products  539 us (29%)
  other arithmetic  226 us (12%)
  local copies, waits for them, and re-layouts  194 us (10%)
  blocking collectives  174 us (9%)
  loops' own time  45 us (2%)
  between operations  21.1 us (1%)
    reduce_scatter x1, waiting for transfers between devices, per_device(): lax.psum_scatter(grad_qkv, ('head', 'row'), scatter_dimension=0, tiled=True)  139 us
    unnamed x13, waiting for transfers between devices  133 us
    reduce_scatter x1, waiting for transfers between devices, per_device(): lax.psum_scatter(partial_branch, 'head', scatter_dimension=0, tiled=True)  122 us
    all_gather x1, blocking collectives, per_device(): lax.all_gather(gains.astype(jnp.bfloat16), ('head', 'row'), axis=0, tiled...  69.3 us
    reduce_scatter x1, waiting for transfers between devices, per_device(): lax.psum_scatter(grad_out, ('head', 'row'), scatter_dimension=0, tiled=True)  68.4 us
    all_gather x1, blocking collectives, per_device(): lax.all_gather(w_out.astype(jnp.bfloat16), ('head', 'row'), axis=0, tiled...  67.8 us
    reduce_scatter x1, waiting for transfers between devices, per_device(): lax.psum_scatter(partial_input.astype(jnp.bfloat16), 'head', scatter_dime...  67.1 us
    all_gather x1, waiting for transfers between devices, per_device(): lax.all_gather(w_up.astype(jnp.bfloat16), ('head', 'row'), axis=0, tiled=...  55.7 us
  transfers between devices with their start and end apart: 12, of which 8 were waited for; matrix products, arithmetic and copies ran while one was open for 34% of the time, Pallas kernels for 0%

commit v1 on v0

v1 whole, which is shorter than its diff:
```python
import math
from functools import partial

import jax
import jax.numpy as jnp
from jax import lax
from jax.experimental import pallas as pl
from jax.experimental.pallas import tpu as pltpu
from jax.sharding import PartitionSpec as P

D = 512
HD = 64
FEATS = 256
FF = 2048
CHUNK = 256
SPAN = 1024
ROWS = 512
PAIRS = D // (2 * HD)

bf16 = jnp.bfloat16
f32 = jnp.float32
norm_eps = 1e-06
beta_first = 0.9
beta_second = 0.999
adam_eps = 1e-08
max_norm = 1.0
matrix_rate = 0.08
output_rate = 0.3
gain_rate = 1.5
matrix_decay = 0.1
feature_scale = HD ** (-0.25)
log2e = math.log2(math.e)
AXES = ("head", "row")


def dot(a, b, ca=1, cb=0):
    return lax.dot_general(a, b, (((ca,), (cb,)), ((), ())), preferred_element_type=f32)


def lanes(width):
    return lax.broadcasted_iota(jnp.int32, (1, width), 1)


def half_masks(width):
    first = (lanes(width) % 128 < HD).astype(f32)
    return first.astype(bf16), (1.0 - first).astype(bf16)


def rms_scale(values):
    return lax.rsqrt(jnp.mean(values * values, axis=-1, keepdims=True) + norm_eps)


def features(u, spread):
    raw = dot(u, spread)
    wide = u.astype(f32)
    squares = wide * wide
    own = lanes(2 * HD) < HD
    total_a = jnp.sum(jnp.where(own, squares, 0.0), axis=1, keepdims=True)
    total_b = jnp.sum(jnp.where(own, 0.0, squares), axis=1, keepdims=True)
    c1 = feature_scale * log2e
    c2 = 0.5 * feature_scale * feature_scale * log2e
    down_a = total_a * c2 + 4.0
    down_b = total_b * c2 + 4.0
    left = jnp.exp2(raw[:, :FEATS] * c1 - down_a)
    right = jnp.exp2(raw[:, FEATS:] * c1 - down_b)
    return jnp.concatenate([left, right], axis=1).astype(bf16)


def masked_pair(first, second, width):
    ma, mb = half_masks(width)
    return jnp.concatenate([first * ma, second * mb], axis=0)


def forward_kernel(
    before_ref, last_ref, xh_ref, xo_ref, segc_ref, segr_ref, wq_ref, gain_ref, spread_ref,
    h1_ref, qkv_ref, pq_ref, pk_ref, p_ref, t_ref, o_ref, of_ref, rden_ref,
    state_ref,
):
    step = pl.program_id(0)
    halo = SPAN // CHUNK
    before = before_ref[step]
    last = last_ref[step]
    ones = jnp.ones((CHUNK, 2 * HD), bf16)

    @pl.when(step == 0)
    def _():
        state_ref[...] = jnp.zeros_like(state_ref)

    @pl.when(step < halo)
    def _():
        x = xh_ref[...].astype(f32)
        h1 = (x * rms_scale(x) * gain_ref[...]).astype(bf16)
        kv = dot(h1, wq_ref[:, D:]).astype(bf16)
        chosen = (segc_ref[...] == last).astype(f32).astype(bf16)
        for p in range(PAIRS):
            k2 = kv[:, 128 * p : 128 * (p + 1)]
            v2 = kv[:, D + 128 * p : D + 128 * (p + 1)]
            pk = features(k2, spread_ref[...])
            vw = jnp.concatenate([v2, ones], axis=1) * chosen
            state_ref[p] = state_ref[p] + dot(pk, vw, 0, 0)

    @pl.when(step >= halo)
    def _():
        x = xo_ref[...].astype(f32)
        h1 = (x * rms_scale(x) * gain_ref[...]).astype(bf16)
        h1_ref[...] = h1
        qkv = dot(h1, wq_ref[...]).astype(bf16)
        qkv_ref[...] = qkv
        segc = segc_ref[...]
        segr = segr_ref[0]
        chosen = (segc == last).astype(f32).astype(bf16)
        follows = (segc == before).astype(f32).astype(bf16)
        keep = (last == before).astype(f32)
        rows = lax.broadcasted_iota(jnp.int32, (CHUNK, CHUNK), 0)
        cols = lax.broadcasted_iota(jnp.int32, (CHUNK, CHUNK), 1)
        allowed = ((rows >= cols) & (segc == segr)).astype(f32).astype(bf16)
        for p in range(PAIRS):
            cut = slice(128 * p, 128 * (p + 1))
            wide = slice(512 * p, 512 * (p + 1))
            q2 = qkv[:, 128 * p : 128 * (p + 1)]
            k2 = qkv[:, D + 128 * p : D + 128 * (p + 1)]
            v2 = qkv[:, 2 * D + 128 * p : 2 * D + 128 * (p + 1)]
            pq = features(q2, spread_ref[...])
            pk = features(k2, spread_ref[...])
            pq_ref[:, wide] = pq
            pk_ref[:, wide] = pk
            scores = jnp.concatenate(
                [
                    dot(pq[:, :FEATS], pk[:, :FEATS], 1, 1).astype(bf16) * allowed,
                    dot(pq[:, FEATS:], pk[:, FEATS:], 1, 1).astype(bf16) * allowed,
                ],
                axis=1,
            )
            p_ref[:, wide] = scores
            v1 = jnp.concatenate([v2, ones], axis=1)
            state = state_ref[p]
            narrow = state.astype(bf16)
            narrow = masked_pair(narrow[:FEATS], narrow[FEATS:], 256)
            t_ref[0, p] = narrow
            both = dot(scores, masked_pair(v1, v1, 256)) + dot(pq * follows, narrow)
            rden = 1.0 / both[:, 128:]
            of = both[:, :128] * rden
            rden_ref[:, cut] = rden
            of_ref[:, cut] = of
            o_ref[:, cut] = of.astype(bf16)
            state_ref[p] = keep * state + dot(pk, v1 * chosen, 0, 0)


def middle_kernel(
    before_ref, x_ref, g_ref, o_ref, of_ref, rden_ref, pq_ref, segc_ref, wo_ref, wu_ref, wd_ref,
    gain_ref,
    out_ref, dy1_ref, dn_ref, gup_ref, gdown_ref, gout_ref, gg_ref, back_ref,
    up_acc, down_acc, out_acc, gg_acc, back_acc, act_ref, dup_ref,
):
    step = pl.program_id(0)
    steps = pl.num_programs(0)

    @pl.when(step == 0)
    def _():
        up_acc[...] = jnp.zeros_like(up_acc)
        down_acc[...] = jnp.zeros_like(down_acc)
        out_acc[...] = jnp.zeros_like(out_acc)
        gg_acc[...] = jnp.zeros_like(gg_acc)
        back_acc[...] = jnp.zeros_like(back_acc)

    o = o_ref[...]
    g = g_ref[...]
    gain = gain_ref[...]
    y1 = x_ref[...].astype(f32) + dot(o, wo_ref[...], 1, 1)
    r2 = rms_scale(y1)
    n2 = y1 * r2
    h2 = (n2 * gain).astype(bf16)
    cut = 512
    for f in range(FF // cut):
        fs = slice(cut * f, cut * (f + 1))
        up = dot(h2, wu_ref[:, fs])
        d_act = dot(g, wd_ref[fs, :], 1, 1)
        cdf = 0.5 * (1.0 + lax.erf(up * math.sqrt(0.5)))
        density = jnp.exp(up * up * -0.5) * (1.0 / math.sqrt(2.0 * math.pi))
        act = (up * cdf).astype(bf16)
        d_up = (d_act * (cdf + up * density)).astype(bf16)
        act_ref[:, fs] = act
        dup_ref[:, fs] = d_up
        down_acc[fs, :] += dot(act, g, 0, 0)
        up_acc[:, fs] += dot(h2, d_up, 0, 0)
    out_ref[...] = (y1 + dot(act_ref[...], wd_ref[...])).astype(bf16)
    d_h2 = dot(dup_ref[...], wu_ref[...], 1, 1)
    gg_acc[...] += jnp.sum(d_h2 * n2, axis=0, keepdims=True)
    e2 = d_h2 * gain
    dy1 = g.astype(f32) + r2 * (e2 - n2 * jnp.mean(e2 * n2, axis=-1, keepdims=True))
    dy1_ref[...] = dy1
    da = dy1.astype(bf16)
    out_acc[...] += dot(da, o, 0, 0)
    d_o = dot(da, wo_ref[...])
    product = d_o * of_ref[...]
    high = product.astype(bf16)
    low = (product - high.astype(f32)).astype(bf16)
    rden = rden_ref[...]
    ma, mb = half_masks(128)
    same = jnp.concatenate(
        [jnp.broadcast_to(ma, (HD, 128)), jnp.broadcast_to(mb, (HD, 128))], axis=0
    )
    same = jnp.concatenate([same, same], axis=0)
    lane = lanes(128) % HD
    m0 = (lane == 0).astype(f32).astype(bf16)
    m1 = (lane == 1).astype(f32).astype(bf16)
    parts = []
    for p in range(PAIRS):
        ps = slice(128 * p, 128 * (p + 1))
        total = dot(jnp.concatenate([high[:, ps], low[:, ps]], axis=1), same)
        d_den = -total * rden[:, ps]
        d_hi = d_den.astype(bf16)
        d_lo = (d_den - d_hi.astype(f32)).astype(bf16)
        d_num = (d_o[:, ps] * rden[:, ps]).astype(bf16)
        dn = jnp.concatenate([d_num, d_hi * m0 + d_lo * m1], axis=1)
        dn_ref[:, 256 * p : 256 * (p + 1)] = dn
        parts.append(dn)

    @pl.when(step < SPAN // ROWS)
    def _():
        follows = (segc_ref[...] == before_ref[0]).astype(f32).astype(bf16)
        for p in range(PAIRS):
            back_acc[p] = back_acc[p] + dot(
                pq_ref[:, 512 * p : 512 * (p + 1)], dn_ref[:, 256 * p : 256 * (p + 1)] * follows, 0, 0
            )

    @pl.when(step == steps - 1)
    def _():
        gup_ref[...] = up_acc[...].astype(bf16)
        gdown_ref[...] = down_acc[...].astype(bf16)
        gout_ref[...] = out_acc[...].astype(bf16)
        gg_ref[...] = gg_acc[...]
        for p in range(PAIRS):
            back = back_acc[p].astype(bf16)
            back_ref[p] = masked_pair(back[:FEATS], back[FEATS:], 256)


def backward_kernel(
    before_ref, last_ref, p_ref, pq_ref, pk_ref, qkv_ref, dn_ref, t_ref, segc_ref, segr_ref,
    back_ref, gather_ref,
    dqkv_ref,
    state_ref,
):
    step = pl.program_id(0)
    chunk = pl.num_programs(0) - 1 - step
    before = before_ref[chunk]
    last = last_ref[chunk]

    @pl.when(step == 0)
    def _():
        state_ref[...] = back_ref[...].astype(f32)

    segc = segc_ref[...]
    segr = segr_ref[0]
    chosen = (segc == last).astype(f32).astype(bf16)
    follows = (segc == before).astype(f32).astype(bf16)
    keep = (last == before).astype(f32)
    rows = lax.broadcasted_iota(jnp.int32, (CHUNK, CHUNK), 0)
    cols = lax.broadcasted_iota(jnp.int32, (CHUNK, CHUNK), 1)
    allowed = ((rows >= cols) & (segc == segr)).astype(f32).astype(bf16)
    lane = lanes(128) % HD
    two = jnp.broadcast_to((lane < 2).astype(f32).astype(bf16), (CHUNK, 128))
    ones = jnp.ones((CHUNK, 128), bf16)
    ma, mb = half_masks(128)
    for p in range(PAIRS):
        wide = slice(512 * p, 512 * (p + 1))
        q2 = qkv_ref[:, 128 * p : 128 * (p + 1)]
        k2 = qkv_ref[:, D + 128 * p : D + 128 * (p + 1)]
        v2 = qkv_ref[:, 2 * D + 128 * p : 2 * D + 128 * (p + 1)]
        pq = pq_ref[:, wide]
        pk = pk_ref[:, wide]
        dn = dn_ref[:, 256 * p : 256 * (p + 1)]
        scores = p_ref[:, wide]
        narrow = t_ref[0, p]
        state = state_ref[p]
        back = state.astype(bf16)
        back = masked_pair(back[:FEATS], back[FEATS:], 256)
        v1 = jnp.concatenate([v2, two], axis=1)
        d_p = dot(dn, masked_pair(v1, v1, 256), 1, 1).astype(bf16)
        d_pa = d_p[:, :CHUNK] * allowed
        d_pb = d_p[:, CHUNK:] * allowed
        dn_f = dn * follows
        d_pq = dot(dn_f, narrow, 1, 1) + jnp.concatenate(
            [dot(d_pa, pk[:, :FEATS]), dot(d_pb, pk[:, FEATS:])], axis=1
        )
        vw = jnp.concatenate([v2, ones], axis=1) * chosen
        d_pk = dot(vw, back, 1, 1) + jnp.concatenate(
            [dot(d_pa, pq[:, :FEATS], 0, 0), dot(d_pb, pq[:, FEATS:], 0, 0)], axis=1
        )
        d_num = dn[:, :128]
        d_v = (
            dot(pk * chosen, back[:, :128])
            + dot(scores[:, :CHUNK], d_num * ma, 0, 0)
            + dot(scores[:, CHUNK:], d_num * mb, 0, 0)
        )
        through_q = dot(d_pq.astype(bf16) * pq, gather_ref[...])
        through_k = dot(d_pk.astype(bf16) * pk, gather_ref[...])
        scale2 = feature_scale * feature_scale
        d_q = through_q[:, :128] * feature_scale - q2.astype(f32) * through_q[:, 128:] * scale2
        d_k = through_k[:, :128] * feature_scale - k2.astype(f32) * through_k[:, 128:] * scale2
        dqkv_ref[:, 128 * p : 128 * (p + 1)] = d_q.astype(bf16)
        dqkv_ref[:, D + 128 * p : D + 128 * (p + 1)] = d_k.astype(bf16)
        dqkv_ref[:, 2 * D + 128 * p : 2 * D + 128 * (p + 1)] = d_v.astype(bf16)
        state_ref[p] = keep * state + dot(pq, dn_f, 0, 0)


def input_kernel(dqkv_ref, wq_ref, x_ref, dy1_ref, gain_ref, dx_ref, gg_ref, gg_acc):
    step = pl.program_id(0)

    @pl.when(step == 0)
    def _():
        gg_acc[...] = jnp.zeros_like(gg_acc)

    d_h1 = dot(dqkv_ref[...], wq_ref[...], 1, 1)
    x = x_ref[...].astype(f32)
    r1 = rms_scale(x)
    n1 = x * r1
    gg_acc[...] += jnp.sum(d_h1 * n1, axis=0, keepdims=True)
    e1 = d_h1 * gain_ref[...]
    dx_ref[...] = dy1_ref[...] + r1 * (e1 - n1 * jnp.mean(e1 * n1, axis=-1, keepdims=True))

    @pl.when(step == pl.num_programs(0) - 1)
    def _():
        gg_ref[...] = gg_acc[...]


def axis_bits():
    row_bits = (lax.axis_size("row") - 1).bit_length()
    head_bits = (lax.axis_size("head") - 1).bit_length()
    row = [("row", b, b) for b in range(row_bits)]
    head = [("head", b, row_bits + b) for b in range(head_bits)]
    return row, head


def swap(value, axis, bit):
    size = lax.axis_size(axis)
    return lax.ppermute(value, axis, [(i, i ^ (1 << bit)) for i in range(size)])


def gather_all(shard, order):
    held = []
    buf = shard
    for axis, bit, place in order:
        mine = (lax.axis_index(axis) >> bit) & 1
        other = swap(buf, axis, bit)
        at = sum(1 for h in held if h > place)
        buf = jnp.where(
            mine == 0, jnp.stack([buf, other], axis=at), jnp.stack([other, buf], axis=at)
        )
        held = sorted(held + [place], reverse=True)
    return buf.reshape((-1,) + shard.shape[1:])


def scatter_sum(whole, order):
    places = sorted([place for _, _, place in order], reverse=True)
    count = 1 << len(places)
    buf = whole.reshape((2,) * len(places) + (whole.shape[0] // count,) + whole.shape[1:])
    for axis, bit, place in order:
        at = places.index(place)
        places.remove(place)
        mine = (lax.axis_index(axis) >> bit) & 1
        low = lax.index_in_dim(buf, 0, at, keepdims=False)
        high = lax.index_in_dim(buf, 1, at, keepdims=False)
        send = jnp.where(mine == 0, high, low).astype(bf16)
        kept = jnp.where(mine == 0, low, high)
        buf = kept.astype(f32) + swap(send, axis, bit).astype(f32)
        if places:
            buf = buf.astype(bf16)
    return buf


def tree_sum(value):
    row, head = axis_bits()
    for axis, bit, _ in head + row:
        value = value + swap(value, axis, bit)
    return value


def adam_update(
    weight, gradient, first_moment, second_moment, clip_factor, step_value, step_rate, decay_rate
):
    clipped = gradient * clip_factor
    next_first = beta_first * first_moment + (1.0 - beta_first) * clipped
    next_second = beta_second * second_moment + (1.0 - beta_second) * clipped * clipped
    first_hat = next_first / (1.0 - beta_first**step_value)
    second_hat = next_second / (1.0 - beta_second**step_value)
    updated = weight - step_rate * (
        first_hat / (jnp.sqrt(second_hat) + adam_eps) + decay_rate * weight
    )
    return (clipped, next_first, next_second, updated)


def params(limit=60):
    return pltpu.CompilerParams(
        dimension_semantics=("arbitrary",), vmem_limit_bytes=limit << 20
    )


def fixed(shape):
    zeros = (0,) * len(shape)
    return pl.BlockSpec(shape, lambda *_: zeros, pipeline_mode=pl.Buffered(1))


def per_device(
    inputs,
    cotangent,
    segments,
    feature_matrix,
    w_qkv,
    w_out,
    w_up,
    w_down,
    gains,
    first_qkv,
    second_qkv,
    first_out,
    second_out,
    first_up,
    second_up,
    first_down,
    second_down,
    first_gains,
    second_gains,
    step_count,
):
    heads = lax.axis_size("head")
    row_bits, head_bits = axis_bits()
    x = inputs[0]
    g = cotangent[0]
    length = x.shape[0]
    chunks = length // CHUNK
    halo = SPAN // CHUNK

    share = w_qkv.shape[0]
    packed = jnp.concatenate(
        [
            w_qkv.reshape(share, 3 * D).astype(bf16),
            jnp.pad(gains.astype(bf16), ((0, 0), (0, 126))),
        ],
        axis=1,
    )
    forward_pairs = [(i, i + 1) for i in range(heads - 1)]
    backward_pairs = [(i + 1, i) for i in range(heads - 1)]
    x_ahead = lax.ppermute(x[length - SPAN :], "head", forward_pairs)
    order_a = row_bits[::-1] + head_bits[::-1]
    packed_full = gather_all(packed, order_a)
    wq = packed_full[:, : 3 * D]
    gain_first = packed_full[:, 3 * D].astype(f32).reshape(1, D)
    gain_second = packed_full[:, 3 * D + 1].astype(f32).reshape(1, D)
    w_out_full = gather_all(w_out.astype(bf16), order_a)
    w_up_full = gather_all(w_up.astype(bf16), order_a)
    w_down_full = gather_all(w_down.astype(bf16), order_a)

    row_segments = segments[0]
    padded = jnp.concatenate([jnp.full((SPAN,), -1, jnp.int32), row_segments])
    near = lax.dynamic_slice_in_dim(padded, lax.axis_index("head") * length, length + SPAN)
    seg_cols = near.reshape(-1, 1)
    seg_rows = near.reshape(-1, 1, CHUNK)
    ends = near[CHUNK - 1 :: CHUNK]
    own_before = ends[halo - 1 : -1]
    own_last = ends[halo:]
    ahead_last = jnp.full((halo,), 1, jnp.int32) * ends[halo - 1]
    all_before = jnp.concatenate([ahead_last, own_before])
    all_last = jnp.concatenate([ahead_last, own_last])
    own_cols = seg_cols[SPAN:]
    own_rows = seg_rows[halo:]

    fm = feature_matrix
    nothing = jnp.zeros_like(fm.T)
    spread = jnp.concatenate(
        [
            jnp.concatenate([fm.T, nothing], axis=1),
            jnp.concatenate([nothing, fm.T], axis=1),
        ],
        axis=0,
    )
    zero = jnp.zeros((FEATS, HD), bf16)
    one = jnp.ones((FEATS, HD), bf16)
    gather = jnp.concatenate(
        [
            jnp.concatenate([fm, zero, one, zero], axis=1),
            jnp.concatenate([zero, fm, zero, one], axis=1),
        ],
        axis=0,
    )

    def own(shape):
        rest = (0,) * (len(shape) - 1)
        return pl.BlockSpec(shape, lambda c, *_: (jnp.maximum(c - halo, 0),) + rest)

    wide = PAIRS * 2 * FEATS
    h1, qkv, pq, pk, scores, states, o, of, rden = pl.pallas_call(
        forward_kernel,
        grid_spec=pltpu.PrefetchScalarGridSpec(
            num_scalar_prefetch=2,
            grid=(halo + chunks,),
            in_specs=[
                pl.BlockSpec((CHUNK, D), lambda c, *_: (jnp.minimum(c, halo - 1), 0)),
                own((CHUNK, D)),
                pl.BlockSpec((CHUNK, 1), lambda c, *_: (c, 0)),
                pl.BlockSpec((1, 1, CHUNK), lambda c, *_: (c, 0, 0)),
                fixed((D, 3 * D)),
                fixed((1, D)),
                fixed((2 * HD, 2 * FEATS)),
            ],
            out_specs=[
                own((CHUNK, D)),
                own((CHUNK, 3 * D)),
                own((CHUNK, wide)),
                own((CHUNK, wide)),
                own((CHUNK, wide)),
                own((1, PAIRS, 2 * FEATS, 256)),
                own((CHUNK, D)),
                own((CHUNK, D)),
                own((CHUNK, D)),
            ],
            scratch_shapes=[pltpu.VMEM((PAIRS, 2 * FEATS, 256), f32)],
        ),
        out_shape=[
            jax.ShapeDtypeStruct((length, D), bf16),
            jax.ShapeDtypeStruct((length, 3 * D), bf16),
            jax.ShapeDtypeStruct((length, wide), bf16),
            jax.ShapeDtypeStruct((length, wide), bf16),
            jax.ShapeDtypeStruct((length, wide), bf16),
            jax.ShapeDtypeStruct((chunks, PAIRS, 2 * FEATS, 256), bf16),
            jax.ShapeDtypeStruct((length, D), bf16),
            jax.ShapeDtypeStruct((length, D), f32),
            jax.ShapeDtypeStruct((length, D), f32),
        ],
        compiler_params=params(),
        name="forward",
    )(all_before, all_last, x_ahead, x, seg_cols, seg_rows, wq, gain_first, spread)

    def by_step(shape):
        rest = (0,) * (len(shape) - 1)
        return pl.BlockSpec(shape, lambda c, *_: (c,) + rest)

    near_steps = SPAN // ROWS
    out_act, dy1, dn, g_up, g_down, g_out, gg_second, back = pl.pallas_call(
        middle_kernel,
        grid_spec=pltpu.PrefetchScalarGridSpec(
            num_scalar_prefetch=1,
            grid=(length // ROWS,),
            in_specs=[
                by_step((ROWS, D)),
                by_step((ROWS, D)),
                by_step((ROWS, D)),
                by_step((ROWS, D)),
                by_step((ROWS, D)),
                pl.BlockSpec((ROWS, wide), lambda c, *_: (jnp.minimum(c, near_steps - 1), 0)),
                by_step((ROWS, 1)),
                fixed((D, D)),
                fixed((D, FF)),
                fixed((FF, D)),
                fixed((1, D)),
            ],
            out_specs=[
                by_step((ROWS, D)),
                by_step((ROWS, D)),
                by_step((ROWS, PAIRS * 256)),
                fixed((D, FF)),
                fixed((FF, D)),
                fixed((D, D)),
                fixed((1, D)),
                fixed((PAIRS, 2 * FEATS, 256)),
            ],
            scratch_shapes=[
                pltpu.VMEM((D, FF), f32),
                pltpu.VMEM((FF, D), f32),
                pltpu.VMEM((D, D), f32),
                pltpu.VMEM((1, D), f32),
                pltpu.VMEM((PAIRS, 2 * FEATS, 256), f32),
                pltpu.VMEM((ROWS, FF), bf16),
                pltpu.VMEM((ROWS, FF), bf16),
            ],
        ),
        out_shape=[
            jax.ShapeDtypeStruct((length, D), bf16),
            jax.ShapeDtypeStruct((length, D), f32),
            jax.ShapeDtypeStruct((length, PAIRS * 256), bf16),
            jax.ShapeDtypeStruct((D, FF), bf16),
            jax.ShapeDtypeStruct((FF, D), bf16),
            jax.ShapeDtypeStruct((D, D), bf16),
            jax.ShapeDtypeStruct((1, D), f32),
            jax.ShapeDtypeStruct((PAIRS, 2 * FEATS, 256), bf16),
        ],
        compiler_params=params(),
        name="middle",
    )(own_before, x, g, o, of, rden, pq, own_cols, w_out_full, w_up_full, w_down_full, gain_second)

    back_in = lax.ppermute(back, "head", backward_pairs)

    def falling(shape):
        rest = (0,) * (len(shape) - 1)
        return pl.BlockSpec(shape, lambda c, *_: (chunks - 1 - c,) + rest)

    d_qkv = pl.pallas_call(
        backward_kernel,
        grid_spec=pltpu.PrefetchScalarGridSpec(
            num_scalar_prefetch=2,
            grid=(chunks,),
            in_specs=[
                falling((CHUNK, wide)),
                falling((CHUNK, wide)),
                falling((CHUNK, wide)),
                falling((CHUNK, 3 * D)),
                falling((CHUNK, PAIRS * 256)),
                falling((1, PAIRS, 2 * FEATS, 256)),
                falling((CHUNK, 1)),
                falling((1, 1, CHUNK)),
                fixed((PAIRS, 2 * FEATS, 256)),
                fixed((2 * FEATS, 256)),
            ],
            out_specs=falling((CHUNK, 3 * D)),
            scratch_shapes=[pltpu.VMEM((PAIRS, 2 * FEATS, 256), f32)],
        ),
        out_shape=jax.ShapeDtypeStruct((length, 3 * D), bf16),
        compiler_params=params(),
        name="backward",
    )(own_before, own_last, scores, pq, pk, qkv, dn, states, own_cols, own_rows, back_in, gather)

    g_qkv = dot(h1, d_qkv, 0, 0).astype(bf16)

    dx, gg_first = pl.pallas_call(
        input_kernel,
        grid=(length // ROWS,),
        in_specs=[
            by_step((ROWS, 3 * D)),
            fixed((D, 3 * D)),
            by_step((ROWS, D)),
            by_step((ROWS, D)),
            fixed((1, D)),
        ],
        out_specs=[by_step((ROWS, D)), fixed((1, D))],
        out_shape=[
            jax.ShapeDtypeStruct((length, D), f32),
            jax.ShapeDtypeStruct((1, D), f32),
        ],
        scratch_shapes=[pltpu.VMEM((1, D), f32)],
        compiler_params=params(),
        name="input_grad",
    )(d_qkv, wq, x, dy1, gain_first)

    order_g = head_bits[:1] + head_bits[1:] + row_bits
    sum_up = scatter_sum(g_up, order_g)
    sum_down = scatter_sum(g_down, order_g)
    sum_out = scatter_sum(g_out, order_g)
    sum_qkv = scatter_sum(g_qkv, order_g).reshape(share, 3, D)
    gg = tree_sum(jnp.concatenate([gg_first, gg_second], axis=0))
    place = lax.axis_index(AXES) * share
    sum_gains = lax.dynamic_slice_in_dim(gg, place, share, 1).T

    reduced = (sum_qkv, sum_out, sum_up, sum_down, sum_gains)
    local_squares = jnp.float32(0.0)
    for gradient in reduced:
        local_squares = local_squares + jnp.sum(gradient * gradient)
    total_squares = tree_sum(local_squares.reshape(1, 1))[0, 0]
    grad_norm = jnp.sqrt(total_squares)
    clip_factor = jnp.minimum(1.0, max_norm / (grad_norm + 1e-06))
    step_value = step_count.astype(f32)
    update = partial(adam_update, clip_factor=clip_factor, step_value=step_value)
    qkv_parts = update(
        w_qkv, reduced[0], first_qkv, second_qkv, step_rate=matrix_rate, decay_rate=matrix_decay
    )
    out_parts = update(
        w_out, reduced[1], first_out, second_out, step_rate=output_rate, decay_rate=matrix_decay
    )
    up_parts = update(
        w_up, reduced[2], first_up, second_up, step_rate=matrix_rate, decay_rate=matrix_decay
    )
    down_parts = update(
        w_down, reduced[3], first_down, second_down, step_rate=matrix_rate, decay_rate=matrix_decay
    )
    gain_parts = update(
        gains, reduced[4], first_gains, second_gains, step_rate=gain_rate, decay_rate=0.0
    )
    return (
        (out_act[None], dx[None], grad_norm)
        + qkv_parts
        + out_parts
        + up_parts
        + down_parts
        + gain_parts
    )


def solution(mesh):
    token = P("row", "head", None)
    three = P(AXES, None, None)
    two = P(AXES, None)
    placed = (token, token, P("row", None), P(), three, two, two, two, two)
    placed = placed + (three, three) + (two,) * 8 + (P(),)
    return jax.shard_map(
        per_device,
        mesh=mesh,
        in_specs=placed,
        out_specs=(token, token, P()) + (three,) * 4 + (two,) * 16,
        check_vma=False,
    )
```

time: 1860 us -> 344 us (0.18); the launches traced: 1830 us -> 343 us
  matrix products: 539 us -> 3.59 us
  waiting for transfers between devices: 634 us -> 104 us
  other arithmetic: 226 us -> 27.4 us
  local copies, waits for them, and re-layouts: 194 us -> 17.2 us
  blocking collectives: 174 us -> 0 us
  Pallas kernels: 0 us -> 126 us
  starting transfers between devices: 0.88 us -> 54.9 us
  loops' own time: 45 us -> 0 us
    dot_general x239 -> x1, matrix products: 527 us -> 3.59 us  [dot(): lax.dot_general(a, b, (((ca,), (cb,)), ((), ())), preferred_element_type=...]
    reduce_scatter x6 -> x0, waiting for transfers between devices: 396 us -> none  [the longest x1 139 us: per_device(): lax.psum_scatter(grad_qkv, ('head', 'row'), scatter_dimension=0, tiled=True)]
    all_gather x2 -> x0, blocking collectives: 137 us -> none  [the longest x1 69.3 us: per_device(): lax.all_gather(gains.astype(jnp.bfloat16), ('head', 'row'), axis=0, tiled...]
    unnamed x13 -> x0, waiting for transfers between devices: 133 us -> none
    pallas_call x0 -> x4, Pallas kernels: none -> 126 us  [the longest x1 48.5 us: per_device(): pl.pallas_call(middle_kernel, grid_spec=pltpu.PrefetchScalarGridSpec(num_...]
    all_gather x5 -> x0, waiting for transfers between devices: 104 us -> none  [the longest x1 55.7 us: per_device(): lax.all_gather(w_up.astype(jnp.bfloat16), ('head', 'row'), axis=0, tiled=...]
    ppermute x0 -> x52, waiting for transfers between devices: none -> 104 us  [the longest x50 104 us: swap(): return lax.ppermute(value, axis, [(i, i ^ 1 << bit) for i in range(size)])]
    reduce_sum x39 -> x0, other arithmetic: 71.7 us -> none  [the longest x2 25.1 us: feature_backward(): totals = jnp.sum(grad_logits, axis=-1, keepdims=True)]
  transfers between devices with their start and end apart: 12 -> 52, of which waited for: 8 -> 31; matrix products, arithmetic and copies ran while one was open for 34% -> 11% of each run, Pallas kernels for 0% -> 22%
where the time goes in v1:
time: 344 us; the launch traced here: 343 us
  Pallas kernels  126 us (37%)
  waiting for transfers between devices  104 us (30%)
  starting transfers between devices  54.9 us (16%)
  other arithmetic  27.4 us (8%)
  local copies, waits for them, and re-layouts  17.2 us (5%)
  between operations  10.1 us (3%)
  matrix products  3.59 us (1%)
    ppermute x50, waiting for transfers between devices, swap(): return lax.ppermute(value, axis, [(i, i ^ 1 << bit) for i in range(size)])  104 us
    ppermute x50, starting transfers between devices, swap(): return lax.ppermute(value, axis, [(i, i ^ 1 << bit) for i in range(size)])  51.1 us
    pallas_call x1, Pallas kernels, per_device(): pl.pallas_call(middle_kernel, grid_spec=pltpu.PrefetchScalarGridSpec(num_...  48.5 us
    pallas_call x1, Pallas kernels, per_device(): pl.pallas_call(forward_kernel, grid_spec=pltpu.PrefetchScalarGridSpec(num...  34.9 us
    pallas_call x1, Pallas kernels, per_device(): pl.pallas_call(backward_kernel, grid_spec=pltpu.PrefetchScalarGridSpec(nu...  31.9 us
    pallas_call x1, Pallas kernels, per_device(): pl.pallas_call(input_kernel, grid=(length // ROWS,), in_specs=[by_step((R...  10.3 us
  transfers between devices with their start and end apart: 52, of which 31 were waited for; matrix products, arithmetic and copies ran while one was open for 11% of the time, Pallas kernels for 22%

profile of v1, /device:TPU:0, one launch (start us, length us, event | category | flops | bytes accessed | tf_op | source)
XLA Modules:
  0.0 343.0 jit_solution(17929460280302678393)
XLA Ops:
  2.5 4.1 %collective-permute-start.1 = (bf16[16,1664]{1,0:T(8,128)(2,1)S(1)}, bf16[16,1664]{1,0:T(8,128)(2,1)S(1)}, u32[]{:S(2)}, u32[]{:S(2)}) collective-permute-start(bf16[16,1664]{1,0:T(8,128)(2,1)S(1)} %get-tuple-element.139), channel_id=1, source_target_pairs={{0,4},{1,5},{2,6},{3,7},{4,0},{5,1},{6,2},{7,3},{8,12},{9,13},{10,... | collective-permute-start | bytes 159752 | tf_op jit(solution)/shard_map/ppermute | solution.py:337
  6.6 2.3 slice_bitcast_fusion
  8.9 2.5 collective-permute-start
  11.7 2.7 collective-permute-start.16
  23.7 2.4 collective-permute-done.7
  38.5 3.5 %collective-permute-done.3 = bf16[2,2,16,1664]{3,2,0,1:T(8,128)(2,1)S(1)} collective-permute-done((bf16[2,2,16,1664]{3,2,0,1:T(8,128)(2,1)S(1)}, bf16[2,2,16,1664]{3,2,0,1:T(8,128)(2,1)S(1)}, u32[]{:S(2)}, u32[]{:S(2)}) %collective-permute-start.3) | collective-permute-done | bytes 213024 | tf_op jit(solution)/shard_map/ppermute | solution.py:337
  42.4 3.8 %collective-permute-done.13 = bf16[2,2,16,2048]{3,2,0,1:T(8,128)(2,1)S(1)} collective-permute-done((bf16[2,2,16,2048]{3,2,0,1:T(8,128)(2,1)S(1)}, bf16[2,2,16,2048]{3,2,0,1:T(8,128)(2,1)S(1)}, u32[]{:S(2)}, u32[]{:S(2)}) %collective-permute-start.13) | collective-permute-done | bytes 262176 | tf_op jit(solution)/shard_map/ppermute | solution.py:337
  51.3 3.6 %collective-permute-done.4 = bf16[2,2,2,16,1664]{4,3,0,1,2:T(8,128)(2,1)S(1)} collective-permute-done((bf16[2,2,2,16,1664]{4,3,0,1,2:T(8,128)(2,1)S(1)}, bf16[2,2,2,16,1664]{4,3,0,1,2:T(8,128)(2,1)S(1)}, u32[]{:S(2)}, u32[]{:S(2)}) %collective-permute-start.4) | collective-permute-done | bytes 426016 | tf_op jit(solution)/shard_map/ppermute | solution.py:337
  55.1 11.0 %collective-permute-done.14 = bf16[2,2,2,16,2048]{4,3,0,1,2:T(8,128)(2,1)S(1)} collective-permute-done((bf16[2,2,2,16,2048]{4,3,0,1,2:T(8,128)(2,1)S(1)}, bf16[2,2,2,16,2048]{4,3,0,1,2:T(8,128)(2,1)S(1)}, u32[]{:S(2)}, u32[]{:S(2)}) %collective-permute-start.14) | collective-permute-done | bytes 524320 | tf_op jit(solution)/shard_map/ppermute | solution.py:337
  67.5 5.9 %collective-permute-done.19 = bf16[2,2,2,64,512]{4,3,0,1,2:T(8,128)(2,1)S(1)} collective-permute-done((bf16[2,2,2,64,512]{4,3,0,1,2:T(8,128)(2,1)S(1)}, bf16[2,2,2,64,512]{4,3,0,1,2:T(8,128)(2,1)S(1)}, u32[]{:S(2)}, u32[]{:S(2)}) %collective-permute-start.19) | collective-permute-done | bytes 524320 | tf_op jit(solution)/shard_map/ppermute | solution.py:337
  77.5 34.9 %forward.1 = (bf16[2048,512]{1,0:T(8,128)(2,1)}, bf16[2048,1536]{1,0:T(8,128)(2,1)}, bf16[2048,2048]{1,0:T(8,128)(2,1)}, bf16[2048,2048]{1,0:T(8,128)(2,1)}, bf1...) custom-call(s32[12]{0:T(128)} %concatenate.474.before_ref, ...), custom_call_target="tpu_custom_call" | custom-call | tf_op jit(solution)/shard_map/forward/pallas_call | solution.py:492
  114.2 2.0 maximum_select_fusion.1
  117.6 48.5 %middle.1 = (bf16[2048,512]{1,0:T(8,128)(2,1)}, f32[2048,512]{1,0:T(8,128)}, bf16[2048,1024]{1,0:T(8,128)(2,1)}, bf16[512,2048]{1,0:T(8,128)(2,1)}, bf16[2048,51...) custom-call(s32[8]{0:T(128)} %copy-done.22, ...), custom_call_target="tpu_custom_call" | custom-call | tf_op jit(solution)/shard_map/middle/pallas_call | solution.py:539
  174.6 11.3 %collective-permute-done.28 = bf16[2,2,2,16,512]{4,3,0,1,2:T(8,128)(2,1)S(1)} collective-permute-done((bf16[2,2,2,16,512]{4,3,0,1,2:T(8,128)(2,1)S(1)}, bf16[2,2,2,16,512]{4,3,0,1,2:T(8,128)(2,1)S(1)}, u32[]{:S(2)}, u32[]{:S(2)}) %collective-permute-start.28) | collective-permute-done | bytes 131104 | tf_op jit(solution)/shard_map/ppermute | solution.py:337
  187.4 2.9 collective-permute-done.29
  195.0 2.5 collective-permute-start.31
  200.4 31.9 %backward.1.dqkv_ref = bf16[2048,1536]{1,0:T(8,128)(2,1)} custom-call(s32[8]{0:T(128)} %copy-done.22, s32[8]{0:T(128)} %copy-done.23, bf16[2048,2048]{1,0:T(8,128)(2,1)} %get-tuple-element.47.p_ref, bf16[2048,2048]{1,0:T(8,128)(2,1)} %get-tuple-element.45.pq_ref, bf16[2048,2048]{1,0:T(8,128)(2,1)} %get-tuple-element.48.pk_ref, ...), custom_call_target="tpu_custom_call" | custom-call | tf_op jit(solution)/shard_map/backward/pallas_call | solution.py:597
  232.4 10.3 %input_grad.1 = (f32[2048,512]{1,0:T(8,128)}, f32[1,512]{1,0:T(1,128)}) custom-call(bf16[2048,1536]{1,0:T(8,128)(2,1)} %backward.1.dqkv_ref, bf16[512,1536]{1,0:T(8,128)(2,1)} %slice.217.wq_ref, bf16[2048,512]{1,0:T(8,128)(2,1)} %bitcast.222, f32[2048,512]{1,0:T(8,128)} %get-tuple-element.53.dy1_ref, f32[1,512]{1,0:T(1,128)} %bitcast.290), custom_call_target="tpu_custom_call" | custom-call | tf_op jit(solution)/shard_map/input_grad/pallas_call | solution.py:624
  249.7 10.6 %collective-permute-done.43 = f32[2,512]{1,0:T(2,128)S(1)} collective-permute-done((f32[2,512]{1,0:T(2,128)S(1)}, f32[2,512]{1,0:T(2,128)S(1)}, u32[]{:S(2)}, u32[]{:S(2)}) %collective-permute-start.43) | collective-permute-done | bytes 4128 | tf_op jit(solution)/shard_map/ppermute | solution.py:337
  261.6 3.6 %convolution_convert_fusion = bf16[512,1536]{1,0:T(8,128)(2,1)S(1)} fusion(bf16[2048,512]{1,0:T(8,128)(2,1)S(1)} %copy-done.27, bf16[2048,1536]{1,0:T(8,128)(2,1)S(1)} %copy-done), kind=kOutput, calls=%fused_computation | convolution fusion | flops 3222011904 | bytes 9961472 | tf_op jit(solution)/shard_map/dot_general | solution.py:37
  266.7 2.2 collective-permute-done.45
  268.9 2.6 collective-permute-start.46
  276.8 6.9 %collective-permute-done.39 = bf16[2,2,64,512]{3,2,0,1:T(8,128)(2,1)S(1)} collective-permute-done((bf16[2,2,64,512]{3,2,0,1:T(8,128)(2,1)S(1)}, bf16[2,2,64,512]{3,2,0,1:T(8,128)(2,1)S(1)}, u32[]{:S(2)}, u32[]{:S(2)}) %collective-permute-start.39) | collective-permute-done | bytes 262176 | tf_op jit(solution)/shard_map/ppermute | solution.py:337
  290.3 2.2 collective-permute-done.35
  292.6 4.8 %collective-permute-done.23 = bf16[2,2,2,16,1536]{4,3,0,1,2:T(8,128)(2,1)S(1)} collective-permute-done((bf16[2,2,2,16,1536]{4,3,0,1,2:T(8,128)(2,1)S(1)}, bf16[2,2,2,16,1536]{4,3,0,1,2:T(8,128)(2,1)S(1)}, u32[]{:S(2)}, u32[]{:S(2)}) %collective-permute-start.23) | collective-permute-done | bytes 393248 | tf_op jit(solution)/shard_map/ppermute | solution.py:337
  298.7 4.8 %collective-permute-done.24 = bf16[2,2,16,1536]{3,2,0,1:T(8,128)(2,1)S(1)} collective-permute-done((bf16[2,2,16,1536]{3,2,0,1:T(8,128)(2,1)S(1)}, bf16[2,2,16,1536]{3,2,0,1:T(8,128)(2,1)S(1)}, u32[]{:S(2)}, u32[]{:S(2)}) %collective-permute-start.24) | collective-permute-done | bytes 196640 | tf_op jit(solution)/shard_map/ppermute | solution.py:337
  305.0 3.2 collective-permute-done.25
  309.5 4.3 %collective-permute-done.26 = bf16[16,1536]{1,0:T(8,128)(2,1)S(1)} collective-permute-done((bf16[16,1536]{1,0:T(8,128)(2,1)S(1)}, bf16[16,1536]{1,0:T(8,128)(2,1)S(1)}, u32[]{:S(2)}, u32[]{:S(2)}) %collective-permute-start.26) | collective-permute-done | bytes 49184 | tf_op jit(solution)/shard_map/ppermute | solution.py:337
  321.3 2.1 collective-permute-done.48
  324.0 2.1 collective-permute-start.49
  330.1 2.0 collective-permute-done.50
  334.1 3.2 collective-permute-done.51
  (272 shorter events, 92.4 us)
Async XLA Ops:
  2.5 25.2 %collective-permute-start.1 = (bf16[16,1664]{1,0:T(8,128)(2,1)S(1)}, bf16[16,1664]{1,0:T(8,128)(2,1)S(1)}, u32[]{:S(2)}, u32[]{:S(2)}) collective-permute-start(bf16[16,1664]{1,0:T(8,128)(2,1)S(1)} %get-tuple-element.139), channel_id=1, source_target_pairs={{0,4},{1,5},{2,6},{3,7},{4,0},{5,1},{6,2},{7,3},{8,12},{9,13},{10,... | collective-permute-start | bytes 159752 | tf_op jit(solution)/shard_map/ppermute | solution.py:337
  8.9 68.6 %collective-permute-start = (bf16[1024,512]{1,0:T(8,128)(2,1)}, bf16[1024,512]{1,0:T(8,128)(2,1)}, u32[]{:S(2)}, u32[]{:S(2)}) collective-permute-start(bf16[1024,512]{1,0:T(8,128)(2,1)} %slice_bitcast_fusion), channel_id=1, source_target_pairs={{0,8},{8,16},{16,24},{1,9},{9,17},{17,25},{2,10},{10,18},{18,26},{... | collective-permute-start | bytes 3145736 | tf_op jit(solution)/shard_map/ppermute | solution.py:444
  11.3 18.0 %collective-permute-start.11 = (bf16[16,2048]{1,0:T(8,128)(2,1)S(1)}, bf16[16,2048]{1,0:T(8,128)(2,1)S(1)}, u32[]{:S(2)}, u32[]{:S(2)}) collective-permute-start(bf16[16,2048]{1,0:T(8,128)(2,1)S(1)} %convert_element_type.286), channel_id=1, source_target_pairs={{0,4},{1,5},{2,6},{3,7},{4,0},{5,1},{6,2},{7,3},{8,12},{9,13},{10,... | collective-permute-start | bytes 196616 | tf_op jit(solution)/shard_map/ppermute | solution.py:337
  11.7 18.3 %collective-permute-start.16 = (bf16[64,512]{1,0:T(8,128)(2,1)S(1)}, bf16[64,512]{1,0:T(8,128)(2,1)S(1)}, u32[]{:S(2)}, u32[]{:S(2)}) collective-permute-start(bf16[64,512]{1,0:T(8,128)(2,1)S(1)} %convert_element_type.287), channel_id=1, source_target_pairs={{0,4},{1,5},{2,6},{3,7},{4,0},{5,1},{6,2},{7,3},{8,12},{9,13},{10,... | collective-permute-start | bytes 196616 | tf_op jit(solution)/shard_map/ppermute | solution.py:337
  14.4 7.7 %collective-permute-start.6 = (bf16[16,512]{1,0:T(8,128)(2,1)S(1)}, bf16[16,512]{1,0:T(8,128)(2,1)S(1)}, u32[]{:S(2)}, u32[]{:S(2)}) collective-permute-start(bf16[16,512]{1,0:T(8,128)(2,1)S(1)} %convert_element_type.285), channel_id=1, source_target_pairs={{0,4},{1,5},{2,6},{3,7},{4,0},{5,1},{6,2},{7,3},{8,12},{9,13},{10,... | collective-permute-start | bytes 49160 | tf_op jit(solution)/shard_map/ppermute | solution.py:337
  29.4 6.6 %collective-permute-start.12 = (bf16[2,16,2048]{2,1,0:T(8,128)(2,1)S(1)}, bf16[2,16,2048]{2,1,0:T(8,128)(2,1)S(1)}, u32[]{:S(2)}, u32[]{:S(2)}) collective-permute-start(bf16[2,16,2048]{2,1,0:T(8,128)(2,1)S(1)} %maximum_select_fusion.27), channel_id=1, source_target_pairs={{0,2},{1,3},{2,0},{3,1},{4,6},{5,7},{6,4},{7,5},{8,10},{9,11},{10,... | collective-permute-start | bytes 393224 | tf_op jit(solution)/shard_map/ppermute | solution.py:337
  30.1 7.3 %collective-permute-start.17 = (bf16[2,64,512]{2,1,0:T(8,128)(2,1)S(1)}, bf16[2,64,512]{2,1,0:T(8,128)(2,1)S(1)}, u32[]{:S(2)}, u32[]{:S(2)}) collective-permute-start(bf16[2,64,512]{2,1,0:T(8,128)(2,1)S(1)} %maximum_select_fusion.29), channel_id=1, source_target_pairs={{0,2},{1,3},{2,0},{3,1},{4,6},{5,7},{6,4},{7,5},{8,10},{9,11},{10,... | collective-permute-start | bytes 393224 | tf_op jit(solution)/shard_map/ppermute | solution.py:337
  31.7 6.7 %collective-permute-start.9 = (bf16[2,2,2,16,512]{4,3,0,1,2:T(8,128)(2,1)S(1)}, bf16[2,2,2,16,512]{4,3,0,1,2:T(8,128)(2,1)S(1)}, u32[]{:S(2)}, u32[]{:S(2)}) collective-permute-start(bf16[2,2,2,16,512]{4,3,0,1,2:T(8,128)(2,1)S(1)} %maximum_select_fusion.25), channel_id=1, source_target_pairs={{0,16},{8,24},{16,0},{24,8},{1,17},{9,25},{17,1},{25,9},{2,18},{10... | collective-permute-start | bytes 393224 | tf_op jit(solution)/shard_map/ppermute | solution.py:337
  33.7 8.3 %collective-permute-start.3 = (bf16[2,2,16,1664]{3,2,0,1:T(8,128)(2,1)S(1)}, bf16[2,2,16,1664]{3,2,0,1:T(8,128)(2,1)S(1)}, u32[]{:S(2)}, u32[]{:S(2)}) collective-permute-start(bf16[2,2,16,1664]{3,2,0,1:T(8,128)(2,1)S(1)} %maximum_select_fusion.23), channel_id=1, source_target_pairs={{0,1},{1,0},{2,3},{3,2},{4,5},{5,4},{6,7},{7,6},{8,9},{9,8},{10,11... | collective-permute-start | bytes 638984 | tf_op jit(solution)/shard_map/ppermute | solution.py:337
  36.0 10.2 %collective-permute-start.13 = (bf16[2,2,16,2048]{3,2,0,1:T(8,128)(2,1)S(1)}, bf16[2,2,16,2048]{3,2,0,1:T(8,128)(2,1)S(1)}, u32[]{:S(2)}, u32[]{:S(2)}) collective-permute-start(bf16[2,2,16,2048]{3,2,0,1:T(8,128)(2,1)S(1)} %maximum_select_fusion.19), channel_id=1, source_target_pairs={{0,1},{1,0},{2,3},{3,2},{4,5},{5,4},{6,7},{7,6},{8,9},{9,8},{10,11... | collective-permute-start | bytes 786440 | tf_op jit(solution)/shard_map/ppermute | solution.py:337
  37.4 11.6 %collective-permute-start.18 = (bf16[2,2,64,512]{3,2,0,1:T(8,128)(2,1)S(1)}, bf16[2,2,64,512]{3,2,0,1:T(8,128)(2,1)S(1)}, u32[]{:S(2)}, u32[]{:S(2)}) collective-permute-start(bf16[2,2,64,512]{3,2,0,1:T(8,128)(2,1)S(1)} %maximum_select_fusion.21), channel_id=1, source_target_pairs={{0,1},{1,0},{2,3},{3,2},{4,5},{5,4},{6,7},{7,6},{8,9},{9,8},{10,11... | collective-permute-start | bytes 786440 | tf_op jit(solution)/shard_map/ppermute | solution.py:337
  38.4 11.9 %collective-permute-start.10 = (bf16[2,2,2,2,16,512]{5,4,1,2,3,0:T(8,128)(2,1)S(1)}, bf16[2,2,2,2,16,512]{5,4,1,2,3,0:T(8,128)(2,1)S(1)}, u32[]{:S(2)}, u32[]{:S(2)}) collective-permute-start(bf16[2,2,2,2,16,512]{5,4,1,2,3,0:T(8,128)(2,1)S(1)} %maximum_select_fusion.17), channel_id=1, source_target_pairs={{0,8},{8,0},{16,24},{24,16},{1,9},{9,1},{17,25},{25,17},{2,10},{10... | collective-permute-start | bytes 786440 | tf_op jit(solution)/shard_map/ppermute | solution.py:337
  42.1 12.8 %collective-permute-start.4 = (bf16[2,2,2,16,1664]{4,3,0,1,2:T(8,128)(2,1)S(1)}, bf16[2,2,2,16,1664]{4,3,0,1,2:T(8,128)(2,1)S(1)}, u32[]{:S(2)}, u32[]{:S(2)}) collective-permute-start(bf16[2,2,2,16,1664]{4,3,0,1,2:T(8,128)(2,1)S(1)} %maximum_select_fusion.15), channel_id=1, source_target_pairs={{0,16},{8,24},{16,0},{24,8},{1,17},{9,25},{17,1},{25,9},{2,18},{10... | collective-permute-start | bytes 1277960 | tf_op jit(solution)/shard_map/ppermute | solution.py:337
  46.3 19.9 %collective-permute-start.14 = (bf16[2,2,2,16,2048]{4,3,0,1,2:T(8,128)(2,1)S(1)}, bf16[2,2,2,16,2048]{4,3,0,1,2:T(8,128)(2,1)S(1)}, u32[]{:S(2)}, u32[]{:S(2)}) collective-permute-start(bf16[2,2,2,16,2048]{4,3,0,1,2:T(8,128)(2,1)S(1)} %maximum_select_fusion.11), channel_id=1, source_target_pairs={{0,16},{8,24},{16,0},{24,8},{1,17},{9,25},{17,1},{25,9},{2,18},{10... | collective-permute-start | bytes 1572872 | tf_op jit(solution)/shard_map/ppermute | solution.py:337
  49.1 24.3 %collective-permute-start.19 = (bf16[2,2,2,64,512]{4,3,0,1,2:T(8,128)(2,1)S(1)}, bf16[2,2,2,64,512]{4,3,0,1,2:T(8,128)(2,1)S(1)}, u32[]{:S(2)}, u32[]{:S(2)}) collective-permute-start(bf16[2,2,2,64,512]{4,3,0,1,2:T(8,128)(2,1)S(1)} %maximum_select_fusion.13), channel_id=1, source_target_pairs={{0,16},{8,24},{16,0},{24,8},{1,17},{9,25},{17,1},{25,9},{2,18},{10... | collective-permute-start | bytes 1572872 | tf_op jit(solution)/shard_map/ppermute | solution.py:337
  55.1 19.8 %collective-permute-start.5 = (bf16[2,2,2,2,16,1664]{5,4,1,2,3,0:T(8,128)(2,1)S(1)}, bf16[2,2,2,2,16,1664]{5,4,1,2,3,0:T(8,128)(2,1)S(1)}, u32[]{:S(2)}, u32[]{:S(2)}) collective-permute-start(bf16[2,2,2,2,16,1664]{5,4,1,2,3,0:T(8,128)(2,1)S(1)} %maximum_select_fusion.8), channel_id=1, source_target_pairs={{0,8},{8,0},{16,24},{24,16},{1,9},{9,1},{17,25},{25,17},{2,10},{10... | collective-permute-start | bytes 2555912 | tf_op jit(solution)/shard_map/ppermute | solution.py:337
  67.3 45.0 %collective-permute-start.15 = (bf16[2,2,2,2,16,2048]{5,4,1,2,3,0:T(8,128)(2,1)}, bf16[2,2,2,2,16,2048]{5,4,1,2,3,0:T(8,128)(2,1)S(1)}, u32[]{:S(2)}, u32[]{:S(2)}) collective-permute-start(bf16[2,2,2,2,16,2048]{5,4,1,2,3,0:T(8,128)(2,1)} %maximum_select_fusion.4), channel_id=1, source_target_pairs={{0,8},{8,0},{16,24},{24,16},{1,9},{9,1},{17,25},{25,17},{2,10},{10... | collective-permute-start | bytes 3145736 | tf_op jit(solution)/shard_map/ppermute | solution.py:337
  74.5 39.7 %collective-permute-start.20 = (bf16[2,2,2,2,64,512]{5,4,1,2,3,0:T(8,128)(2,1)}, bf16[2,2,2,2,64,512]{5,4,1,2,3,0:T(8,128)(2,1)}, u32[]{:S(2)}, u32[]{:S(2)}) collective-permute-start(bf16[2,2,2,2,64,512]{5,4,1,2,3,0:T(8,128)(2,1)} %maximum_select_fusion.6), channel_id=1, source_target_pairs={{0,8},{8,0},{16,24},{24,16},{1,9},{9,1},{17,25},{25,17},{2,10},{10... | collective-permute-start | bytes 3145736 | tf_op jit(solution)/shard_map/ppermute | solution.py:337
  166.1 34.4 %collective-permute-start.21 = (bf16[4,512,256]{2,1,0:T(8,128)(2,1)}, bf16[4,512,256]{2,1,0:T(8,128)(2,1)}, u32[]{:S(2)}, u32[]{:S(2)}) collective-permute-start(bf16[4,512,256]{2,1,0:T(8,128)(2,1)} %get-tuple-element.52), channel_id=1, source_target_pairs={{8,0},{16,8},{24,16},{9,1},{17,9},{25,17},{10,2},{18,10},{26,18},{... | collective-permute-start | bytes 3145736 | tf_op jit(solution)/shard_map/ppermute | solution.py:591
  171.6 14.3 %collective-permute-start.28 = (bf16[2,2,2,16,512]{4,3,0,1,2:T(8,128)(2,1)S(1)}, bf16[2,2,2,16,512]{4,3,0,1,2:T(8,128)(2,1)S(1)}, u32[]{:S(2)}, u32[]{:S(2)}) collective-permute-start(bf16[2,2,2,16,512]{4,3,0,1,2:T(8,128)(2,1)S(1)} %select_bitcast_fusion.12), channel_id=1, source_target_pairs={{0,16},{8,24},{16,0},{24,8},{1,17},{9,25},{17,1},{25,9},{2,18},{10... | collective-permute-start | bytes 393224 | tf_op jit(solution)/shard_map/ppermute | solution.py:337
  174.4 69.1 %collective-permute-start.37 = (bf16[2,2,2,2,64,512]{5,4,1,2,3,0:T(8,128)(2,1)}, bf16[2,2,2,2,64,512]{5,4,1,2,3,0:T(8,128)(2,1)}, u32[]{:S(2)}, u32[]{:S(2)}) collective-permute-start(bf16[2,2,2,2,64,512]{5,4,1,2,3,0:T(8,128)(2,1)} %select_bitcast_fusion), channel_id=1, source_target_pairs={{0,8},{8,0},{16,24},{24,16},{1,9},{9,1},{17,25},{25,17},{2,10},{10... | collective-permute-start | bytes 3145736 | tf_op jit(solution)/shard_map/ppermute | solution.py:337
  192.8 52.7 %collective-permute-start.32 = (bf16[2,2,2,2,16,2048]{5,4,1,2,3,0:T(8,128)(2,1)}, bf16[2,2,2,2,16,2048]{5,4,1,2,3,0:T(8,128)(2,1)}, u32[]{:S(2)}, u32[]{:S(2)}) collective-permute-start(bf16[2,2,2,2,16,2048]{5,4,1,2,3,0:T(8,128)(2,1)} %select_bitcast_fusion.1), channel_id=1, source_target_pairs={{0,8},{8,0},{16,24},{24,16},{1,9},{9,1},{17,25},{25,17},{2,10},{10... | collective-permute-start | bytes 3145736 | tf_op jit(solution)/shard_map/ppermute | solution.py:337
  245.4 28.6 %collective-permute-start.38 = (bf16[2,2,2,64,512]{4,3,0,1,2:T(8,128)(2,1)S(1)}, bf16[2,2,2,64,512]{4,3,0,1,2:T(8,128)(2,1)S(1)}, u32[]{:S(2)}, u32[]{:S(2)}) collective-permute-start(bf16[2,2,2,64,512]{4,3,0,1,2:T(8,128)(2,1)S(1)} %select_bitcast_fusion.3), channel_id=1, source_target_pairs={{0,16},{8,24},{16,0},{24,8},{1,17},{9,25},{17,1},{25,9},{2,18},{10... | collective-permute-start | bytes 1572872 | tf_op jit(solution)/shard_map/ppermute | solution.py:337
  247.5 12.8 %collective-permute-start.43 = (f32[2,512]{1,0:T(2,128)S(1)}, f32[2,512]{1,0:T(2,128)S(1)}, u32[]{:S(2)}, u32[]{:S(2)}) collective-permute-start(f32[2,512]{1,0:T(2,128)S(1)} %fusion.30), channel_id=1, source_target_pairs={{0,16},{8,24},{16,0},{24,8},{1,17},{9,25},{17,1},{25,9},{2,18},{10... | collective-permute-start | bytes 12296 | tf_op jit(solution)/shard_map/ppermute | solution.py:337
  249.4 25.8 %collective-permute-start.33 = (bf16[2,2,2,16,2048]{4,3,0,1,2:T(8,128)(2,1)S(1)}, bf16[2,2,2,16,2048]{4,3,0,1,2:T(8,128)(2,1)S(1)}, u32[]{:S(2)}, u32[]{:S(2)}) collective-permute-start(bf16[2,2,2,16,2048]{4,3,0,1,2:T(8,128)(2,1)S(1)} %select_bitcast_fusion.4), channel_id=1, source_target_pairs={{0,16},{8,24},{16,0},{24,8},{1,17},{9,25},{17,1},{25,9},{2,18},{10... | collective-permute-start | bytes 1572872 | tf_op jit(solution)/shard_map/ppermute | solution.py:337
  271.5 16.9 %collective-permute-start.22 = (bf16[2,2,2,2,16,1536]{5,4,1,2,3,0:T(8,128)(2,1)S(1)}, bf16[2,2,2,2,16,1536]{5,4,1,2,3,0:T(8,128)(2,1)S(1)}, u32[]{:S(2)}, u32[]{:S(2)}) collective-permute-start(bf16[2,2,2,2,16,1536]{5,4,1,2,3,0:T(8,128)(2,1)S(1)} %select_bitcast_fusion.2), channel_id=1, source_target_pairs={{0,8},{8,0},{16,24},{24,16},{1,9},{9,1},{17,25},{25,17},{2,10},{10... | collective-permute-start | bytes 2359304 | tf_op jit(solution)/shard_map/ppermute | solution.py:337
  274.3 9.3 %collective-permute-start.39 = (bf16[2,2,64,512]{3,2,0,1:T(8,128)(2,1)S(1)}, bf16[2,2,64,512]{3,2,0,1:T(8,128)(2,1)S(1)}, u32[]{:S(2)}, u32[]{:S(2)}) collective-permute-start(bf16[2,2,64,512]{3,2,0,1:T(8,128)(2,1)S(1)} %select_bitcast_fusion.6), channel_id=1, source_target_pairs={{0,1},{1,0},{2,3},{3,2},{4,5},{5,4},{6,7},{7,6},{8,9},{9,8},{10,11... | collective-permute-start | bytes 786440 | tf_op jit(solution)/shard_map/ppermute | solution.py:337
  275.5 11.4 %collective-permute-start.34 = (bf16[2,2,16,2048]{3,2,0,1:T(8,128)(2,1)S(1)}, bf16[2,2,16,2048]{3,2,0,1:T(8,128)(2,1)S(1)}, u32[]{:S(2)}, u32[]{:S(2)}) collective-permute-start(bf16[2,2,16,2048]{3,2,0,1:T(8,128)(2,1)S(1)} %select_bitcast_fusion.7), channel_id=1, source_target_pairs={{0,1},{1,0},{2,3},{3,2},{4,5},{5,4},{6,7},{7,6},{8,9},{9,8},{10,11... | collective-permute-start | bytes 786440 | tf_op jit(solution)/shard_map/ppermute | solution.py:337
  283.8 6.3 %collective-permute-start.40 = (bf16[2,64,512]{2,1,0:T(8,128)(2,1)S(1)}, bf16[2,64,512]{2,1,0:T(8,128)(2,1)S(1)}, u32[]{:S(2)}, u32[]{:S(2)}) collective-permute-start(bf16[2,64,512]{2,1,0:T(8,128)(2,1)S(1)} %select_bitcast_fusion.10), channel_id=1, source_target_pairs={{0,2},{1,3},{2,0},{3,1},{4,6},{5,7},{6,4},{7,5},{8,10},{9,11},{10,... | collective-permute-start | bytes 393224 | tf_op jit(solution)/shard_map/ppermute | solution.py:337
  288.8 8.6 %collective-permute-start.23 = (bf16[2,2,2,16,1536]{4,3,0,1,2:T(8,128)(2,1)S(1)}, bf16[2,2,2,16,1536]{4,3,0,1,2:T(8,128)(2,1)S(1)}, u32[]{:S(2)}, u32[]{:S(2)}) collective-permute-start(bf16[2,2,2,16,1536]{4,3,0,1,2:T(8,128)(2,1)S(1)} %select_bitcast_fusion.5), channel_id=1, source_target_pairs={{0,16},{8,24},{16,0},{24,8},{1,17},{9,25},{17,1},{25,9},{2,18},{10... | collective-permute-start | bytes 1179656 | tf_op jit(solution)/shard_map/ppermute | solution.py:337
  290.1 14.3 %collective-permute-start.41 = (bf16[64,512]{1,0:T(8,128)(2,1)S(1)}, bf16[64,512]{1,0:T(8,128)(2,1)S(1)}, u32[]{:S(2)}, u32[]{:S(2)}) collective-permute-start(bf16[64,512]{1,0:T(8,128)(2,1)S(1)} %select_bitcast_fusion.14), channel_id=1, source_target_pairs={{0,4},{1,5},{2,6},{3,7},{4,0},{5,1},{6,2},{7,3},{8,12},{9,13},{10,... | collective-permute-start | bytes 196616 | tf_op jit(solution)/shard_map/ppermute | solution.py:337
  298.5 10.3 %collective-permute-start.36 = (bf16[16,2048]{1,0:T(8,128)(2,1)S(1)}, bf16[16,2048]{1,0:T(8,128)(2,1)S(1)}, u32[]{:S(2)}, u32[]{:S(2)}) collective-permute-start(bf16[16,2048]{1,0:T(8,128)(2,1)S(1)} %select_bitcast_fusion.15), channel_id=1, source_target_pairs={{0,4},{1,5},{2,6},{3,7},{4,0},{5,1},{6,2},{7,3},{8,12},{9,13},{10,... | collective-permute-start | bytes 196616 | tf_op jit(solution)/shard_map/ppermute | solution.py:337
  (48 other events, 774.3 us)

commit v2 on v1

v2 whole, which is shorter than its diff:
```python
import math
from functools import partial

import jax
import jax.numpy as jnp
from jax import lax
from jax.experimental import pallas as pl
from jax.experimental.pallas import tpu as pltpu
from jax.sharding import PartitionSpec as P

D = 512
HD = 64
FEATS = 256
FF = 2048
CHUNK = 256
SPAN = 1024
ROWS = 512
PAIRS = D // (2 * HD)

bf16 = jnp.bfloat16
f32 = jnp.float32
norm_eps = 1e-06
beta_first = 0.9
beta_second = 0.999
adam_eps = 1e-08
max_norm = 1.0
matrix_rate = 0.08
output_rate = 0.3
gain_rate = 1.5
matrix_decay = 0.1
feature_scale = HD ** (-0.25)
log2e = math.log2(math.e)
AXES = ("head", "row")


def dot(a, b, ca=1, cb=0):
    return lax.dot_general(a, b, (((ca,), (cb,)), ((), ())), preferred_element_type=f32)


def lanes(width):
    return lax.broadcasted_iota(jnp.int32, (1, width), 1)


def half_masks(width):
    first = (lanes(width) % 128 < HD).astype(f32)
    return first.astype(bf16), (1.0 - first).astype(bf16)


def rms_scale(values):
    return lax.rsqrt(jnp.mean(values * values, axis=-1, keepdims=True) + norm_eps)


def features(u, spread):
    raw = dot(u, spread)
    wide = u.astype(f32)
    squares = wide * wide
    own = lanes(2 * HD) < HD
    total_a = jnp.sum(jnp.where(own, squares, 0.0), axis=1, keepdims=True)
    total_b = jnp.sum(jnp.where(own, 0.0, squares), axis=1, keepdims=True)
    c1 = feature_scale * log2e
    c2 = 0.5 * feature_scale * feature_scale * log2e
    down_a = total_a * c2 + 4.0
    down_b = total_b * c2 + 4.0
    left = jnp.exp2(raw[:, :FEATS] * c1 - down_a)
    right = jnp.exp2(raw[:, FEATS:] * c1 - down_b)
    return jnp.concatenate([left, right], axis=1).astype(bf16)


def masked_pair(first, second, width):
    ma, mb = half_masks(width)
    return jnp.concatenate([first * ma, second * mb], axis=0)


def as_column(row):
    return jnp.broadcast_to(row, (8, row.shape[1])).T[:, :1]


def flag(condition):
    return condition.astype(f32).astype(bf16)


def chunk_mask(seg_row):
    seg_col = as_column(seg_row)
    rows = lax.broadcasted_iota(jnp.int32, (CHUNK, CHUNK), 0)
    cols = lax.broadcasted_iota(jnp.int32, (CHUNK, CHUNK), 1)
    return seg_col, flag((rows >= cols) & (seg_col == seg_row))


def forward_kernel(
    ends_ref, xh_ref, xo_ref, seg_ref, wq_ref, spread_ref,
    h1_ref, qkv_ref, pq_ref, pk_ref, p_ref, t_ref, o_ref, of_ref, rden_ref, gains_ref,
    state_ref,
):
    step = pl.program_id(0)
    halo = SPAN // CHUNK
    ones = jnp.ones((CHUNK, 2 * HD), bf16)

    @pl.when(step == 0)
    def _():
        state_ref[...] = jnp.zeros_like(state_ref)
        gains_ref[...] = wq_ref[:, 3 * D :].astype(f32).T[:8]

    gain = gains_ref[0:1]

    @pl.when(step < halo)
    def _():
        x = xh_ref[...].astype(f32)
        h1 = (x * rms_scale(x) * gain).astype(bf16)
        chosen = flag(as_column(seg_ref[0]) == ends_ref[halo - 1])
        for p in range(PAIRS):
            kv = dot(h1, wq_ref[:, 384 * p + 128 : 384 * (p + 1)]).astype(bf16)
            pk = features(kv[:, :128], spread_ref[...])
            vw = jnp.concatenate([kv[:, 128:], ones], axis=1) * chosen
            state_ref[p] = state_ref[p] + dot(pk, vw, 0, 0)

    @pl.when(step >= halo)
    def _():
        before = ends_ref[step - 1]
        last = ends_ref[step]
        x = xo_ref[...].astype(f32)
        h1 = (x * rms_scale(x) * gain).astype(bf16)
        h1_ref[...] = h1
        qkv = dot(h1, wq_ref[:, : 3 * D]).astype(bf16)
        qkv_ref[...] = qkv
        seg_col, allowed = chunk_mask(seg_ref[0])
        chosen = flag(seg_col == last)
        follows = flag(seg_col == before)
        keep = (last == before).astype(f32)
        for p in range(PAIRS):
            cut = slice(128 * p, 128 * (p + 1))
            wide = slice(512 * p, 512 * (p + 1))
            q2 = qkv[:, 384 * p : 384 * p + 128]
            k2 = qkv[:, 384 * p + 128 : 384 * p + 256]
            v2 = qkv[:, 384 * p + 256 : 384 * p + 384]
            pq = features(q2, spread_ref[...])
            pk = features(k2, spread_ref[...])
            pq_ref[:, wide] = pq
            pk_ref[:, wide] = pk
            scores = jnp.concatenate(
                [
                    dot(pq[:, :FEATS], pk[:, :FEATS], 1, 1).astype(bf16) * allowed,
                    dot(pq[:, FEATS:], pk[:, FEATS:], 1, 1).astype(bf16) * allowed,
                ],
                axis=1,
            )
            p_ref[:, wide] = scores
            v1 = jnp.concatenate([v2, ones], axis=1)
            state = state_ref[p]
            narrow = state.astype(bf16)
            narrow = masked_pair(narrow[:FEATS], narrow[FEATS:], 256)
            t_ref[0, p] = narrow
            both = dot(scores, masked_pair(v1, v1, 256)) + dot(pq * follows, narrow)
            rden = 1.0 / both[:, 128:]
            of = both[:, :128] * rden
            rden_ref[:, cut] = rden
            of_ref[:, cut] = of
            o_ref[:, cut] = of.astype(bf16)
            state_ref[p] = keep * state + dot(pk, v1 * chosen, 0, 0)


def middle_kernel(
    group,
    ends_ref, core_ref, x_ref, g_ref, o_ref, of_ref, rden_ref, pq_ref, seg_ref, gains_ref,
    wu0_ref, wu1_ref, wu2_ref, wu3_ref, wd_ref, wo_ref,
    out_ref, dy1_ref, dn_ref, sent_up_ref, sent_rest_ref, kept_up_ref, kept_rest_ref, back_ref,
    up_acc, down_acc, out_acc, back_acc, act_ref, dup_ref,
):
    step = pl.program_id(0)
    steps = pl.num_programs(0)
    cut = 512
    wu_refs = (wu0_ref, wu1_ref, wu2_ref, wu3_ref)
    blocks = wd_ref.shape[0] // len(wu_refs)

    @pl.when(step == 0)
    def _():
        up_acc[...] = jnp.zeros_like(up_acc)
        down_acc[...] = jnp.zeros_like(down_acc)
        out_acc[...] = jnp.zeros_like(out_acc)
        back_acc[...] = jnp.zeros_like(back_acc)

    o = o_ref[...]
    g = g_ref[...]
    gain = gains_ref[1:2]
    wo = wo_ref[...].reshape(D, D)
    y1 = x_ref[...].astype(f32) + dot(o, wo, 1, 1)
    r2 = rms_scale(y1)
    n2 = y1 * r2
    h2 = (n2 * gain).astype(bf16)
    for f in range(FF // cut):
        fs = slice(cut * f, cut * (f + 1))
        wd = wd_ref[blocks * f : blocks * (f + 1)].reshape(cut, D)
        up = dot(h2, wu_refs[f][...].reshape(D, cut))
        d_act = dot(g, wd, 1, 1)
        cdf = 0.5 * (1.0 + lax.erf(up * math.sqrt(0.5)))
        density = jnp.exp(up * up * -0.5) * (1.0 / math.sqrt(2.0 * math.pi))
        act = (up * cdf).astype(bf16)
        d_up = (d_act * (cdf + up * density)).astype(bf16)
        act_ref[:, fs] = act
        dup_ref[:, fs] = d_up
        down_acc[fs, :] += dot(act, g, 0, 0)
        up_acc[:, fs] += dot(h2, d_up, 0, 0)
    out_ref[...] = (y1 + dot(act_ref[...], wd_ref[...].reshape(FF, D))).astype(bf16)
    d_h2 = dot(dup_ref[:, :cut], wu0_ref[...].reshape(D, cut), 1, 1)
    for f in range(1, FF // cut):
        d_h2 = d_h2 + dot(
            dup_ref[:, cut * f : cut * (f + 1)], wu_refs[f][...].reshape(D, cut), 1, 1
        )
    e2 = d_h2 * gain
    dy1 = g.astype(f32) + r2 * (e2 - n2 * jnp.mean(e2 * n2, axis=-1, keepdims=True))
    dy1_ref[...] = dy1
    da = dy1.astype(bf16)
    out_acc[...] += dot(da, o, 0, 0)
    d_o = dot(da, wo)
    product = d_o * of_ref[...]
    high = product.astype(bf16)
    low = (product - high.astype(f32)).astype(bf16)
    rden = rden_ref[...]
    ma, mb = half_masks(128)
    same = jnp.concatenate(
        [jnp.broadcast_to(ma, (HD, 128)), jnp.broadcast_to(mb, (HD, 128))], axis=0
    )
    same = jnp.concatenate([same, same], axis=0)
    lane = lanes(128) % HD
    m0 = (lane == 0).astype(f32).astype(bf16)
    m1 = (lane == 1).astype(f32).astype(bf16)
    for p in range(PAIRS):
        ps = slice(128 * p, 128 * (p + 1))
        total = dot(jnp.concatenate([high[:, ps], low[:, ps]], axis=1), same)
        d_den = -total * rden[:, ps]
        d_hi = d_den.astype(bf16)
        d_lo = (d_den - d_hi.astype(f32)).astype(bf16)
        d_num = (d_o[:, ps] * rden[:, ps]).astype(bf16)
        dn = jnp.concatenate([d_num, d_hi * m0 + d_lo * m1], axis=1)
        dn_ref[:, 256 * p : 256 * (p + 1)] = dn

    @pl.when(step < SPAN // ROWS)
    def _():
        follows = flag(as_column(seg_ref[0]) == ends_ref[SPAN // CHUNK - 1])
        for p in range(PAIRS):
            back_acc[p] = back_acc[p] + dot(
                pq_ref[:, 512 * p : 512 * (p + 1)], dn_ref[:, 256 * p : 256 * (p + 1)] * follows, 0, 0
            )

    @pl.when(step == steps - 1)
    def _():
        core = core_ref[0]
        for ups, others, side in (
            (sent_up_ref, sent_rest_ref, 1 - core),
            (kept_up_ref, kept_rest_ref, core),
        ):
            for far in range(ups.shape[0] // group):
                at = (2 * far + side) * group
                here = slice(group * far, group * (far + 1))
                thin = pl.ds(pl.multiple_of(at * 16, 16), group * 16)
                tall = pl.ds(pl.multiple_of(at * 64, 64), group * 64)
                for f in range(FF // cut):
                    piece = up_acc[thin, cut * f : cut * (f + 1)].astype(bf16)
                    ups[here, 16 * f : 16 * (f + 1)] = piece.reshape(group, 16, cut)
                others[here, :64] = down_acc[tall].astype(bf16).reshape(group, 64, D)
                others[here, 64:] = out_acc[thin].astype(bf16).reshape(group, 16, D)
        for p in range(PAIRS):
            back = back_acc[p].astype(bf16)
            ma2, mb2 = half_masks(256)
            back_ref[p] = back[:FEATS] * ma2 + back[FEATS:] * mb2


def backward_kernel(pairs, ends_ref, seg_ref, gather_ref, *refs):
    refs = refs[: 7 * pairs] + refs[-2:]
    halo = SPAN // CHUNK
    step = pl.program_id(0)
    chunk = pl.num_programs(0) - 1 - step
    before = ends_ref[chunk + halo - 1]
    last = ends_ref[chunk + halo]
    ma2, mb2 = half_masks(256)
    dqkv_ref, state_ref = refs[7 * pairs :]
    back_refs = refs[6 * pairs : 7 * pairs]

    @pl.when(step == 0)
    def _():
        for p in range(pairs):
            state_ref[p, :FEATS] = (back_refs[p][0] * ma2).astype(f32)
            state_ref[p, FEATS:] = (back_refs[p][0] * mb2).astype(f32)

    seg_col, allowed = chunk_mask(seg_ref[0])
    chosen = flag(seg_col == last)
    follows = flag(seg_col == before)
    keep = (last == before).astype(f32)
    two = jnp.broadcast_to(flag(lanes(128) % HD < 2), (CHUNK, 128))
    ones = jnp.ones((CHUNK, 128), bf16)
    ma, mb = half_masks(128)
    for p in range(pairs):
        scores, pq, pk, qkv, dn = [refs[i * pairs + p][...] for i in range(5)]
        narrow = refs[5 * pairs + p][0, 0]
        q2, k2, v2 = qkv[:, :128], qkv[:, 128:256], qkv[:, 256:]
        state = state_ref[p]
        back = state.astype(bf16)
        back = masked_pair(back[:FEATS], back[FEATS:], 256)
        v1 = jnp.concatenate([v2, two], axis=1)
        d_p = dot(dn, masked_pair(v1, v1, 256), 1, 1).astype(bf16)
        d_pa = d_p[:, :CHUNK] * allowed
        d_pb = d_p[:, CHUNK:] * allowed
        dn_f = dn * follows
        d_pq = dot(dn_f, narrow, 1, 1) + jnp.concatenate(
            [dot(d_pa, pk[:, :FEATS]), dot(d_pb, pk[:, FEATS:])], axis=1
        )
        vw = jnp.concatenate([v2, ones], axis=1) * chosen
        d_pk = dot(vw, back, 1, 1) + jnp.concatenate(
            [dot(d_pa, pq[:, :FEATS], 0, 0), dot(d_pb, pq[:, FEATS:], 0, 0)], axis=1
        )
        d_num = dn[:, :128]
        d_v = (
            dot(pk * chosen, back[:, :128])
            + dot(scores[:, :CHUNK], d_num * ma, 0, 0)
            + dot(scores[:, CHUNK:], d_num * mb, 0, 0)
        )
        through_q = dot(d_pq.astype(bf16) * pq, gather_ref[...])
        through_k = dot(d_pk.astype(bf16) * pk, gather_ref[...])
        scale2 = feature_scale * feature_scale
        d_q = through_q[:, :128] * feature_scale - q2.astype(f32) * through_q[:, 128:] * scale2
        d_k = through_k[:, :128] * feature_scale - k2.astype(f32) * through_k[:, 128:] * scale2
        dqkv_ref[:, 384 * p : 384 * p + 128] = d_q.astype(bf16)
        dqkv_ref[:, 384 * p + 128 : 384 * p + 256] = d_k.astype(bf16)
        dqkv_ref[:, 384 * p + 256 : 384 * p + 384] = d_v.astype(bf16)
        state_ref[p] = keep * state + dot(pq, dn_f, 0, 0)


def input_kernel(dqkv_ref, wq_ref, x_ref, dy1_ref, gains_ref, dx_ref):
    d_h1 = dot(dqkv_ref[...], wq_ref[:, : 3 * D], 1, 1)
    x = x_ref[...].astype(f32)
    r1 = rms_scale(x)
    n1 = x * r1
    e1 = d_h1 * gains_ref[0:1]
    dx_ref[...] = dy1_ref[...] + r1 * (e1 - n1 * jnp.mean(e1 * n1, axis=-1, keepdims=True))


def finish_kernel(q_ref, kept_ref, came_ref, packed_ref, later_ref, sq_ref, sr_ref, gg_ref, spread_ref):
    share = q_ref.shape[1]
    sum_q = jnp.sum(q_ref[...].astype(f32), axis=0)
    sum_r = kept_ref[...].astype(f32) + came_ref[...].astype(f32)
    sq_ref[...] = sum_q
    sr_ref[...] = sum_r
    packed = packed_ref[...].astype(f32)
    tops = jnp.sum(packed[:, : 3 * D] * sum_q, axis=1, keepdims=True)
    rows = jnp.sum(later_ref[: 4 * share].astype(f32) * sum_r[: 4 * share], axis=1, keepdims=True)
    lows = rows[:share]
    for f in range(1, 4):
        lows = lows + rows[share * f : share * (f + 1)]
    gg = jnp.concatenate([tops, lows], axis=1) / packed[:, 3 * D : 3 * D + 2]
    gg_ref[...] = gg
    total = jnp.sum(sum_q * sum_q) + jnp.sum(sum_r * sum_r) + jnp.sum(gg * gg)
    spread_ref[...] = jnp.full(spread_ref.shape, total, f32)


def axis_bits():
    row_bits = (lax.axis_size("row") - 1).bit_length()
    head_bits = (lax.axis_size("head") - 1).bit_length()
    row = [("row", b, b) for b in range(row_bits)]
    head = [("head", b, row_bits + b) for b in range(head_bits)]
    return row, head


def swap(value, axis, bit):
    size = lax.axis_size(axis)
    return lax.ppermute(value, axis, [(i, i ^ (1 << bit)) for i in range(size)])


def tied(value, *others):
    return lax.optimization_barrier((value,) + others)[0]


class Gather:
    def __init__(self, shard):
        self.shape = shard.shape
        self.buf = shard
        self.held = []

    def start(self, axis, bit, place):
        self.came = swap(self.buf, axis, bit)
        self.mine = (lax.axis_index(axis) >> bit) & 1
        self.place = place

    def finish(self, *others):
        own = tied(self.buf, *others) if others else self.buf
        at = sum(1 for h in self.held if h > self.place)
        self.buf = jnp.where(
            self.mine == 0,
            jnp.stack([own, self.came], axis=at),
            jnp.stack([self.came, own], axis=at),
        )
        self.held = sorted(self.held + [self.place], reverse=True)

    def whole(self):
        return self.buf.reshape((-1,) + self.shape[1:])


class Halving:
    def __init__(self, kept, came, places):
        self.places = sorted(places, reverse=True)
        self.parts = [kept] if came is None else [kept, came]
        self.parts = [self.split(part) for part in self.parts]

    def split(self, part):
        inner = part.shape[1:] if part.ndim == 3 else part.shape[-2:]
        return part.reshape((2,) * len(self.places) + inner)

    def take(self, index, at):
        total = sum(
            lax.dynamic_index_in_dim(part, index, at, keepdims=False).astype(f32)
            for part in self.parts
        )
        return total.astype(bf16)

    def after(self, *others):
        self.parts[0] = tied(self.parts[0], *others)
        return self

    def send(self, axis, bit, place):
        at = self.places.index(place)
        mine = (lax.axis_index(axis) >> bit) & 1
        sent = self.take(1 - mine, at)
        came = swap(sent, axis, bit)
        self.parts = [self.take(mine, at), came]
        self.places.remove(place)
        return sent

    def total(self):
        return sum(part.astype(f32) for part in self.parts)


def ups_by_device(blocks, share):
    ups = blocks.reshape(-1, 4, 16 // share, share, 512)
    return ups.transpose(0, 2, 1, 3, 4).reshape(-1, 4 * share, 512)


def rest_by_device(blocks, share):
    downs = blocks[:, :64].reshape(-1, 4 * share, 512)
    outs = blocks[:, 64:].reshape(-1, share, 512)
    return jnp.concatenate([downs, outs], axis=1)


def core_groups():
    heads, rows = lax.axis_size("head"), lax.axis_size("row")
    return [[h * rows + r for h in range(c, heads, 2) for r in range(rows)] for c in (0, 1)]


def exchange(blocks):
    return lax.all_to_all(
        blocks, AXES, split_axis=0, concat_axis=0, axis_index_groups=core_groups(), tiled=True
    )


def total_of(spread):
    came = lax.all_to_all(spread, AXES, split_axis=0, concat_axis=0, tiled=True)
    return jnp.sum(came[:, 0, 0])


def adam_update(
    weight, gradient, first_moment, second_moment, clip_factor, step_value, step_rate, decay_rate
):
    clipped = gradient * clip_factor
    next_first = beta_first * first_moment + (1.0 - beta_first) * clipped
    next_second = beta_second * second_moment + (1.0 - beta_second) * clipped * clipped
    first_hat = next_first / (1.0 - beta_first**step_value)
    second_hat = next_second / (1.0 - beta_second**step_value)
    updated = weight - step_rate * (
        first_hat / (jnp.sqrt(second_hat) + adam_eps) + decay_rate * weight
    )
    return (clipped, next_first, next_second, updated)


def params(limit=60):
    return pltpu.CompilerParams(
        dimension_semantics=("arbitrary",), vmem_limit_bytes=limit << 20
    )


def cost(us):
    return pl.CostEstimate(flops=us * 50000000, transcendentals=0, bytes_accessed=us * 150000)


def fixed(shape):
    zeros = (0,) * len(shape)
    return pl.BlockSpec(shape, lambda *_: zeros, pipeline_mode=pl.Buffered(1))


def per_device(
    inputs,
    cotangent,
    segments,
    feature_matrix,
    w_qkv,
    w_out,
    w_up,
    w_down,
    gains,
    first_qkv,
    second_qkv,
    first_out,
    second_out,
    first_up,
    second_up,
    first_down,
    second_down,
    first_gains,
    second_gains,
    step_count,
):
    heads = lax.axis_size("head")
    row_bits, head_bits = axis_bits()
    x = inputs[0]
    g = cotangent[0]
    length = x.shape[0]
    chunks = length // CHUNK
    halo = SPAN // CHUNK
    share = w_qkv.shape[0]
    group = lax.axis_size("row") * share // 16

    packed = jnp.concatenate(
        [
            w_qkv.reshape(share, 3, PAIRS, 128).transpose(0, 2, 1, 3).reshape(share, 3 * D),
            gains,
            jnp.zeros((share, 126), f32),
        ],
        axis=1,
    ).astype(bf16)
    forward_pairs = [(i, i + 1) for i in range(heads - 1)]
    backward_pairs = [(i + 1, i) for i in range(heads - 1)]
    weights = Gather(packed)
    order = row_bits[::-1] + head_bits[::-1]
    weights.start(*order[0])
    later = jnp.concatenate(
        [w_up[:, 512 * j : 512 * (j + 1)] for j in range(FF // 512)] + [w_down, w_out], axis=0
    ).astype(bf16)
    tail = x[length - SPAN :]
    x_ahead = lax.ppermute(tail, "head", forward_pairs)
    weights.finish(tail)
    later_own = tied(later, weights.buf)
    later = lax.all_gather(later_own, AXES, axis=0)
    if share != 16:
        parts = 16 // share
        later = later.reshape(D // 16, parts, 9 * share, 512)
        ups = later[:, :, : 4 * share].reshape(D // 16, parts, 4, share, 512)
        ups = ups.transpose(0, 2, 1, 3, 4).reshape(D // 16, 64, 512)
        downs = later[:, :, 4 * share : 8 * share].reshape(D // 16, 64, 512)
        outs = later[:, :, 8 * share :].reshape(D // 16, 16, 512)
        later = jnp.concatenate([ups, downs, outs], axis=1)

    weights.start(*order[1])
    row_segments = tied(segments[0], weights.buf)
    padded = jnp.concatenate([jnp.full((SPAN,), -1, jnp.int32), row_segments])
    near = lax.dynamic_slice_in_dim(padded, lax.axis_index("head") * length, length + SPAN)
    ends = near[CHUNK - 1 :: CHUNK]
    seg_rows = near.astype(f32).reshape(-1, 1, CHUNK)
    near_rows = near[SPAN : 2 * SPAN].astype(f32).reshape(-1, 1, ROWS)
    fm = feature_matrix
    nothing = jnp.zeros_like(fm.T)
    spread = jnp.concatenate(
        [
            jnp.concatenate([fm.T, nothing], axis=1),
            jnp.concatenate([nothing, fm.T], axis=1),
        ],
        axis=0,
    )
    zero = jnp.zeros((FEATS, HD), bf16)
    one = jnp.ones((FEATS, HD), bf16)
    gather = jnp.concatenate(
        [
            jnp.concatenate([fm, zero, one, zero], axis=1),
            jnp.concatenate([zero, fm, zero, one], axis=1),
        ],
        axis=0,
    )
    weights.finish(ends, seg_rows, near_rows)
    weights.start(*order[2])
    weights.finish(spread, gather, x_ahead)
    for stage in order[3:]:
        weights.start(*stage)
        weights.finish()
    wq = weights.whole()
    core = (lax.axis_index("head") & 1).reshape(1)

    def own(shape):
        rest = (0,) * (len(shape) - 1)
        return pl.BlockSpec(shape, lambda c, *_: (jnp.maximum(c - halo, 0),) + rest)

    wide = PAIRS * 2 * FEATS
    h1, qkv, pq, pk, scores, states, o, of, rden, gain_rows = pl.pallas_call(
        forward_kernel,
        grid_spec=pltpu.PrefetchScalarGridSpec(
            num_scalar_prefetch=1,
            grid=(halo + chunks,),
            in_specs=[
                pl.BlockSpec((CHUNK, D), lambda c, *_: (jnp.minimum(c, halo - 1), 0)),
                own((CHUNK, D)),
                pl.BlockSpec((1, 1, CHUNK), lambda c, *_: (c, 0, 0)),
                fixed((D, 3 * D + 128)),
                fixed((2 * HD, 2 * FEATS)),
            ],
            out_specs=[
                own((CHUNK, D)),
                own((CHUNK, 3 * D)),
                own((CHUNK, wide)),
                own((CHUNK, wide)),
                own((CHUNK, wide)),
                own((1, PAIRS, 2 * FEATS, 256)),
                own((CHUNK, D)),
                own((CHUNK, D)),
                own((CHUNK, D)),
                fixed((8, D)),
            ],
            scratch_shapes=[pltpu.VMEM((PAIRS, 2 * FEATS, 256), f32)],
        ),
        out_shape=[
            jax.ShapeDtypeStruct((length, D), bf16),
            jax.ShapeDtypeStruct((length, 3 * D), bf16),
            jax.ShapeDtypeStruct((length, wide), bf16),
            jax.ShapeDtypeStruct((length, wide), bf16),
            jax.ShapeDtypeStruct((length, wide), bf16),
            jax.ShapeDtypeStruct((chunks, PAIRS, 2 * FEATS, 256), bf16),
            jax.ShapeDtypeStruct((length, D), bf16),
            jax.ShapeDtypeStruct((length, D), f32),
            jax.ShapeDtypeStruct((length, D), f32),
            jax.ShapeDtypeStruct((8, D), f32),
        ],
        compiler_params=params(),
        cost_estimate=cost(35),
        name="forward",
    )(ends, x_ahead, x, seg_rows, wq, spread)

    def by_step(shape):
        rest = (0,) * (len(shape) - 1)
        return pl.BlockSpec(shape, lambda c, *_: (c,) + rest)

    near_steps = SPAN // ROWS

    def columns(block):
        return pl.BlockSpec(
            (D // 16, 16, 512), lambda *_: (0, block, 0), pipeline_mode=pl.Buffered(1)
        )

    out_act, dy1, dn, sent_up, sent_rest, kept_up, kept_rest, back = pl.pallas_call(
        partial(middle_kernel, group),
        grid_spec=pltpu.PrefetchScalarGridSpec(
            num_scalar_prefetch=2,
            grid=(length // ROWS,),
            in_specs=[
                by_step((ROWS, D)),
                by_step((ROWS, D)),
                by_step((ROWS, D)),
                by_step((ROWS, D)),
                by_step((ROWS, D)),
                pl.BlockSpec((ROWS, wide), lambda c, *_: (jnp.minimum(c, near_steps - 1), 0)),
                pl.BlockSpec((1, 1, ROWS), lambda c, *_: (jnp.minimum(c, near_steps - 1), 0, 0)),
                fixed((8, D)),
                columns(0),
                columns(1),
                columns(2),
                columns(3),
                pl.BlockSpec(
                    (D // 16, 64, 512), lambda *_: (0, 1, 0), pipeline_mode=pl.Buffered(1)
                ),
                columns(8),
            ],
            out_specs=[
                by_step((ROWS, D)),
                by_step((ROWS, D)),
                by_step((ROWS, PAIRS * 256)),
                fixed((D // 32, 64, 512)),
                fixed((D // 32, 80, 512)),
                fixed((D // 32, 64, 512)),
                fixed((D // 32, 80, 512)),
                fixed((PAIRS, FEATS, 256)),
            ],
            scratch_shapes=[
                pltpu.VMEM((D, FF), f32),
                pltpu.VMEM((FF, D), f32),
                pltpu.VMEM((D, D), f32),
                pltpu.VMEM((PAIRS, 2 * FEATS, 256), f32),
                pltpu.VMEM((ROWS, FF), bf16),
                pltpu.VMEM((ROWS, FF), bf16),
            ],
        ),
        out_shape=[
            jax.ShapeDtypeStruct((length, D), bf16),
            jax.ShapeDtypeStruct((length, D), f32),
            jax.ShapeDtypeStruct((length, PAIRS * 256), bf16),
            jax.ShapeDtypeStruct((D // 32, 64, 512), bf16),
            jax.ShapeDtypeStruct((D // 32, 80, 512), bf16),
            jax.ShapeDtypeStruct((D // 32, 64, 512), bf16),
            jax.ShapeDtypeStruct((D // 32, 80, 512), bf16),
            jax.ShapeDtypeStruct((PAIRS, FEATS, 256), bf16),
        ],
        compiler_params=params(),
        cost_estimate=cost(48),
        name="middle",
    )(
        ends, core, x, g, o, of, rden, pq, near_rows, gain_rows,
        later, later, later, later, later, later,
    )

    if share != 16:
        sent_up, kept_up = ups_by_device(sent_up, share), ups_by_device(kept_up, share)
        sent_rest, kept_rest = rest_by_device(sent_rest, share), rest_by_device(kept_rest, share)
    back_in = lax.ppermute(back, "head", backward_pairs)
    came_up = swap(sent_up, "head", 0)
    came_rest = swap(sent_rest, "head", 0)

    def attention_back(at, back_in, *written):
        chosen = range(at * PAIRS // 2, (at + 1) * PAIRS // 2)
        count = len(chosen)

        def falling(shape, at=0):
            rest = (0,) * (len(shape) - 2)
            return pl.BlockSpec(shape, lambda c, *_: (chunks - 1 - c, at) + rest)

        def state(at):
            return pl.BlockSpec(
                (1, FEATS, 256), lambda *_: (at, 0, 0), pipeline_mode=pl.Buffered(1)
            )

        specs = [pl.BlockSpec((1, 1, CHUNK), lambda c, *_: (chunks + halo - 1 - c, 0, 0))]
        specs += [fixed((2 * FEATS, 256))]
        for shape in ((CHUNK, 512),) * 3 + ((CHUNK, 384), (CHUNK, 256), (1, 1, 512, 256)):
            specs += [falling(shape, p) for p in chosen]
        specs += [state(p) for p in chosen]
        operands = []
        for array in (scores, pq, pk, qkv, dn, states, back_in):
            operands += [array] * count
        return pl.pallas_call(
            partial(backward_kernel, count),
            grid_spec=pltpu.PrefetchScalarGridSpec(
                num_scalar_prefetch=1,
                grid=(chunks,),
                in_specs=specs + [pl.BlockSpec(memory_space=pl.ANY)] * len(written),
                out_specs=falling((CHUNK, 384 * count), at),
                scratch_shapes=[pltpu.VMEM((count, 2 * FEATS, 256), f32)],
            ),
            out_shape=jax.ShapeDtypeStruct((length, 3 * D), bf16),
            input_output_aliases={3 + len(operands): 0} if written else {},
            compiler_params=params(),
            cost_estimate=cost(8 * count),
            name="backward",
        )(ends, seg_rows, gather, *operands, *written)

    core_bit, *far_bits = head_bits
    places = [place for _, _, place in far_bits + row_bits]
    lower = [(axis, bit, place - (place > core_bit[2])) for axis, bit, place in far_bits]
    first_order = lower + row_bits[:1]
    second_order = row_bits[:1] + lower
    last_order = row_bits[1:]
    places = [place for _, _, place in first_order + last_order]
    cut = 4 * share

    dqkv = attention_back(0, tied(back_in, sent_up, sent_rest))
    kept_up, kept_rest = tied(kept_up, dqkv), tied(kept_rest, dqkv)
    first = Halving(kept_up, came_up, places)
    second = Halving(kept_rest, came_rest, places)
    back_in = tied(back_in, first.send(*first_order[0]), second.send(*second_order[0]))
    dqkv = attention_back(1, back_in, dqkv)

    ready = tied(h1, dqkv, first.parts[1], second.parts[1])
    g_qkv = dot(ready, dqkv, 0, 0).astype(bf16).reshape(heads // 2, 2, -1, 3 * D)
    sent_qkv = lax.dynamic_index_in_dim(g_qkv, 1 - core[0], 1, False)
    came_qkv = swap(sent_qkv, "head", 0)
    moved = []
    for left, right in zip(first_order[1:], second_order[1:]):
        moved.append(first.after(sent_qkv).send(*left))
        moved.append(second.after(sent_qkv).send(*right))
    kept_qkv = tied(lax.dynamic_index_in_dim(g_qkv, core[0], 1, False), *moved)
    merged_qkv = (kept_qkv.astype(f32) + came_qkv.astype(f32)).astype(bf16)
    all_qkv = exchange(merged_qkv.reshape(-1, share, 3 * D))
    dx = pl.pallas_call(
        input_kernel,
        grid=(length // ROWS,),
        in_specs=[
            by_step((ROWS, 3 * D)),
            fixed((D, 3 * D + 128)),
            by_step((ROWS, D)),
            by_step((ROWS, D)),
            fixed((8, D)),
        ],
        out_specs=by_step((ROWS, D)),
        out_shape=jax.ShapeDtypeStruct((length, D), f32),
        compiler_params=params(),
        cost_estimate=cost(10),
        name="input_grad",
    )(dqkv, wq, x, tied(dy1, merged_qkv), gain_rows)
    left, right = [[tied(part, dx) for part in h.parts] for h in (first, second)]
    rest = Halving(jnp.concatenate([left[0], right[0]], axis=-2), None, first.places)
    rest.parts.append(jnp.concatenate([left[1], right[1]], axis=-2))
    for stage in last_order:
        rest.send(*stage)
    kept, came = rest.parts
    count = lax.axis_size(AXES)
    sum_qkv, sums, sum_gains, spread = pl.pallas_call(
        finish_kernel,
        out_shape=[
            jax.ShapeDtypeStruct((share, 3 * D), f32),
            jax.ShapeDtypeStruct((9 * share, 512), f32),
            jax.ShapeDtypeStruct((share, 2), f32),
            jax.ShapeDtypeStruct((count, 8, 128), f32),
        ],
        name="finish",
    )(all_qkv, kept, came, packed, later_own)
    total_squares = total_of(spread)
    sum_qkv = sum_qkv.reshape(share, PAIRS, 3, 128).transpose(0, 2, 1, 3).reshape(share, 3, D)
    sum_up = sums[: 4 * share].reshape(4, share, 512).transpose(1, 0, 2).reshape(share, FF)
    sum_down = sums[4 * share : 8 * share]
    sum_out = sums[8 * share :]
    reduced = (sum_qkv, sum_out, sum_up, sum_down, sum_gains)
    grad_norm = jnp.sqrt(total_squares)
    clip_factor = jnp.minimum(1.0, max_norm / (grad_norm + 1e-06))
    step_value = step_count.astype(f32)
    update = partial(adam_update, clip_factor=clip_factor, step_value=step_value)
    qkv_parts = update(
        w_qkv, reduced[0], first_qkv, second_qkv, step_rate=matrix_rate, decay_rate=matrix_decay
    )
    out_parts = update(
        w_out, reduced[1], first_out, second_out, step_rate=output_rate, decay_rate=matrix_decay
    )
    up_parts = update(
        w_up, reduced[2], first_up, second_up, step_rate=matrix_rate, decay_rate=matrix_decay
    )
    down_parts = update(
        w_down, reduced[3], first_down, second_down, step_rate=matrix_rate, decay_rate=matrix_decay
    )
    gain_parts = update(
        gains, reduced[4], first_gains, second_gains, step_rate=gain_rate, decay_rate=0.0
    )
    return (
        (out_act[None], dx[None], grad_norm)
        + qkv_parts
        + out_parts
        + up_parts
        + down_parts
        + gain_parts
    )


def solution(mesh):
    token = P("row", "head", None)
    three = P(AXES, None, None)
    two = P(AXES, None)
    placed = (token, token, P("row", None), P(), three, two, two, two, two)
    placed = placed + (three, three) + (two,) * 8 + (P(),)
    return jax.shard_map(
        per_device,
        mesh=mesh,
        in_specs=placed,
        out_specs=(token, token, P()) + (three,) * 4 + (two,) * 16,
        check_vma=False,
    )
```

time: 344 us -> 273 us (0.79)
  waiting for transfers between devices: 104 us -> 48.1 us
  starting transfers between devices: 54.9 us -> 38.5 us
  other arithmetic: 27.4 us -> 16.5 us
  Pallas kernels: 126 us -> 135 us
  between operations: 10.1 us -> 17.3 us
  local copies, waits for them, and re-layouts: 17.2 us -> 10.5 us
    ppermute x50 -> x14, waiting for transfers between devices: 104 us -> 37.7 us  [swap(): return lax.ppermute(value, axis, [(i, i ^ 1 << bit) for i in range(size)])]
    ppermute x50 -> x14, starting transfers between devices: 51.1 us -> 26.5 us  [swap(): return lax.ppermute(value, axis, [(i, i ^ 1 << bit) for i in range(size)])]
    all_to_all x0 -> x2, starting transfers between devices: none -> 9.32 us  [the longest x1 5.71 us: exchange(): lax.all_to_all(blocks, AXES, split_axis=0, concat_axis=0, axis_index_grou...]
    select_n x56 -> x7, other arithmetic: 9.8 us -> 0.85 us  [finish(): jnp.where(self.mine == 0, jnp.stack([own, self.came], axis=at), jnp.stack...]
    slice x10 -> x1, local copies, waits for them, and re-layouts: 8.67 us -> 1.29 us  [per_device(): tail = x[length - SPAN:]]
    all_to_all x0 -> x2, waiting for transfers between devices: none -> 6.63 us  [the longest x1 6.63 us: total_of(): came = lax.all_to_all(spread, AXES, split_axis=0, concat_axis=0, tiled=True)]
    pallas_call x2 -> x4, Pallas kernels: 80.4 us -> 86.6 us  [the longest x1 47.5 us: per_device(): pl.pallas_call(partial(middle_kernel, group), grid_spec=pltpu.PrefetchSca...]
    unnamed x58 -> x72, local copies, waits for them, and re-layouts: 0.35 us -> 4.82 us
  transfers between devices with their start and end apart: 52 -> 19, of which waited for: 31 -> 11; matrix products, arithmetic and copies ran while one was open for 11% -> 4% of each run, Pallas kernels for 22% -> 31%
where the time goes in v2:
time: 273 us; the launch traced here: 272 us
  Pallas kernels  135 us (49%)
  waiting for transfers between devices  48.1 us (18%)
  starting transfers between devices  38.5 us (14%)
  between operations  17.3 us (6%)
  other arithmetic  16.5 us (6%)
  local copies, waits for them, and re-layouts  10.5 us (4%)
  matrix products  6.88 us (3%)
    pallas_call x1, Pallas kernels, per_device(): pl.pallas_call(partial(middle_kernel, group), grid_spec=pltpu.PrefetchSca...  47.5 us
    pallas_call x1, Pallas kernels, per_device(): pl.pallas_call(forward_kernel, grid_spec=pltpu.PrefetchScalarGridSpec(num...  38.4 us
    ppermute x14, waiting for transfers between devices, swap(): return lax.ppermute(value, axis, [(i, i ^ 1 << bit) for i in range(size)])  37.7 us
    pallas_call x2, Pallas kernels, attention_back(): pl.pallas_call(partial(backward_kernel, count), grid_spec=pltpu.PrefetchS...  36.8 us
    ppermute x14, starting transfers between devices, swap(): return lax.ppermute(value, axis, [(i, i ^ 1 << bit) for i in range(size)])  26.5 us
    pallas_call x1, Pallas kernels, per_device(): pl.pallas_call(input_kernel, grid=(length // ROWS,), in_specs=[by_step((R...  9.65 us
    dot_general x1, matrix products, dot(): lax.dot_general(a, b, (((ca,), (cb,)), ((), ())), preferred_element_type=...  6.88 us
    all_to_all x1, waiting for transfers between devices, total_of(): came = lax.all_to_all(spread, AXES, split_axis=0, concat_axis=0, tiled=True)  6.63 us
  transfers between devices with their start and end apart: 19, of which 11 were waited for; matrix products, arithmetic and copies ran while one was open for 4% of the time, Pallas kernels for 31%

profile of v2, /device:TPU:0, one launch (start us, length us, event | category | flops | bytes accessed | tf_op | source)
XLA Modules:
  0.0 272.3 jit_solution(2981970775312264516)
XLA Ops:
  9.3 4.0 %collective-permute-start = (bf16[16,1664]{1,0:T(8,128)(2,1)S(1)}, bf16[16,1664]{1,0:T(8,128)(2,1)S(1)}, u32[]{:S(2)}, u32[]{:S(2)}) collective-permute-start(bf16[16,1664]{1,0:T(8,128)(2,1)S(1)} %concatenate.81.packed_ref), channel_id=1, source_target_pairs={{0,4},{1,5},{2,6},{3,7},{4,0},{5,1},{6,2},{7,3},{8,12},{9,13},{10,... | collective-permute-start | bytes 159752 | tf_op jit(solution)/shard_map/ppermute | solution.py:364
  17.6 1.4 collective-permute-start.2
  20.8 1.6 collective-permute-done.2
  22.4 1.8 collective-permute-start.3
  25.8 5.6 %collective-permute-done.3 = bf16[2,2,16,1664]{3,2,0,1:T(8,128)(2,1)S(1)} collective-permute-done((bf16[2,2,16,1664]{3,2,0,1:T(8,128)(2,1)S(1)}, bf16[2,2,16,1664]{3,2,0,1:T(8,128)(2,1)S(1)}, u32[]{:S(2)}, u32[]{:S(2)}) %collective-permute-start.3) | collective-permute-done | bytes 213024 | tf_op jit(solution)/shard_map/ppermute | solution.py:364
  31.5 3.6 %collective-permute-start.4 = (bf16[2,2,2,16,1664]{4,3,0,1,2:T(8,128)(2,1)S(1)}, bf16[2,2,2,16,1664]{4,3,0,1,2:T(8,128)(2,1)S(1)}, u32[]{:S(2)}, u32[]{:S(2)}) collective-permute-start(bf16[2,2,2,16,1664]{4,3,0,1,2:T(8,128)(2,1)S(1)} %maximum_select_fusion.4), channel_id=1, source_target_pairs={{0,16},{8,24},{16,0},{24,8},{1,17},{9,25},{17,1},{25,9},{2,18},{10... | collective-permute-start | bytes 1277960 | tf_op jit(solution)/shard_map/ppermute | solution.py:364
  35.2 9.3 %collective-permute-done.4 = bf16[2,2,2,16,1664]{4,3,0,1,2:T(8,128)(2,1)S(1)} collective-permute-done((bf16[2,2,2,16,1664]{4,3,0,1,2:T(8,128)(2,1)S(1)}, bf16[2,2,2,16,1664]{4,3,0,1,2:T(8,128)(2,1)S(1)}, u32[]{:S(2)}, u32[]{:S(2)}) %collective-permute-start.4) | collective-permute-done | bytes 426016 | tf_op jit(solution)/shard_map/ppermute | solution.py:364
  44.9 2.1 collective-permute-done.5
  47.4 1.4 copy.116
  48.8 38.4 %forward.1 = (bf16[2048,512]{1,0:T(8,128)(2,1)}, bf16[2048,1536]{1,0:T(8,128)(2,1)}, bf16[2048,2048]{1,0:T(8,128)(2,1)}, bf16[2048,2048]{1,0:T(8,128)(2,1)}, bf1...) custom-call(s32[12]{0:T(128)} %slice.50.ends_ref, ...), custom_call_target="tpu_custom_call" | custom-call | flops 1750000000 | bytes 5250000 | tf_op jit(solution)/shard_map/forward/pallas_call | solution.py:587
  87.2 47.5 %middle.1 = (bf16[2048,512]{1,0:T(8,128)(2,1)}, f32[2048,512]{1,0:T(8,128)}, bf16[2048,1024]{1,0:T(8,128)(2,1)}, bf16[16,64,512]{2,1,0:T(8,128)(2,1)}, bf16[16,8...) custom-call(s32[12]{0:T(128)} %slice.50.ends_ref, ...), custom_call_target="tpu_custom_call" | custom-call | flops 2400000000 | bytes 7200000 | tf_op jit(solution)/shard_map/middle/pallas_call | solution.py:641
  136.5 3.7 %collective-permute-done.6.refs_12_.refs_13_ = bf16[4,256,256]{2,1,0:T(8,128)(2,1)S(1)} collective-permute-done((bf16[4,256,256]{2,1,0:T(8,128)(2,1)}, bf16[4,256,256]{2,1,0:T(8,128)(2,1)S(1)}, u32[]{:S(2)}, u32[]{:S(2)}) %collective-permute-start.6) | collective-permute-done | bytes 524320 | tf_op jit(solution)/shard_map/ppermute | solution.py:704
  141.0 18.6 %backward.2.refs_14_ = bf16[2048,1536]{1,0:T(8,128)(2,1)} custom-call(s32[12]{0:T(128)} %slice.50.ends_ref, f32[12,1,256]{2,1,0:T(1,128)} %bitcast.124, bf16[512,256]{1,0:T(8,128)(2,1)} %maximum_maximum_fusion.gather_ref, bf16[2048,2048]{1,0:T(8,128)(2,1)} %get-tuple-element.74.refs_0_.refs_1_, bf16[2048,2048]{1,0:T(8,128)(2,1)} %get-tuple-element.74.refs_0_.refs_1_, ...), custom_call_target="tpu_custom_call" | custom-call | flops 800000000 | bytes 2400000 | tf_op jit(solution)/shard_map/backward/pallas_call | solution.py:729
  159.7 1.4 constant_dynamic-slice_fusion
  162.5 1.5 collective-permute-start.10
  164.2 5.7 %collective-permute-start.9 = (bf16[2,2,2,64,512]{4,3,1,0,2:T(8,128)(2,1)S(1)}, bf16[2,2,2,64,512]{4,3,1,0,2:T(8,128)(2,1)}, u32[]{:S(2)}, u32[]{:S(2)}) collective-permute-start(bf16[2,2,2,64,512]{4,3,1,0,2:T(8,128)(2,1)S(1)} %fusion.2), channel_id=1, source_target_pairs={{0,16},{8,24},{16,0},{24,8},{1,17},{9,25},{17,1},{25,9},{2,18},{10... | collective-permute-start | bytes 1572872 | tf_op jit(solution)/shard_map/ppermute | solution.py:364
  169.9 18.2 %backward.3.dqkv_ref = bf16[2048,1536]{1,0:T(8,128)(2,1)} custom-call(s32[12]{0:T(128)} %slice.50.ends_ref, f32[12,1,256]{2,1,0:T(1,128)} %bitcast.125, bf16[512,256]{1,0:T(8,128)(2,1)} %maximum_maximum_fusion.gather_ref, bf16[2048,2048]{1,0:T(8,128)(2,1)} %get-tuple-element.74.refs_0_.refs_1_, ...), custom_call_target="tpu_custom_call", output_to_operand_aliasing={{}: (17, {})} | custom-call | flops 800000000 | bytes 2400000 | tf_op jit(solution)/shard_map/backward/pallas_call | solution.py:729
  188.1 6.9 %convolution_convert_fusion = bf16[512,1536]{1,0:T(8,128)(2,1)S(1)} fusion(bf16[2048,512]{1,0:T(8,128)(2,1)} %get-tuple-element.90, bf16[2048,1536]{1,0:T(8,128)(2,1)} %backward.3.dqkv_ref), kind=kOutput, calls=%fused_computation | convolution fusion | flops 3222011904 | bytes 9961472 | tf_op jit(solution)/shard_map/dot_general | solution.py:37
  198.6 5.7 %all-to-all-start = ((bf16[16,16,1536]{2,1,0:T(8,128)(2,1)}), bf16[16,16,1536]{2,1,0:T(8,128)(2,1)S(1)}, u32[]{:S(2)}, u32[]{:S(2)}) async-start(bf16[16,16,1536]{2,1,0:T(8,128)(2,1)} %bitcast.38), calls=%async_computation | async-start | bytes 1572864 | tf_op jit(solution)/shard_map/all_to_all | solution.py:447
  204.3 1.9 collective-permute-start.13
  206.2 1.5 collective-permute-start.12
  207.7 9.7 %input_grad.1 = f32[2048,512]{1,0:T(8,128)} custom-call(bf16[2048,1536]{1,0:T(8,128)(2,1)} %backward.3.dqkv_ref, bf16[512,1664]{1,0:T(8,128)(2,1)} %bitcast.97, bf16[2048,512]{1,0:T(8,128)(2,1)} %bitcast.95, f32[2048,512]{1,0:T(8,128)} %get-tuple-element.94.dy1_ref, f32[8,512]{1,0:T(8,128)} %get-tuple-element.71.gains_ref), custom_call_target="tpu_custom_call" | custom-call | flops 500000000 | bytes 1500000 | tf_op jit(solution)/shard_map/input_grad/pallas_call | solution.py:772
  217.3 4.1 %collective-permute-done.13 = bf16[2,2,80,512]{3,2,1,0:T(8,128)(2,1)S(1)} collective-permute-done((bf16[2,2,80,512]{3,2,1,0:T(8,128)(2,1)S(1)}, bf16[2,2,80,512]{3,2,1,0:T(8,128)(2,1)S(1)}, u32[]{:S(2)}, u32[]{:S(2)}) %collective-permute-start.13) | collective-permute-done | bytes 327712 | tf_op jit(solution)/shard_map/ppermute | solution.py:364
  221.8 2.1 collective-permute-start.14
  223.9 6.6 %collective-permute-done.14 = bf16[2,144,512]{2,1,0:T(8,128)(2,1)S(1)} collective-permute-done((bf16[2,144,512]{2,1,0:T(8,128)(2,1)S(1)}, bf16[2,144,512]{2,1,0:T(8,128)(2,1)S(1)}, u32[]{:S(2)}, u32[]{:S(2)}) %collective-permute-start.14) | collective-permute-done | bytes 294944 | tf_op jit(solution)/shard_map/ppermute | solution.py:364
  231.3 2.1 collective-permute-start.15
  233.4 6.5 %collective-permute-done.15.came_ref = bf16[144,512]{1,0:T(8,128)(2,1)S(1)} collective-permute-done((bf16[144,512]{1,0:T(8,128)(2,1)S(1)}, bf16[144,512]{1,0:T(8,128)(2,1)S(1)}, u32[]{:S(2)}, u32[]{:S(2)}) %collective-permute-start.15) | collective-permute-done | bytes 147488 | tf_op jit(solution)/shard_map/ppermute | solution.py:364
  240.9 2.4 finish.1
  243.3 3.6 %all-to-all-start.1 = ((f32[32,8,128]{2,1,0:T(8,128)}), f32[32,8,128]{2,1,0:T(8,128)S(1)}, u32[]{:S(2)}, u32[]{:S(2)}) async-start(f32[32,8,128]{2,1,0:T(8,128)} %get-tuple-element.99), calls=%async_computation.1 | async-start | bytes 262144 | tf_op jit(solution)/shard_map/all_to_all | solution.py:453
  248.0 6.6 %all-to-all-done.1 = f32[32,8,128]{2,1,0:T(8,128)S(1)} async-done(((f32[32,8,128]{2,1,0:T(8,128)}), f32[32,8,128]{2,1,0:T(8,128)S(1)}, u32[]{:S(2)}, u32[]{:S(2)}) %all-to-all-start.1) | async-done | bytes 131104 | tf_op jit(solution)/shard_map/all_to_all | solution.py:453
  259.3 1.8 multiply_subtract_fusion
  261.3 1.5 multiply_subtract_fusion.3
  (142 shorter events, 26.3 us)
Async XLA Ops:
  7.2 79.9 %all-gather.3.cloned.1.call-start = ((), (), s32[]{:S(2)}) async-start(), calls=%async_computation.2 | async-start | bytes 4866048 | tf_op jit(solution)/shard_map/all_gather | solution.py:538
  9.3 6.7 %collective-permute-start = (bf16[16,1664]{1,0:T(8,128)(2,1)S(1)}, bf16[16,1664]{1,0:T(8,128)(2,1)S(1)}, u32[]{:S(2)}, u32[]{:S(2)}) collective-permute-start(bf16[16,1664]{1,0:T(8,128)(2,1)S(1)} %concatenate.81.packed_ref), channel_id=1, source_target_pairs={{0,4},{1,5},{2,6},{3,7},{4,0},{5,1},{6,2},{7,3},{8,12},{9,13},{10,... | collective-permute-start | bytes 159752 | tf_op jit(solution)/shard_map/ppermute | solution.py:364
  16.1 9.7 %collective-permute-start.1 = (bf16[1024,512]{1,0:T(8,128)(2,1)S(1)}, bf16[1024,512]{1,0:T(8,128)(2,1)S(1)}, u32[]{:S(2)}, u32[]{:S(2)}) collective-permute-start(bf16[1024,512]{1,0:T(8,128)(2,1)S(1)} %slice_bitcast_fusion), channel_id=1, source_target_pairs={{0,8},{8,16},{16,24},{1,9},{9,17},{17,25},{2,10},{10,18},{18,26},{... | collective-permute-start | bytes 3145736 | tf_op jit(solution)/shard_map/ppermute | solution.py:535
  17.6 4.8 %collective-permute-start.2 = (bf16[2,16,1664]{2,1,0:T(8,128)(2,1)S(1)}, bf16[2,16,1664]{2,1,0:T(8,128)(2,1)S(1)}, u32[]{:S(2)}, u32[]{:S(2)}) collective-permute-start(bf16[2,16,1664]{2,1,0:T(8,128)(2,1)S(1)} %maximum_select_fusion.6), channel_id=1, source_target_pairs={{0,2},{1,3},{2,0},{3,1},{4,6},{5,7},{6,4},{7,5},{8,10},{9,11},{10,... | collective-permute-start | bytes 319496 | tf_op jit(solution)/shard_map/ppermute | solution.py:364
  22.4 9.0 %collective-permute-start.3 = (bf16[2,2,16,1664]{3,2,0,1:T(8,128)(2,1)S(1)}, bf16[2,2,16,1664]{3,2,0,1:T(8,128)(2,1)S(1)}, u32[]{:S(2)}, u32[]{:S(2)}) collective-permute-start(bf16[2,2,16,1664]{3,2,0,1:T(8,128)(2,1)S(1)} %maximum_select_fusion.5), channel_id=1, source_target_pairs={{0,1},{1,0},{2,3},{3,2},{4,5},{5,4},{6,7},{7,6},{8,9},{9,8},{10,11... | collective-permute-start | bytes 638984 | tf_op jit(solution)/shard_map/ppermute | solution.py:364
  31.5 13.0 %collective-permute-start.4 = (bf16[2,2,2,16,1664]{4,3,0,1,2:T(8,128)(2,1)S(1)}, bf16[2,2,2,16,1664]{4,3,0,1,2:T(8,128)(2,1)S(1)}, u32[]{:S(2)}, u32[]{:S(2)}) collective-permute-start(bf16[2,2,2,16,1664]{4,3,0,1,2:T(8,128)(2,1)S(1)} %maximum_select_fusion.4), channel_id=1, source_target_pairs={{0,16},{8,24},{16,0},{24,8},{1,17},{9,25},{17,1},{25,9},{2,18},{10... | collective-permute-start | bytes 1277960 | tf_op jit(solution)/shard_map/ppermute | solution.py:364
  44.6 2.4 collective-permute-start.5
  134.6 26.5 %collective-permute-start.8 = (bf16[16,80,512]{2,1,0:T(8,128)(2,1)}, bf16[16,80,512]{2,1,0:T(8,128)(2,1)S(1)}, u32[]{:S(2)}, u32[]{:S(2)}) collective-permute-start(bf16[16,80,512]{2,1,0:T(8,128)(2,1)} %get-tuple-element.82), channel_id=1, source_target_pairs={{0,8},{8,0},{16,24},{24,16},{1,9},{9,1},{17,25},{25,17},{2,10},{10... | collective-permute-start | bytes 3932168 | tf_op jit(solution)/shard_map/ppermute | solution.py:364
  134.8 24.9 %collective-permute-start.7 = (bf16[16,64,512]{2,1,0:T(8,128)(2,1)}, bf16[16,64,512]{2,1,0:T(8,128)(2,1)}, u32[]{:S(2)}, u32[]{:S(2)}) collective-permute-start(bf16[16,64,512]{2,1,0:T(8,128)(2,1)} %get-tuple-element.81), channel_id=1, source_target_pairs={{0,8},{8,0},{16,24},{24,16},{1,9},{9,1},{17,25},{25,17},{2,10},{10... | collective-permute-start | bytes 3145736 | tf_op jit(solution)/shard_map/ppermute | solution.py:364
  135.2 5.0 %collective-permute-start.6 = (bf16[4,256,256]{2,1,0:T(8,128)(2,1)}, bf16[4,256,256]{2,1,0:T(8,128)(2,1)S(1)}, u32[]{:S(2)}, u32[]{:S(2)}) collective-permute-start(bf16[4,256,256]{2,1,0:T(8,128)(2,1)} %get-tuple-element.79), channel_id=1, source_target_pairs={{8,0},{16,8},{24,16},{9,1},{17,9},{25,17},{10,2},{18,10},{26,18},{... | collective-permute-start | bytes 1572872 | tf_op jit(solution)/shard_map/ppermute | solution.py:704
  162.5 25.6 %collective-permute-start.10 = (bf16[2,2,2,80,512]{4,3,2,1,0:T(8,128)(2,1)}, bf16[2,2,2,80,512]{4,3,2,1,0:T(8,128)(2,1)S(1)}, u32[]{:S(2)}, u32[]{:S(2)}) collective-permute-start(bf16[2,2,2,80,512]{4,3,2,1,0:T(8,128)(2,1)} %get-tuple-element.216), channel_id=1, source_target_pairs={{0,1},{1,0},{2,3},{3,2},{4,5},{5,4},{6,7},{7,6},{8,9},{9,8},{10,11... | collective-permute-start | bytes 1966088 | tf_op jit(solution)/shard_map/ppermute | solution.py:364
  164.2 24.0 %collective-permute-start.9 = (bf16[2,2,2,64,512]{4,3,1,0,2:T(8,128)(2,1)S(1)}, bf16[2,2,2,64,512]{4,3,1,0,2:T(8,128)(2,1)}, u32[]{:S(2)}, u32[]{:S(2)}) collective-permute-start(bf16[2,2,2,64,512]{4,3,1,0,2:T(8,128)(2,1)S(1)} %fusion.2), channel_id=1, source_target_pairs={{0,16},{8,24},{16,0},{24,8},{1,17},{9,25},{17,1},{25,9},{2,18},{10... | collective-permute-start | bytes 1572872 | tf_op jit(solution)/shard_map/ppermute | solution.py:364
  195.2 2.4 collective-permute-start.11
  198.6 41.3 %all-to-all-start = ((bf16[16,16,1536]{2,1,0:T(8,128)(2,1)}), bf16[16,16,1536]{2,1,0:T(8,128)(2,1)S(1)}, u32[]{:S(2)}, u32[]{:S(2)}) async-start(bf16[16,16,1536]{2,1,0:T(8,128)(2,1)} %bitcast.38), calls=%async_computation | async-start | bytes 1572864 | tf_op jit(solution)/shard_map/all_to_all | solution.py:447
  204.3 17.1 %collective-permute-start.13 = (bf16[2,2,80,512]{3,2,1,0:T(8,128)(2,1)S(1)}, bf16[2,2,80,512]{3,2,1,0:T(8,128)(2,1)S(1)}, u32[]{:S(2)}, u32[]{:S(2)}) collective-permute-start(bf16[2,2,80,512]{3,2,1,0:T(8,128)(2,1)S(1)} %get-tuple-element.220), channel_id=1, source_target_pairs={{0,16},{8,24},{16,0},{24,8},{1,17},{9,25},{17,1},{25,9},{2,18},{10... | collective-permute-start | bytes 983048 | tf_op jit(solution)/shard_map/ppermute | solution.py:364
  206.2 15.2 %collective-permute-start.12 = (bf16[2,2,64,512]{3,2,1,0:T(8,128)(2,1)S(1)}, bf16[2,2,64,512]{3,2,1,0:T(8,128)(2,1)S(1)}, u32[]{:S(2)}, u32[]{:S(2)}) collective-permute-start(bf16[2,2,64,512]{3,2,1,0:T(8,128)(2,1)S(1)} %get-tuple-element.224), channel_id=1, source_target_pairs={{0,1},{1,0},{2,3},{3,2},{4,5},{5,4},{6,7},{7,6},{8,9},{9,8},{10,11... | collective-permute-start | bytes 786440 | tf_op jit(solution)/shard_map/ppermute | solution.py:364
  221.5 25.4 %copy-start.27 = (f32[16,2]{0,1:T(2,128)S(1)}, f32[16,2]{0,1:T(2,128)}, u32[]{:S(2)}) copy-start(f32[16,2]{0,1:T(2,128)} %param.37) | copy-start | bytes 388
  221.5 25.4 %copy-start.26 = (f32[16,2]{0,1:T(2,128)S(1)}, f32[16,2]{0,1:T(2,128)}, u32[]{:S(2)}) copy-start(f32[16,2]{0,1:T(2,128)} %param.28) | copy-start | bytes 388
  221.5 26.4 %copy-start.28 = (f32[16,2]{0,1:T(2,128)S(1)}, f32[16,2]{0,1:T(2,128)}, u32[]{:S(2)}) copy-start(f32[16,2]{0,1:T(2,128)} %param.38) | copy-start | bytes 388
  221.5 37.7 %copy-start.8 = (f32[64,512]{1,0:T(8,128)S(1)}, f32[64,512]{1,0:T(8,128)}, u32[]{:S(2)}) copy-start(f32[64,512]{1,0:T(8,128)} %param.27) | copy-start | bytes 393220
  221.6 37.7 %copy-start.19 = (f32[64,512]{1,0:T(8,128)S(1)}, f32[64,512]{1,0:T(8,128)}, u32[]{:S(2)}) copy-start(f32[64,512]{1,0:T(8,128)} %param.36) | copy-start | bytes 393220
  221.6 37.7 %copy-start.20 = (f32[64,512]{1,0:T(8,128)S(1)}, f32[64,512]{1,0:T(8,128)}, u32[]{:S(2)}) copy-start(f32[64,512]{1,0:T(8,128)} %param.35) | copy-start | bytes 393220
  221.8 8.8 %collective-permute-start.14 = (bf16[2,144,512]{2,1,0:T(8,128)(2,1)S(1)}, bf16[2,144,512]{2,1,0:T(8,128)(2,1)S(1)}, u32[]{:S(2)}, u32[]{:S(2)}) collective-permute-start(bf16[2,144,512]{2,1,0:T(8,128)(2,1)S(1)} %get-tuple-element.222), channel_id=1, source_target_pairs={{0,2},{1,3},{2,0},{3,1},{4,6},{5,7},{6,4},{7,5},{8,10},{9,11},{10,... | collective-permute-start | bytes 884744 | tf_op jit(solution)/shard_map/ppermute | solution.py:364
  231.3 30.0 %copy-start.18 = (f32[16,512]{1,0:T(8,128)S(1)}, f32[16,512]{1,0:T(8,128)}, u32[]{:S(2)}) copy-start(f32[16,512]{1,0:T(8,128)} %param.25) | copy-start | bytes 98308
  231.3 30.0 %copy-start.24 = (f32[16,512]{1,0:T(8,128)S(1)}, f32[16,512]{1,0:T(8,128)}, u32[]{:S(2)}) copy-start(f32[16,512]{1,0:T(8,128)} %param.32) | copy-start | bytes 98308
  231.3 30.1 %copy-start.25 = (f32[16,512]{1,0:T(8,128)S(1)}, f32[16,512]{1,0:T(8,128)}, u32[]{:S(2)}) copy-start(f32[16,512]{1,0:T(8,128)} %param.31) | copy-start | bytes 98308
  231.3 8.6 %collective-permute-start.15 = (bf16[144,512]{1,0:T(8,128)(2,1)S(1)}, bf16[144,512]{1,0:T(8,128)(2,1)S(1)}, u32[]{:S(2)}, u32[]{:S(2)}) collective-permute-start(bf16[144,512]{1,0:T(8,128)(2,1)S(1)} %get-tuple-element.229), channel_id=1, source_target_pairs={{0,4},{1,5},{2,6},{3,7},{4,0},{5,1},{6,2},{7,3},{8,12},{9,13},{10,... | collective-permute-start | bytes 442376 | tf_op jit(solution)/shard_map/ppermute | solution.py:364
  240.9 21.9 %copy-start.15 = (f32[16,2048]{1,0:T(8,128)S(1)}, f32[16,2048]{1,0:T(8,128)}, u32[]{:S(2)}) copy-start(f32[16,2048]{1,0:T(8,128)} %param.34) | copy-start | bytes 393220
  240.9 21.9 %copy-start.16 = (f32[16,2048]{1,0:T(8,128)S(1)}, f32[16,2048]{1,0:T(8,128)}, u32[]{:S(2)}) copy-start(f32[16,2048]{1,0:T(8,128)} %param.33) | copy-start | bytes 393220
  243.2 20.4 %copy-start.10 = (f32[16,3,512]{2,0,1:T(8,128)S(1)}, f32[16,3,512]{2,0,1:T(8,128)}, u32[]{:S(2)}) copy-start(f32[16,3,512]{2,0,1:T(8,128)} %param.24) | copy-start | bytes 294916
  243.2 20.4 %copy-start.22 = (f32[16,3,512]{2,0,1:T(8,128)S(1)}, f32[16,3,512]{2,0,1:T(8,128)}, u32[]{:S(2)}) copy-start(f32[16,3,512]{2,0,1:T(8,128)} %param.30) | copy-start | bytes 294916
  243.3 11.4 %all-to-all-start.1 = ((f32[32,8,128]{2,1,0:T(8,128)}), f32[32,8,128]{2,1,0:T(8,128)S(1)}, u32[]{:S(2)}, u32[]{:S(2)}) async-start(f32[32,8,128]{2,1,0:T(8,128)} %get-tuple-element.99), calls=%async_computation.1 | async-start | bytes 262144 | tf_op jit(solution)/shard_map/all_to_all | solution.py:453
  (17 other events, 138.7 us)
Sparse Core Ops, SparseCore 0:
  16.2 65.3 all-gather.2

commit v3 on v2

--- a/solution.py
+++ b/solution.py
@@ -86,14 +86,20 @@
     return seg_col, flag((rows >= cols) & (seg_col == seg_row))
 
 
+def compacted(first, second):
+    ma, mb = half_masks(256)
+    return first * ma + second * mb
+
+
 def forward_kernel(
     ends_ref, xh_ref, xo_ref, seg_ref, wq_ref, spread_ref,
-    h1_ref, qkv_ref, pq_ref, pk_ref, p_ref, t_ref, o_ref, of_ref, rden_ref, gains_ref,
+    h1_ref, qkv_ref, pq_ref, pk_ref, p_ref, t_ref, o_ref, rden_ref, gains_ref,
     state_ref,
 ):
     step = pl.program_id(0)
-    halo = SPAN // CHUNK
-    ones = jnp.ones((CHUNK, 2 * HD), bf16)
+    halo = SPAN // ROWS
+    subs = ROWS // CHUNK
+    ones = jnp.ones((ROWS, 2 * HD), bf16)
 
     @pl.when(step == 0)
     def _():
@@ -106,61 +112,62 @@
     def _():
         x = xh_ref[...].astype(f32)
         h1 = (x * rms_scale(x) * gain).astype(bf16)
-        chosen = flag(as_column(seg_ref[0]) == ends_ref[halo - 1])
+        chosen = flag(as_column(seg_ref[0]) == ends_ref[halo * subs - 1])
+        kvs = [dot(h1, wq_ref[:, 384 * p + 128 : 384 * (p + 1)]).astype(bf16) for p in range(PAIRS)]
         for p in range(PAIRS):
-            kv = dot(h1, wq_ref[:, 384 * p + 128 : 384 * (p + 1)]).astype(bf16)
-            pk = features(kv[:, :128], spread_ref[...])
-            vw = jnp.concatenate([kv[:, 128:], ones], axis=1) * chosen
-            state_ref[p] = state_ref[p] + dot(pk, vw, 0, 0)
+            pk_ref[:, 512 * p : 512 * (p + 1)] = features(kvs[p][:, :128], spread_ref[...])
+        for p in range(PAIRS):
+            vw = jnp.concatenate([kvs[p][:, 128:], ones], axis=1) * chosen
+            state_ref[p] = state_ref[p] + dot(pk_ref[:, 512 * p : 512 * (p + 1)], vw, 0, 0)
 
     @pl.when(step >= halo)
     def _():
-        before = ends_ref[step - 1]
-        last = ends_ref[step]
         x = xo_ref[...].astype(f32)
         h1 = (x * rms_scale(x) * gain).astype(bf16)
         h1_ref[...] = h1
-        qkv = dot(h1, wq_ref[:, : 3 * D]).astype(bf16)
-        qkv_ref[...] = qkv
-        seg_col, allowed = chunk_mask(seg_ref[0])
-        chosen = flag(seg_col == last)
-        follows = flag(seg_col == before)
-        keep = (last == before).astype(f32)
+        qkv_ref[...] = dot(h1, wq_ref[:, : 3 * D]).astype(bf16)
         for p in range(PAIRS):
-            cut = slice(128 * p, 128 * (p + 1))
             wide = slice(512 * p, 512 * (p + 1))
-            q2 = qkv[:, 384 * p : 384 * p + 128]
-            k2 = qkv[:, 384 * p + 128 : 384 * p + 256]
-            v2 = qkv[:, 384 * p + 256 : 384 * p + 384]
-            pq = features(q2, spread_ref[...])
-            pk = features(k2, spread_ref[...])
-            pq_ref[:, wide] = pq
-            pk_ref[:, wide] = pk
-            scores = jnp.concatenate(
-                [
-                    dot(pq[:, :FEATS], pk[:, :FEATS], 1, 1).astype(bf16) * allowed,
-                    dot(pq[:, FEATS:], pk[:, FEATS:], 1, 1).astype(bf16) * allowed,
-                ],
-                axis=1,
-            )
-            p_ref[:, wide] = scores
-            v1 = jnp.concatenate([v2, ones], axis=1)
-            state = state_ref[p]
-            narrow = state.astype(bf16)
-            narrow = masked_pair(narrow[:FEATS], narrow[FEATS:], 256)
-            t_ref[0, p] = narrow
-            both = dot(scores, masked_pair(v1, v1, 256)) + dot(pq * follows, narrow)
-            rden = 1.0 / both[:, 128:]
-            of = both[:, :128] * rden
-            rden_ref[:, cut] = rden
-            of_ref[:, cut] = of
-            o_ref[:, cut] = of.astype(bf16)
-            state_ref[p] = keep * state + dot(pk, v1 * chosen, 0, 0)
+            pq_ref[:, wide] = features(qkv_ref[:, 384 * p : 384 * p + 128], spread_ref[...])
+            pk_ref[:, wide] = features(qkv_ref[:, 384 * p + 128 : 384 * p + 256], spread_ref[...])
+        seg = seg_ref[0]
+        for j in range(subs):
+            rows = slice(CHUNK * j, CHUNK * (j + 1))
+            _, allowed = chunk_mask(seg[:, rows])
+            for h in range(2 * PAIRS):
+                cut = slice(FEATS * h, FEATS * (h + 1))
+                p_ref[rows, CHUNK * h : CHUNK * (h + 1)] = (
+                    dot(pq_ref[rows, cut], pk_ref[rows, cut], 1, 1).astype(bf16) * allowed
+                )
+        seg_col = as_column(seg)
+        for j in range(subs):
+            rows = slice(CHUNK * j, CHUNK * (j + 1))
+            before = ends_ref[step * subs + j - 1]
+            last = ends_ref[step * subs + j]
+            chosen = flag(seg_col[rows] == last)
+            follows = flag(seg_col[rows] == before)
+            keep = (last == before).astype(f32)
+            for p in range(PAIRS):
+                cut = slice(128 * p, 128 * (p + 1))
+                wide = slice(512 * p, 512 * (p + 1))
+                v2 = qkv_ref[rows, 384 * p + 256 : 384 * p + 384]
+                v1 = jnp.concatenate([v2, ones[:CHUNK]], axis=1)
+                state = state_ref[p]
+                narrow = state.astype(bf16)
+                narrow = masked_pair(narrow[:FEATS], narrow[FEATS:], 256)
+                t_ref[j, p] = narrow[:FEATS] + narrow[FEATS:]
+                both = dot(p_ref[rows, wide], masked_pair(v1, v1, 256)) + dot(
+                    pq_ref[rows, wide] * follows, narrow
+                )
+                state_ref[p] = keep * state + dot(pk_ref[rows, wide], v1 * chosen, 0, 0)
+                rden = 1.0 / both[:, 128:]
+                rden_ref[rows, cut] = rden
+                o_ref[rows, cut] = (both[:, :128] * rden).astype(bf16)
 
 
 def middle_kernel(
     group,
-    ends_ref, core_ref, x_ref, g_ref, o_ref, of_ref, rden_ref, pq_ref, seg_ref, gains_ref,
+    ends_ref, core_ref, x_ref, g_ref, o_ref, rden_ref, pq_ref, seg_ref, gains_ref,
     wu0_ref, wu1_ref, wu2_ref, wu3_ref, wd_ref, wo_ref,
     out_ref, dy1_ref, dn_ref, sent_up_ref, sent_rest_ref, kept_up_ref, kept_rest_ref, back_ref,
     up_acc, down_acc, out_acc, back_acc, act_ref, dup_ref,
@@ -211,7 +218,7 @@
     da = dy1.astype(bf16)
     out_acc[...] += dot(da, o, 0, 0)
     d_o = dot(da, wo)
-    product = d_o * of_ref[...]
+    product = d_o * o.astype(f32)
     high = product.astype(bf16)
     low = (product - high.astype(f32)).astype(bf16)
     rden = rden_ref[...]
@@ -260,20 +267,20 @@
                 others[here, 64:] = out_acc[thin].astype(bf16).reshape(group, 16, D)
         for p in range(PAIRS):
             back = back_acc[p].astype(bf16)
-            ma2, mb2 = half_masks(256)
-            back_ref[p] = back[:FEATS] * ma2 + back[FEATS:] * mb2
+            back_ref[p] = compacted(back[:FEATS], back[FEATS:])
 
 
 def backward_kernel(pairs, ends_ref, seg_ref, gather_ref, *refs):
-    refs = refs[: 7 * pairs] + refs[-2:]
-    halo = SPAN // CHUNK
+    refs = refs[: 7 * pairs] + refs[-4:]
+    subs = ROWS // CHUNK
     step = pl.program_id(0)
-    chunk = pl.num_programs(0) - 1 - step
-    before = ends_ref[chunk + halo - 1]
-    last = ends_ref[chunk + halo]
+    steps = pl.num_programs(0)
+    at = (SPAN // ROWS + steps - 1 - step) * subs
+    dqkv_ref, state_ref, grad_ref, logit_ref = refs[7 * pairs :]
+    p_refs, pq_refs, pk_refs, qkv_refs, dn_refs, t_refs, back_refs = [
+        refs[i * pairs : (i + 1) * pairs] for i in range(7)
+    ]
     ma2, mb2 = half_masks(256)
-    dqkv_ref, state_ref = refs[7 * pairs :]
-    back_refs = refs[6 * pairs : 7 * pairs]
 
     @pl.when(step == 0)
     def _():
@@ -281,47 +288,60 @@
             state_ref[p, :FEATS] = (back_refs[p][0] * ma2).astype(f32)
             state_ref[p, FEATS:] = (back_refs[p][0] * mb2).astype(f32)
 
-    seg_col, allowed = chunk_mask(seg_ref[0])
-    chosen = flag(seg_col == last)
-    follows = flag(seg_col == before)
-    keep = (last == before).astype(f32)
+    seg = seg_ref[0]
+    seg_col = as_column(seg)
     two = jnp.broadcast_to(flag(lanes(128) % HD < 2), (CHUNK, 128))
     ones = jnp.ones((CHUNK, 128), bf16)
     ma, mb = half_masks(128)
+    for j in reversed(range(subs)):
+        rows = slice(CHUNK * j, CHUNK * (j + 1))
+        _, allowed = chunk_mask(seg[:, rows])
+        before = ends_ref[at + j - 1]
+        last = ends_ref[at + j]
+        chosen = flag(seg_col[rows] == last)
+        follows = flag(seg_col[rows] == before)
+        keep = (last == before).astype(f32)
+        for p in range(pairs):
+            v1 = jnp.concatenate([qkv_refs[p][rows, 256:], two], axis=1)
+            d_p = dot(dn_refs[p][rows], masked_pair(v1, v1, 256), 1, 1).astype(bf16)
+            grad_ref[p, :, :CHUNK] = d_p[:, :CHUNK] * allowed
+            grad_ref[p, :, CHUNK:] = d_p[:, CHUNK:] * allowed
+        for p in range(pairs):
+            pq, pk, dn = pq_refs[p][rows], pk_refs[p][rows], dn_refs[p][rows]
+            scores = p_refs[p][rows]
+            v2 = qkv_refs[p][rows, 256:]
+            compact = t_refs[p][j, 0]
+            narrow = masked_pair(compact, compact, 256)
+            state = state_ref[p]
+            back = state.astype(bf16)
+            back = masked_pair(back[:FEATS], back[FEATS:], 256)
+            d_pa = grad_ref[p, :, :CHUNK]
+            d_pb = grad_ref[p, :, CHUNK:]
+            dn_f = dn * follows
+            d_pq = dot(dn_f, narrow, 1, 1) + jnp.concatenate(
+                [dot(d_pa, pk[:, :FEATS]), dot(d_pb, pk[:, FEATS:])], axis=1
+            )
+            logit_ref[0, p, rows] = d_pq.astype(bf16) * pq
+            vw = jnp.concatenate([v2, ones], axis=1) * chosen
+            d_pk = dot(vw, back, 1, 1) + jnp.concatenate(
+                [dot(d_pa, pq[:, :FEATS], 0, 0), dot(d_pb, pq[:, FEATS:], 0, 0)], axis=1
+            )
+            logit_ref[1, p, rows] = d_pk.astype(bf16) * pk
+            d_num = dn[:, :128]
+            d_v = (
+                dot(pk * chosen, back[:, :128])
+                + dot(scores[:, :CHUNK], d_num * ma, 0, 0)
+                + dot(scores[:, CHUNK:], d_num * mb, 0, 0)
+            )
+            dqkv_ref[rows, 384 * p + 256 : 384 * p + 384] = d_v.astype(bf16)
+            state_ref[p] = keep * state + dot(pq, dn_f, 0, 0)
+    scale2 = feature_scale * feature_scale
     for p in range(pairs):
-        scores, pq, pk, qkv, dn = [refs[i * pairs + p][...] for i in range(5)]
-        narrow = refs[5 * pairs + p][0, 0]
-        q2, k2, v2 = qkv[:, :128], qkv[:, 128:256], qkv[:, 256:]
-        state = state_ref[p]
-        back = state.astype(bf16)
-        back = masked_pair(back[:FEATS], back[FEATS:], 256)
-        v1 = jnp.concatenate([v2, two], axis=1)
-        d_p = dot(dn, masked_pair(v1, v1, 256), 1, 1).astype(bf16)
-        d_pa = d_p[:, :CHUNK] * allowed
-        d_pb = d_p[:, CHUNK:] * allowed
-        dn_f = dn * follows
-        d_pq = dot(dn_f, narrow, 1, 1) + jnp.concatenate(
-            [dot(d_pa, pk[:, :FEATS]), dot(d_pb, pk[:, FEATS:])], axis=1
-        )
-        vw = jnp.concatenate([v2, ones], axis=1) * chosen
-        d_pk = dot(vw, back, 1, 1) + jnp.concatenate(
-            [dot(d_pa, pq[:, :FEATS], 0, 0), dot(d_pb, pq[:, FEATS:], 0, 0)], axis=1
-        )
-        d_num = dn[:, :128]
-        d_v = (
-            dot(pk * chosen, back[:, :128])
-            + dot(scores[:, :CHUNK], d_num * ma, 0, 0)
-            + dot(scores[:, CHUNK:], d_num * mb, 0, 0)
-        )
-        through_q = dot(d_pq.astype(bf16) * pq, gather_ref[...])
-        through_k = dot(d_pk.astype(bf16) * pk, gather_ref[...])
-        scale2 = feature_scale * feature_scale
-        d_q = through_q[:, :128] * feature_scale - q2.astype(f32) * through_q[:, 128:] * scale2
-        d_k = through_k[:, :128] * feature_scale - k2.astype(f32) * through_k[:, 128:] * scale2
-        dqkv_ref[:, 384 * p : 384 * p + 128] = d_q.astype(bf16)
-        dqkv_ref[:, 384 * p + 128 : 384 * p + 256] = d_k.astype(bf16)
-        dqkv_ref[:, 384 * p + 256 : 384 * p + 384] = d_v.astype(bf16)
-        state_ref[p] = keep * state + dot(pq, dn_f, 0, 0)
+        for i in range(2):
+            u = qkv_refs[p][:, 128 * i : 128 * (i + 1)].astype(f32)
+            through = dot(logit_ref[i, p], gather_ref[...])
+            d_u = through[:, :128] * feature_scale - u * through[:, 128:] * scale2
+            dqkv_ref[:, 384 * p + 128 * i : 384 * p + 128 * (i + 1)] = d_u.astype(bf16)
 
 
 def input_kernel(dqkv_ref, wq_ref, x_ref, dy1_ref, gains_ref, dx_ref):
@@ -346,7 +366,7 @@
     for f in range(1, 4):
         lows = lows + rows[share * f : share * (f + 1)]
     gg = jnp.concatenate([tops, lows], axis=1) / packed[:, 3 * D : 3 * D + 2]
-    gg_ref[...] = gg
+    gg_ref[...] = jnp.concatenate([gg, jnp.zeros((share, 126), f32)], axis=1).T[:2]
     total = jnp.sum(sum_q * sum_q) + jnp.sum(sum_r * sum_r) + jnp.sum(gg * gg)
     spread_ref[...] = jnp.full(spread_ref.shape, total, f32)
 
@@ -481,6 +501,159 @@
 def fixed(shape):
     zeros = (0,) * len(shape)
     return pl.BlockSpec(shape, lambda *_: zeros, pipeline_mode=pl.Buffered(1))
+
+
+def first_at(shape, offset):
+    rest = (0,) * (len(shape) - 1)
+    return pl.BlockSpec(shape, lambda c, *_: (jnp.maximum(c - offset, 0),) + rest)
+
+
+def by_step(shape):
+    return first_at(shape, 0)
+
+
+def forward_call(ends, x_ahead, x, seg_rows, wq, spread):
+    length = x.shape[0]
+    chunks, halo, wide = length // CHUNK, SPAN // ROWS, PAIRS * 2 * FEATS
+    own = partial(first_at, offset=halo)
+    outs = [
+        ((ROWS, D), (length, D), bf16),
+        ((ROWS, 3 * D), (length, 3 * D), bf16),
+        ((ROWS, wide), (length, wide), bf16),
+        ((ROWS, wide), (length, wide), bf16),
+        ((ROWS, wide), (length, wide), bf16),
+        ((ROWS // CHUNK, PAIRS, FEATS, 256), (chunks, PAIRS, FEATS, 256), bf16),
+        ((ROWS, D), (length, D), bf16),
+        ((ROWS, D), (length, D), f32),
+    ]
+    return pl.pallas_call(
+        forward_kernel,
+        grid_spec=pltpu.PrefetchScalarGridSpec(
+            num_scalar_prefetch=1,
+            grid=(halo + length // ROWS,),
+            in_specs=[
+                pl.BlockSpec((ROWS, D), lambda c, *_: (jnp.minimum(c, halo - 1), 0)),
+                own((ROWS, D)),
+                by_step((1, 1, ROWS)),
+                fixed(wq.shape),
+                fixed(spread.shape),
+            ],
+            out_specs=[own(block) for block, _, _ in outs] + [fixed((8, D))],
+            scratch_shapes=[pltpu.VMEM((PAIRS, 2 * FEATS, 256), f32)],
+        ),
+        out_shape=[jax.ShapeDtypeStruct(shape, kind) for _, shape, kind in outs]
+        + [jax.ShapeDtypeStruct((8, D), f32)],
+        compiler_params=params(),
+        cost_estimate=cost(35),
+        name="forward",
+    )(ends, x_ahead, x, seg_rows, wq, spread)
+
+
+def middle_call(group, ends, core, x, g, o, rden, pq, seg_rows, gain_rows, later):
+    length, wide = x.shape[0], pq.shape[1]
+    near_steps = SPAN // ROWS
+    by_step_ahead = pl.BlockSpec((1, 1, ROWS), lambda c, *_: (c + near_steps, 0, 0))
+
+    def columns(block, height=16):
+        return pl.BlockSpec(
+            (D // 16, height, 512), lambda *_: (0, block, 0), pipeline_mode=pl.Buffered(1)
+        )
+
+    outs = [
+        ((ROWS, D), (length, D), bf16),
+        ((ROWS, D), (length, D), f32),
+        ((ROWS, PAIRS * 256), (length, PAIRS * 256), bf16),
+    ]
+    sums = [(D // 32, 64, 512), (D // 32, 80, 512)] * 2 + [(PAIRS, FEATS, 256)]
+    return pl.pallas_call(
+        partial(middle_kernel, group),
+        grid_spec=pltpu.PrefetchScalarGridSpec(
+            num_scalar_prefetch=2,
+            grid=(length // ROWS,),
+            in_specs=[by_step((ROWS, D))] * 4
+            + [
+                pl.BlockSpec((ROWS, wide), lambda c, *_: (jnp.minimum(c, near_steps - 1), 0)),
+                by_step_ahead,
+                fixed((8, D)),
+            ]
+            + [columns(f) for f in range(4)]
+            + [columns(1, 64), columns(8)],
+            out_specs=[by_step(block) for block, _, _ in outs] + [fixed(shape) for shape in sums],
+            scratch_shapes=[
+                pltpu.VMEM((D, FF), f32),
+                pltpu.VMEM((FF, D), f32),
+                pltpu.VMEM((D, D), f32),
+                pltpu.VMEM((PAIRS, 2 * FEATS, 256), f32),
+                pltpu.VMEM((ROWS, FF), bf16),
+                pltpu.VMEM((ROWS, FF), bf16),
+            ],
+        ),
+        out_shape=[jax.ShapeDtypeStruct(shape, kind) for _, shape, kind in outs]
+        + [jax.ShapeDtypeStruct(shape, bf16) for shape in sums],
+        compiler_params=params(),
+        cost_estimate=cost(48),
+        name="middle",
+    )(ends, core, x, g, o, rden, pq, seg_rows, gain_rows, *[later] * 6)
+
+
+def backward_call(at, parts, ends, seg_rows, gather, arrays, *written):
+    length = arrays[0].shape[0]
+    steps, halo = length // ROWS, SPAN // ROWS
+    count = PAIRS // parts
+    chosen = range(at * count, (at + 1) * count)
+
+    def falling(shape, at=0):
+        rest = (0,) * (len(shape) - 2)
+        return pl.BlockSpec(shape, lambda c, *_: (steps - 1 - c, at) + rest)
+
+    def state(at):
+        return pl.BlockSpec((1, FEATS, 256), lambda *_: (at, 0, 0), pipeline_mode=pl.Buffered(1))
+
+    specs = [pl.BlockSpec((1, 1, ROWS), lambda c, *_: (steps + halo - 1 - c, 0, 0))]
+    specs += [fixed(gather.shape)]
+    for shape in ((ROWS, 512),) * 3 + ((ROWS, 384), (ROWS, 256), (ROWS // CHUNK, 1, 256, 256)):
+        specs += [falling(shape, p) for p in chosen]
+    specs += [state(p) for p in chosen]
+    operands = [array for array in arrays for _ in chosen]
+    return pl.pallas_call(
+        partial(backward_kernel, count),
+        grid_spec=pltpu.PrefetchScalarGridSpec(
+            num_scalar_prefetch=1,
+            grid=(steps,),
+            in_specs=specs + [pl.BlockSpec(memory_space=pl.ANY)] * len(written),
+            out_specs=falling((ROWS, 384 * count), at),
+            scratch_shapes=[
+                pltpu.VMEM((count, 2 * FEATS, 256), f32),
+                pltpu.VMEM((count, CHUNK, 2 * CHUNK), bf16),
+                pltpu.VMEM((2, count, ROWS, 2 * FEATS), bf16),
+            ],
+        ),
+        out_shape=jax.ShapeDtypeStruct((length, 3 * D), bf16),
+        input_output_aliases={3 + len(operands): 0} if written else {},
+        compiler_params=params(),
+        cost_estimate=cost(8 * count),
+        name="backward",
+    )(ends, seg_rows, gather, *operands, *written)
+
+
+def input_call(dqkv, wq, x, dy1, gain_rows):
+    length = x.shape[0]
+    return pl.pallas_call(
+        input_kernel,
+        grid=(length // ROWS,),
+        in_specs=[
+            by_step((ROWS, 3 * D)),
+            fixed(wq.shape),
+            by_step((ROWS, D)),
+            by_step((ROWS, D)),
+            fixed((8, D)),
+        ],
+        out_specs=by_step((ROWS, D)),
+        out_shape=jax.ShapeDtypeStruct((length, D), f32),
+        compiler_params=params(),
+        cost_estimate=cost(10),
+        name="input_grad",
+    )(dqkv, wq, x, dy1, gain_rows)
 
 
 def per_device(
@@ -510,8 +683,6 @@
     x = inputs[0]
     g = cotangent[0]
     length = x.shape[0]
-    chunks = length // CHUNK
-    halo = SPAN // CHUNK
     share = w_qkv.shape[0]
     group = lax.axis_size("row") * share // 16
 
@@ -526,14 +697,16 @@
     forward_pairs = [(i, i + 1) for i in range(heads - 1)]
     backward_pairs = [(i + 1, i) for i in range(heads - 1)]
     weights = Gather(packed)
-    order = row_bits[::-1] + head_bits[::-1]
-    weights.start(*order[0])
+    core_bit, *far_bits = head_bits
+    order = row_bits[::-1] + far_bits + [core_bit]
     later = jnp.concatenate(
         [w_up[:, 512 * j : 512 * (j + 1)] for j in range(FF // 512)] + [w_down, w_out], axis=0
     ).astype(bf16)
     tail = x[length - SPAN :]
+    weights.buf = tied(packed, tail)
     x_ahead = lax.ppermute(tail, "head", forward_pairs)
-    weights.finish(tail)
+    weights.start(*order[0])
+    weights.finish(later)
     later_own = tied(later, weights.buf)
     later = lax.all_gather(later_own, AXES, axis=0)
     if share != 16:
@@ -550,8 +723,7 @@
     padded = jnp.concatenate([jnp.full((SPAN,), -1, jnp.int32), row_segments])
     near = lax.dynamic_slice_in_dim(padded, lax.axis_index("head") * length, length + SPAN)
     ends = near[CHUNK - 1 :: CHUNK]
-    seg_rows = near.astype(f32).reshape(-1, 1, CHUNK)
-    near_rows = near[SPAN : 2 * SPAN].astype(f32).reshape(-1, 1, ROWS)
+    seg_rows = near.astype(f32).reshape(-1, 1, ROWS)
     fm = feature_matrix
     nothing = jnp.zeros_like(fm.T)
     spread = jnp.concatenate(
@@ -570,7 +742,7 @@
         ],
         axis=0,
     )
-    weights.finish(ends, seg_rows, near_rows)
+    weights.finish(ends, seg_rows)
     weights.start(*order[2])
     weights.finish(spread, gather, x_ahead)
     for stage in order[3:]:
@@ -579,125 +751,12 @@
     wq = weights.whole()
     core = (lax.axis_index("head") & 1).reshape(1)
 
-    def own(shape):
-        rest = (0,) * (len(shape) - 1)
-        return pl.BlockSpec(shape, lambda c, *_: (jnp.maximum(c - halo, 0),) + rest)
-
-    wide = PAIRS * 2 * FEATS
-    h1, qkv, pq, pk, scores, states, o, of, rden, gain_rows = pl.pallas_call(
-        forward_kernel,
-        grid_spec=pltpu.PrefetchScalarGridSpec(
-            num_scalar_prefetch=1,
-            grid=(halo + chunks,),
-            in_specs=[
-                pl.BlockSpec((CHUNK, D), lambda c, *_: (jnp.minimum(c, halo - 1), 0)),
-                own((CHUNK, D)),
-                pl.BlockSpec((1, 1, CHUNK), lambda c, *_: (c, 0, 0)),
-                fixed((D, 3 * D + 128)),
-                fixed((2 * HD, 2 * FEATS)),
-            ],
-            out_specs=[
-                own((CHUNK, D)),
-                own((CHUNK, 3 * D)),
-                own((CHUNK, wide)),
-                own((CHUNK, wide)),
-                own((CHUNK, wide)),
-                own((1, PAIRS, 2 * FEATS, 256)),
-                own((CHUNK, D)),
-                own((CHUNK, D)),
-                own((CHUNK, D)),
-                fixed((8, D)),
-            ],
-            scratch_shapes=[pltpu.VMEM((PAIRS, 2 * FEATS, 256), f32)],
-        ),
-        out_shape=[
-            jax.ShapeDtypeStruct((length, D), bf16),
-            jax.ShapeDtypeStruct((length, 3 * D), bf16),
-            jax.ShapeDtypeStruct((length, wide), bf16),
-            jax.ShapeDtypeStruct((length, wide), bf16),
-            jax.ShapeDtypeStruct((length, wide), bf16),
-            jax.ShapeDtypeStruct((chunks, PAIRS, 2 * FEATS, 256), bf16),
-            jax.ShapeDtypeStruct((length, D), bf16),
-            jax.ShapeDtypeStruct((length, D), f32),
-            jax.ShapeDtypeStruct((length, D), f32),
-            jax.ShapeDtypeStruct((8, D), f32),
-        ],
-        compiler_params=params(),
-        cost_estimate=cost(35),
-        name="forward",
-    )(ends, x_ahead, x, seg_rows, wq, spread)
-
-    def by_step(shape):
-        rest = (0,) * (len(shape) - 1)
-        return pl.BlockSpec(shape, lambda c, *_: (c,) + rest)
-
-    near_steps = SPAN // ROWS
-
-    def columns(block):
-        return pl.BlockSpec(
-            (D // 16, 16, 512), lambda *_: (0, block, 0), pipeline_mode=pl.Buffered(1)
-        )
-
-    out_act, dy1, dn, sent_up, sent_rest, kept_up, kept_rest, back = pl.pallas_call(
-        partial(middle_kernel, group),
-        grid_spec=pltpu.PrefetchScalarGridSpec(
-            num_scalar_prefetch=2,
-            grid=(length // ROWS,),
-            in_specs=[
-                by_step((ROWS, D)),
-                by_step((ROWS, D)),
-                by_step((ROWS, D)),
-                by_step((ROWS, D)),
-                by_step((ROWS, D)),
-                pl.BlockSpec((ROWS, wide), lambda c, *_: (jnp.minimum(c, near_steps - 1), 0)),
-                pl.BlockSpec((1, 1, ROWS), lambda c, *_: (jnp.minimum(c, near_steps - 1), 0, 0)),
-                fixed((8, D)),
-                columns(0),
-                columns(1),
-                columns(2),
-                columns(3),
-                pl.BlockSpec(
-                    (D // 16, 64, 512), lambda *_: (0, 1, 0), pipeline_mode=pl.Buffered(1)
-                ),
-                columns(8),
-            ],
-            out_specs=[
-                by_step((ROWS, D)),
-                by_step((ROWS, D)),
-                by_step((ROWS, PAIRS * 256)),
-                fixed((D // 32, 64, 512)),
-                fixed((D // 32, 80, 512)),
-                fixed((D // 32, 64, 512)),
-                fixed((D // 32, 80, 512)),
-                fixed((PAIRS, FEATS, 256)),
-            ],
-            scratch_shapes=[
-                pltpu.VMEM((D, FF), f32),
-                pltpu.VMEM((FF, D), f32),
-                pltpu.VMEM((D, D), f32),
-                pltpu.VMEM((PAIRS, 2 * FEATS, 256), f32),
-                pltpu.VMEM((ROWS, FF), bf16),
-                pltpu.VMEM((ROWS, FF), bf16),
-            ],
-        ),
-        out_shape=[
-            jax.ShapeDtypeStruct((length, D), bf16),
-            jax.ShapeDtypeStruct((length, D), f32),
-            jax.ShapeDtypeStruct((length, PAIRS * 256), bf16),
-            jax.ShapeDtypeStruct((D // 32, 64, 512), bf16),
-            jax.ShapeDtypeStruct((D // 32, 80, 512), bf16),
-            jax.ShapeDtypeStruct((D // 32, 64, 512), bf16),
-            jax.ShapeDtypeStruct((D // 32, 80, 512), bf16),
-            jax.ShapeDtypeStruct((PAIRS, FEATS, 256), bf16),
-        ],
-        compiler_params=params(),
-        cost_estimate=cost(48),
-        name="middle",
-    )(
-        ends, core, x, g, o, of, rden, pq, near_rows, gain_rows,
-        later, later, later, later, later, later,
-    )
-
+    h1, qkv, pq, pk, scores, states, o, rden, gain_rows = forward_call(
+        ends, x_ahead, x, seg_rows, wq, spread
+    )
+    out_act, dy1, dn, sent_up, sent_rest, kept_up, kept_rest, back = middle_call(
+        group, ends, core, x, g, o, rden, pq, seg_rows, gain_rows, later
+    )
     if share != 16:
         sent_up, kept_up = ups_by_device(sent_up, share), ups_by_device(kept_up, share)
         sent_rest, kept_rest = rest_by_device(sent_rest, share), rest_by_device(kept_rest, share)
@@ -706,44 +765,9 @@
     came_rest = swap(sent_rest, "head", 0)
 
     def attention_back(at, back_in, *written):
-        chosen = range(at * PAIRS // 2, (at + 1) * PAIRS // 2)
-        count = len(chosen)
-
-        def falling(shape, at=0):
-            rest = (0,) * (len(shape) - 2)
-            return pl.BlockSpec(shape, lambda c, *_: (chunks - 1 - c, at) + rest)
-
-        def state(at):
-            return pl.BlockSpec(
-                (1, FEATS, 256), lambda *_: (at, 0, 0), pipeline_mode=pl.Buffered(1)
-            )
-
-        specs = [pl.BlockSpec((1, 1, CHUNK), lambda c, *_: (chunks + halo - 1 - c, 0, 0))]
-        specs += [fixed((2 * FEATS, 256))]
-        for shape in ((CHUNK, 512),) * 3 + ((CHUNK, 384), (CHUNK, 256), (1, 1, 512, 256)):
-            specs += [falling(shape, p) for p in chosen]
-        specs += [state(p) for p in chosen]
-        operands = []
-        for array in (scores, pq, pk, qkv, dn, states, back_in):
-            operands += [array] * count
-        return pl.pallas_call(
-            partial(backward_kernel, count),
-            grid_spec=pltpu.PrefetchScalarGridSpec(
-                num_scalar_prefetch=1,
-                grid=(chunks,),
-                in_specs=specs + [pl.BlockSpec(memory_space=pl.ANY)] * len(written),
-                out_specs=falling((CHUNK, 384 * count), at),
-                scratch_shapes=[pltpu.VMEM((count, 2 * FEATS, 256), f32)],
-            ),
-            out_shape=jax.ShapeDtypeStruct((length, 3 * D), bf16),
-            input_output_aliases={3 + len(operands): 0} if written else {},
-            compiler_params=params(),
-            cost_estimate=cost(8 * count),
-            name="backward",
-        )(ends, seg_rows, gather, *operands, *written)
-
-    core_bit, *far_bits = head_bits
-    places = [place for _, _, place in far_bits + row_bits]
+        arrays = (scores, pq, pk, qkv, dn, states, back_in)
+        return backward_call(at, 2, ends, seg_rows, gather, arrays, *written)
+
     lower = [(axis, bit, place - (place > core_bit[2])) for axis, bit, place in far_bits]
     first_order = lower + row_bits[:1]
     second_order = row_bits[:1] + lower
@@ -758,37 +782,25 @@
     back_in = tied(back_in, first.send(*first_order[0]), second.send(*second_order[0]))
     dqkv = attention_back(1, back_in, dqkv)
 
-    ready = tied(h1, dqkv, first.parts[1], second.parts[1])
-    g_qkv = dot(ready, dqkv, 0, 0).astype(bf16).reshape(heads // 2, 2, -1, 3 * D)
+    moved = []
+    for i, (left, right) in enumerate(zip(first_order[1:], second_order[1:])):
+        for half, stage in ((first, left), (second, right)):
+            half.parts = [tied(part, dqkv) for part in half.parts]
+            moved.append(half.send(*stage))
+    g_qkv = dot(tied(h1, dqkv, *moved), dqkv, 0, 0).astype(bf16).reshape(heads // 2, 2, -1, 3 * D)
+    left, right = [[tied(part, g_qkv) for part in half.parts] for half in (first, second)]
+    rest = Halving(jnp.concatenate([left[0], right[0]], axis=-2), None, first.places)
+    rest.parts.append(jnp.concatenate([left[1], right[1]], axis=-2))
+    moved = rest.send(*last_order[0])
+    g_qkv = tied(g_qkv, moved)
     sent_qkv = lax.dynamic_index_in_dim(g_qkv, 1 - core[0], 1, False)
     came_qkv = swap(sent_qkv, "head", 0)
-    moved = []
-    for left, right in zip(first_order[1:], second_order[1:]):
-        moved.append(first.after(sent_qkv).send(*left))
-        moved.append(second.after(sent_qkv).send(*right))
-    kept_qkv = tied(lax.dynamic_index_in_dim(g_qkv, core[0], 1, False), *moved)
+    kept_qkv = tied(lax.dynamic_index_in_dim(g_qkv, core[0], 1, False), *rest.parts)
     merged_qkv = (kept_qkv.astype(f32) + came_qkv.astype(f32)).astype(bf16)
     all_qkv = exchange(merged_qkv.reshape(-1, share, 3 * D))
-    dx = pl.pallas_call(
-        input_kernel,
-        grid=(length // ROWS,),
-        in_specs=[
-            by_step((ROWS, 3 * D)),
-            fixed((D, 3 * D + 128)),
-            by_step((ROWS, D)),
-            by_step((ROWS, D)),
-            fixed((8, D)),
-        ],
-        out_specs=by_step((ROWS, D)),
-        out_shape=jax.ShapeDtypeStruct((length, D), f32),
-        compiler_params=params(),
-        cost_estimate=cost(10),
-        name="input_grad",
-    )(dqkv, wq, x, tied(dy1, merged_qkv), gain_rows)
-    left, right = [[tied(part, dx) for part in h.parts] for h in (first, second)]
-    rest = Halving(jnp.concatenate([left[0], right[0]], axis=-2), None, first.places)
-    rest.parts.append(jnp.concatenate([left[1], right[1]], axis=-2))
-    for stage in last_order:
+    dx = input_call(dqkv, wq, x, tied(dy1, merged_qkv), gain_rows)
+    for stage in last_order[1:]:
+        rest.parts = [tied(part, dx) for part in rest.parts]
         rest.send(*stage)
     kept, came = rest.parts
     count = lax.axis_size(AXES)
@@ -797,17 +809,18 @@
         out_shape=[
             jax.ShapeDtypeStruct((share, 3 * D), f32),
             jax.ShapeDtypeStruct((9 * share, 512), f32),
-            jax.ShapeDtypeStruct((share, 2), f32),
+            jax.ShapeDtypeStruct((2, share), f32),
             jax.ShapeDtypeStruct((count, 8, 128), f32),
         ],
         name="finish",
     )(all_qkv, kept, came, packed, later_own)
-    total_squares = total_of(spread)
     sum_qkv = sum_qkv.reshape(share, PAIRS, 3, 128).transpose(0, 2, 1, 3).reshape(share, 3, D)
     sum_up = sums[: 4 * share].reshape(4, share, 512).transpose(1, 0, 2).reshape(share, FF)
     sum_down = sums[4 * share : 8 * share]
     sum_out = sums[8 * share :]
-    reduced = (sum_qkv, sum_out, sum_up, sum_down, sum_gains)
+    reduced = lax.optimization_barrier((sum_qkv, sum_out, sum_up, sum_down, sum_gains))
+    reduced = reduced[:4] + (reduced[4].T,)
+    total_squares = total_of(spread)
     grad_norm = jnp.sqrt(total_squares)
     clip_factor = jnp.minimum(1.0, max_norm / (grad_norm + 1e-06))
     step_value = step_count.astype(f32)

time: 273 us -> 263 us (0.963)
  Pallas kernels: 135 us -> 126 us
  other arithmetic: 16.5 us -> 11.6 us
  waiting for transfers between devices: 48.1 us -> 53 us
    pallas_call x5, Pallas kernels: 132 us -> 124 us  [the longest x1 47.2 us: middle_call(): pl.pallas_call(partial(middle_kernel, group), grid_spec=pltpu.PrefetchSca...]
    ppermute x14, waiting for transfers between devices: 37.7 us -> 44.9 us  [swap(): return lax.ppermute(value, axis, [(i, i ^ 1 << bit) for i in range(size)])]
  transfers between devices with their start and end apart: 19 -> 19, of which waited for: 11 -> 12; matrix products, arithmetic and copies ran while one was open for 4% -> 7% of each run, Pallas kernels for 31% -> 29%
where the time goes in v3:
time: 263 us; the launch traced here: 262 us
  Pallas kernels  126 us (48%)
  waiting for transfers between devices  53 us (20%)
  starting transfers between devices  36.8 us (14%)
  between operations  17.2 us (7%)
  other arithmetic  11.6 us (4%)
  local copies, waits for them, and re-layouts  11.5 us (4%)
  matrix products  6.3 us (2%)
    pallas_call x1, Pallas kernels, middle_call(): pl.pallas_call(partial(middle_kernel, group), grid_spec=pltpu.PrefetchSca...  47.2 us
    ppermute x14, waiting for transfers between devices, swap(): return lax.ppermute(value, axis, [(i, i ^ 1 << bit) for i in range(size)])  44.9 us
    pallas_call x2, Pallas kernels, backward_call(): pl.pallas_call(partial(backward_kernel, count), grid_spec=pltpu.PrefetchS...  34.2 us
    pallas_call x1, Pallas kernels, forward_call(): pl.pallas_call(forward_kernel, grid_spec=pltpu.PrefetchScalarGridSpec(num...  32.5 us
    ppermute x14, starting transfers between devices, swap(): return lax.ppermute(value, axis, [(i, i ^ 1 << bit) for i in range(size)])  24.6 us
    pallas_call x1, Pallas kernels, input_call(): pl.pallas_call(input_kernel, grid=(length // ROWS,), in_specs=[by_step((R...  9.69 us
    dot_general x1, matrix products, dot(): lax.dot_general(a, b, (((ca,), (cb,)), ((), ())), preferred_element_type=...  6.3 us
    all_to_all x1, starting transfers between devices, exchange(): lax.all_to_all(blocks, AXES, split_axis=0, concat_axis=0, axis_index_grou...  5.9 us
  transfers between devices with their start and end apart: 19, of which 12 were waited for; matrix products, arithmetic and copies ran while one was open for 7% of the time, Pallas kernels for 29%

profile of v3, /device:TPU:0, one launch (start us, length us, event | category | flops | bytes accessed | tf_op | source)
XLA Modules:
  0.0 262.5 jit_solution(18419976266012155930)
XLA Ops:
  7.3 1.4 slice_bitcast_fusion
  9.1 4.0 %collective-permute-start = (bf16[16,1664]{1,0:T(8,128)(2,1)S(1)}, bf16[16,1664]{1,0:T(8,128)(2,1)S(1)}, u32[]{:S(2)}, u32[]{:S(2)}) collective-permute-start(bf16[16,1664]{1,0:T(8,128)(2,1)S(1)} %concatenate.81.packed_ref), channel_id=1, source_target_pairs={{0,4},{1,5},{2,6},{3,7},{4,0},{5,1},{6,2},{7,3},{8,12},{9,13},{10,... | collective-permute-start | bytes 159752 | tf_op jit(solution)/shard_map/ppermute | solution.py:384
  13.3 2.6 collective-permute-done
  15.9 1.4 collective-permute-start.1
  17.4 1.4 collective-permute-start.2
  20.0 2.2 collective-permute-done.2
  22.2 1.8 collective-permute-start.3
  25.6 5.6 %collective-permute-done.3 = bf16[2,2,16,1664]{3,2,0,1:T(8,128)(2,1)S(1)} collective-permute-done((bf16[2,2,16,1664]{3,2,0,1:T(8,128)(2,1)S(1)}, bf16[2,2,16,1664]{3,2,0,1:T(8,128)(2,1)S(1)}, u32[]{:S(2)}, u32[]{:S(2)}) %collective-permute-start.3) | collective-permute-done | bytes 213024 | tf_op jit(solution)/shard_map/ppermute | solution.py:384
  31.3 3.6 %collective-permute-start.4 = (bf16[2,2,2,16,1664]{4,3,0,1,2:T(8,128)(2,1)S(1)}, bf16[2,2,2,16,1664]{4,3,0,1,2:T(8,128)(2,1)S(1)}, u32[]{:S(2)}, u32[]{:S(2)}) collective-permute-start(bf16[2,2,2,16,1664]{4,3,0,1,2:T(8,128)(2,1)S(1)} %maximum_select_fusion.4), channel_id=1, source_target_pairs={{0,16},{8,24},{16,0},{24,8},{1,17},{9,25},{17,1},{25,9},{2,18},{10... | collective-permute-start | bytes 1277960 | tf_op jit(solution)/shard_map/ppermute | solution.py:384
  35.0 9.3 %collective-permute-done.4 = bf16[2,2,2,16,1664]{4,3,0,1,2:T(8,128)(2,1)S(1)} collective-permute-done((bf16[2,2,2,16,1664]{4,3,0,1,2:T(8,128)(2,1)S(1)}, bf16[2,2,2,16,1664]{4,3,0,1,2:T(8,128)(2,1)S(1)}, u32[]{:S(2)}, u32[]{:S(2)}) %collective-permute-start.4) | collective-permute-done | bytes 426016 | tf_op jit(solution)/shard_map/ppermute | solution.py:384
  44.8 2.1 collective-permute-done.5
  47.2 1.4 copy.68
  48.6 32.5 %forward.1 = (bf16[2048,512]{1,0:T(8,128)(2,1)}, bf16[2048,1536]{1,0:T(8,128)(2,1)}, bf16[2048,2048]{1,0:T(8,128)(2,1)}, bf16[2048,2048]{1,0:T(8,128)(2,1)}, bf1...) custom-call(s32[12]{0:T(128)} %slice.43.ends_ref, ...), custom_call_target="tpu_custom_call" | custom-call | flops 1750000000 | bytes 5250000 | tf_op jit(solution)/shard_map/forward/pallas_call | solution.py:529
  81.4 47.2 %middle.1 = (bf16[2048,512]{1,0:T(8,128)(2,1)}, f32[2048,512]{1,0:T(8,128)}, bf16[2048,1024]{1,0:T(8,128)(2,1)}, bf16[16,64,512]{2,1,0:T(8,128)(2,1)}, bf16[16,8...) custom-call(s32[12]{0:T(128)} %slice.43.ends_ref, ...), custom_call_target="tpu_custom_call" | custom-call | flops 2400000000 | bytes 7200000 | tf_op jit(solution)/shard_map/middle/pallas_call | solution.py:568
  130.5 3.7 %collective-permute-done.6.refs_12_.refs_13_ = bf16[4,256,256]{2,1,0:T(8,128)(2,1)S(1)} collective-permute-done((bf16[4,256,256]{2,1,0:T(8,128)(2,1)}, bf16[4,256,256]{2,1,0:T(8,128)(2,1)S(1)}, u32[]{:S(2)}, u32[]{:S(2)}) %collective-permute-start.6) | collective-permute-done | bytes 524320 | tf_op jit(solution)/shard_map/ppermute | solution.py:763
  135.0 17.3 %backward.2.refs_14_ = bf16[2048,1536]{1,0:T(8,128)(2,1)} custom-call(s32[12]{0:T(128)} %slice.43.ends_ref, f32[6,1,512]{2,1,0:T(1,128)} %bitcast.111, bf16[512,256]{1,0:T(8,128)(2,1)} %maximum_maximum_fusion.gather_ref, bf16[2048,2048]{1,0:T(8,128)(2,1)} %get-tuple-element.84.refs_0_.refs_1_, bf16[2048,2048]{1,0:T(8,128)(2,1)} %get-tuple-element.84.refs_0_.refs_1_, ...), custom_call_target="tpu_custom_call" | custom-call | flops 800000000 | bytes 2400000 | tf_op jit(solution)/shard_map/backward/pallas_call | solution.py:618
  153.7 1.3 constant_dynamic-slice_fusion.2
  155.1 5.9 %collective-permute-start.9 = (bf16[2,2,2,64,512]{4,3,0,1,2:T(8,128)(2,1)S(1)}, bf16[2,2,2,64,512]{4,3,0,1,2:T(8,128)(2,1)}, u32[]{:S(2)}, u32[]{:S(2)}) collective-permute-start(bf16[2,2,2,64,512]{4,3,0,1,2:T(8,128)(2,1)S(1)} %fusion.2), channel_id=1, source_target_pairs={{0,16},{8,24},{16,0},{24,8},{1,17},{9,25},{17,1},{25,9},{2,18},{10... | collective-permute-start | bytes 1572872 | tf_op jit(solution)/shard_map/ppermute | solution.py:384
  161.4 1.5 collective-permute-start.10
  163.0 17.0 %backward.3.dqkv_ref = bf16[2048,1536]{1,0:T(8,128)(2,1)} custom-call(s32[12]{0:T(128)} %slice.43.ends_ref, f32[6,1,512]{2,1,0:T(1,128)} %bitcast.112, bf16[512,256]{1,0:T(8,128)(2,1)} %maximum_maximum_fusion.gather_ref, bf16[2048,2048]{1,0:T(8,128)(2,1)} %get-tuple-element.84.refs_0_.refs_1_, ...), custom_call_target="tpu_custom_call", output_to_operand_aliasing={{}: (17, {})} | custom-call | flops 800000000 | bytes 2400000 | tf_op jit(solution)/shard_map/backward/pallas_call | solution.py:618
  180.2 1.3 fusion.9
  182.5 6.3 %convolution_convert_fusion = bf16[512,1536]{1,0:T(8,128)(2,1)S(1)} fusion(bf16[2048,512]{1,0:T(8,128)(2,1)S(1)} %copy-done.27, bf16[2048,1536]{1,0:T(8,128)(2,1)} %backward.3.dqkv_ref), kind=kOutput, calls=%fused_computation | convolution fusion | flops 3222011904 | bytes 9961472 | tf_op jit(solution)/shard_map/dot_general | solution.py:37
  189.7 1.9 collective-permute-done.12
  192.1 1.9 collective-permute-start.13
  194.0 7.6 %collective-permute-done.13 = bf16[2,144,512]{2,1,0:T(8,128)(2,1)S(1)} collective-permute-done((bf16[2,144,512]{2,1,0:T(8,128)(2,1)S(1)}, bf16[2,144,512]{2,1,0:T(8,128)(2,1)S(1)}, u32[]{:S(2)}, u32[]{:S(2)}) %collective-permute-start.13) | collective-permute-done | bytes 294944 | tf_op jit(solution)/shard_map/ppermute | solution.py:384
  202.7 5.9 %all-to-all-start = ((bf16[16,16,1536]{2,1,0:T(8,128)(2,1)}), bf16[16,16,1536]{2,1,0:T(8,128)(2,1)S(1)}, u32[]{:S(2)}, u32[]{:S(2)}) async-start(bf16[16,16,1536]{2,1,0:T(8,128)(2,1)} %bitcast.41), calls=%async_computation | async-start | bytes 1572864 | tf_op jit(solution)/shard_map/all_to_all | solution.py:467
  208.6 9.7 %input_grad.1 = f32[2048,512]{1,0:T(8,128)} custom-call(bf16[2048,1536]{1,0:T(8,128)(2,1)} %backward.3.dqkv_ref, bf16[512,1664]{1,0:T(8,128)(2,1)} %bitcast.87, bf16[2048,512]{1,0:T(8,128)(2,1)} %bitcast.85, f32[2048,512]{1,0:T(8,128)} %get-tuple-element.111.dy1_ref, f32[8,512]{1,0:T(8,128)} %get-tuple-element.81.gains_ref), custom_call_target="tpu_custom_call" | custom-call | flops 500000000 | bytes 1500000 | tf_op jit(solution)/shard_map/input_grad/pallas_call | solution.py:641
  219.1 2.9 %collective-permute-start.15 = (bf16[144,512]{1,0:T(8,128)(2,1)S(1)}, bf16[144,512]{1,0:T(8,128)(2,1)S(1)}, u32[]{:S(2)}, u32[]{:S(2)}) collective-permute-start(bf16[144,512]{1,0:T(8,128)(2,1)S(1)} %get-tuple-element.161), channel_id=1, source_target_pairs={{0,4},{1,5},{2,6},{3,7},{4,0},{5,1},{6,2},{7,3},{8,12},{9,13},{10,... | collective-permute-start | bytes 442376 | tf_op jit(solution)/shard_map/ppermute | solution.py:384
  222.0 12.7 %collective-permute-done.15.came_ref = bf16[144,512]{1,0:T(8,128)(2,1)S(1)} collective-permute-done((bf16[144,512]{1,0:T(8,128)(2,1)S(1)}, bf16[144,512]{1,0:T(8,128)(2,1)S(1)}, u32[]{:S(2)}, u32[]{:S(2)}) %collective-permute-start.15) | collective-permute-done | bytes 147488 | tf_op jit(solution)/shard_map/ppermute | solution.py:384
  235.7 2.3 finish.1
  238.0 3.7 %all-to-all-start.1 = ((f32[32,8,128]{2,1,0:T(8,128)}), f32[32,8,128]{2,1,0:T(8,128)S(1)}, u32[]{:S(2)}, u32[]{:S(2)}) async-start(f32[32,8,128]{2,1,0:T(8,128)} %get-tuple-element.114), calls=%async_computation.1 | async-start | bytes 262144 | tf_op jit(solution)/shard_map/all_to_all | solution.py:473
  245.4 4.1 %all-to-all-done.1 = f32[32,8,128]{2,1,0:T(8,128)S(1)} async-done(((f32[32,8,128]{2,1,0:T(8,128)}), f32[32,8,128]{2,1,0:T(8,128)S(1)}, u32[]{:S(2)}, u32[]{:S(2)}) %all-to-all-start.1) | async-done | bytes 131104 | tf_op jit(solution)/shard_map/all_to_all | solution.py:473
  (131 shorter events, 21.9 us)
Async XLA Ops:
  7.2 10.0 %copy-start.15 = (bf16[256,64]{0,1:T(8,128)(2,1)S(1)}, bf16[256,64]{0,1:T(8,128)(2,1)}, u32[]{:S(2)}) copy-start(bf16[256,64]{0,1:T(8,128)(2,1)} %param.23) | copy-start | bytes 98308
  7.3 11.5 %copy-start.19 = (s32[1,8192]{1,0:T(1,128)S(1)}, s32[1,8192]{1,0:T(1,128)}, u32[]{:S(2)}) copy-start(s32[1,8192]{1,0:T(1,128)} %param.22) | copy-start | bytes 98308
  7.3 74.2 %all-gather.3.cloned.1.call-start = ((), (), s32[]{:S(2)}) async-start(), calls=%async_computation.2 | async-start | bytes 4866048 | tf_op jit(solution)/shard_map/all_gather | solution.py:711
  9.1 13.1 %copy-start.7 = (bf16[16,1664]{1,0:T(8,128)(2,1)}, bf16[16,1664]{1,0:T(8,128)(2,1)S(1)}, u32[]{:S(2)}) copy-start(bf16[16,1664]{1,0:T(8,128)(2,1)S(1)} %concatenate.81.packed_ref) | copy-start | bytes 159748
  9.1 6.7 %collective-permute-start = (bf16[16,1664]{1,0:T(8,128)(2,1)S(1)}, bf16[16,1664]{1,0:T(8,128)(2,1)S(1)}, u32[]{:S(2)}, u32[]{:S(2)}) collective-permute-start(bf16[16,1664]{1,0:T(8,128)(2,1)S(1)} %concatenate.81.packed_ref), channel_id=1, source_target_pairs={{0,4},{1,5},{2,6},{3,7},{4,0},{5,1},{6,2},{7,3},{8,12},{9,13},{10,... | collective-permute-start | bytes 159752 | tf_op jit(solution)/shard_map/ppermute | solution.py:384
  15.9 9.7 %collective-permute-start.1 = (bf16[1024,512]{1,0:T(8,128)(2,1)S(1)}, bf16[1024,512]{1,0:T(8,128)(2,1)S(1)}, u32[]{:S(2)}, u32[]{:S(2)}) collective-permute-start(bf16[1024,512]{1,0:T(8,128)(2,1)S(1)} %slice_bitcast_fusion), channel_id=1, source_target_pairs={{0,8},{8,16},{16,24},{1,9},{9,17},{17,25},{2,10},{10,18},{18,26},{... | collective-permute-start | bytes 3145736 | tf_op jit(solution)/shard_map/ppermute | solution.py:707
  17.4 4.8 %collective-permute-start.2 = (bf16[2,16,1664]{2,1,0:T(8,128)(2,1)S(1)}, bf16[2,16,1664]{2,1,0:T(8,128)(2,1)S(1)}, u32[]{:S(2)}, u32[]{:S(2)}) collective-permute-start(bf16[2,16,1664]{2,1,0:T(8,128)(2,1)S(1)} %maximum_select_fusion.6), channel_id=1, source_target_pairs={{0,2},{1,3},{2,0},{3,1},{4,6},{5,7},{6,4},{7,5},{8,10},{9,11},{10,... | collective-permute-start | bytes 319496 | tf_op jit(solution)/shard_map/ppermute | solution.py:384
  22.2 9.0 %collective-permute-start.3 = (bf16[2,2,16,1664]{3,2,0,1:T(8,128)(2,1)S(1)}, bf16[2,2,16,1664]{3,2,0,1:T(8,128)(2,1)S(1)}, u32[]{:S(2)}, u32[]{:S(2)}) collective-permute-start(bf16[2,2,16,1664]{3,2,0,1:T(8,128)(2,1)S(1)} %maximum_select_fusion.5), channel_id=1, source_target_pairs={{0,1},{1,0},{2,3},{3,2},{4,5},{5,4},{6,7},{7,6},{8,9},{9,8},{10,11... | collective-permute-start | bytes 638984 | tf_op jit(solution)/shard_map/ppermute | solution.py:384
  25.6 18.7 %copy-start.26 = (bf16[1024,512]{1,0:T(8,128)(2,1)}, bf16[1024,512]{1,0:T(8,128)(2,1)S(1)}, u32[]{:S(2)}) copy-start(bf16[1024,512]{1,0:T(8,128)(2,1)S(1)} %collective-permute-done.1.xh_ref) | copy-start | bytes 3145732
  31.3 13.0 %collective-permute-start.4 = (bf16[2,2,2,16,1664]{4,3,0,1,2:T(8,128)(2,1)S(1)}, bf16[2,2,2,16,1664]{4,3,0,1,2:T(8,128)(2,1)S(1)}, u32[]{:S(2)}, u32[]{:S(2)}) collective-permute-start(bf16[2,2,2,16,1664]{4,3,0,1,2:T(8,128)(2,1)S(1)} %maximum_select_fusion.4), channel_id=1, source_target_pairs={{0,16},{8,24},{16,0},{24,8},{1,17},{9,25},{17,1},{25,9},{2,18},{10... | collective-permute-start | bytes 1277960 | tf_op jit(solution)/shard_map/ppermute | solution.py:384
  44.4 2.4 collective-permute-start.5
  128.6 25.1 %collective-permute-start.7 = (bf16[16,64,512]{2,1,0:T(8,128)(2,1)}, bf16[16,64,512]{2,1,0:T(8,128)(2,1)}, u32[]{:S(2)}, u32[]{:S(2)}) collective-permute-start(bf16[16,64,512]{2,1,0:T(8,128)(2,1)} %get-tuple-element.91), channel_id=1, source_target_pairs={{0,8},{8,0},{16,24},{24,16},{1,9},{9,1},{17,25},{25,17},{2,10},{10... | collective-permute-start | bytes 3145736 | tf_op jit(solution)/shard_map/ppermute | solution.py:384
  129.0 32.1 %collective-permute-start.8 = (bf16[16,80,512]{2,1,0:T(8,128)(2,1)}, bf16[16,80,512]{2,1,0:T(8,128)(2,1)S(1)}, u32[]{:S(2)}, u32[]{:S(2)}) collective-permute-start(bf16[16,80,512]{2,1,0:T(8,128)(2,1)} %get-tuple-element.92), channel_id=1, source_target_pairs={{0,8},{8,0},{16,24},{24,16},{1,9},{9,1},{17,25},{25,17},{2,10},{10... | collective-permute-start | bytes 3932168 | tf_op jit(solution)/shard_map/ppermute | solution.py:384
  129.2 5.0 %collective-permute-start.6 = (bf16[4,256,256]{2,1,0:T(8,128)(2,1)}, bf16[4,256,256]{2,1,0:T(8,128)(2,1)S(1)}, u32[]{:S(2)}, u32[]{:S(2)}) collective-permute-start(bf16[4,256,256]{2,1,0:T(8,128)(2,1)} %get-tuple-element.89), channel_id=1, source_target_pairs={{8,0},{16,8},{24,16},{9,1},{17,9},{25,17},{10,2},{18,10},{26,18},{... | collective-permute-start | bytes 1572872 | tf_op jit(solution)/shard_map/ppermute | solution.py:763
  135.0 17.3 %copy-start.3 = (bf16[16,64,512]{2,1,0:T(8,128)(2,1)S(1)}, bf16[16,64,512]{2,1,0:T(8,128)(2,1)}, u32[]{:S(2)}) copy-start(bf16[16,64,512]{2,1,0:T(8,128)(2,1)} %get-tuple-element.94) | copy-start | bytes 3145732
  155.1 25.0 %collective-permute-start.9 = (bf16[2,2,2,64,512]{4,3,0,1,2:T(8,128)(2,1)S(1)}, bf16[2,2,2,64,512]{4,3,0,1,2:T(8,128)(2,1)}, u32[]{:S(2)}, u32[]{:S(2)}) collective-permute-start(bf16[2,2,2,64,512]{4,3,0,1,2:T(8,128)(2,1)S(1)} %fusion.2), channel_id=1, source_target_pairs={{0,16},{8,24},{16,0},{24,8},{1,17},{9,25},{17,1},{25,9},{2,18},{10... | collective-permute-start | bytes 1572872 | tf_op jit(solution)/shard_map/ppermute | solution.py:384
  161.4 20.8 %collective-permute-start.10 = (bf16[2,2,2,80,512]{4,3,1,2,0:T(8,128)(2,1)S(1)}, bf16[2,2,2,80,512]{4,3,1,2,0:T(8,128)(2,1)S(1)}, u32[]{:S(2)}, u32[]{:S(2)}) collective-permute-start(bf16[2,2,2,80,512]{4,3,1,2,0:T(8,128)(2,1)S(1)} %fusion), channel_id=1, source_target_pairs={{0,1},{1,0},{2,3},{3,2},{4,5},{5,4},{6,7},{7,6},{8,9},{9,8},{10,11... | collective-permute-start | bytes 1966088 | tf_op jit(solution)/shard_map/ppermute | solution.py:384
  181.5 8.2 %collective-permute-start.11 = (bf16[2,2,64,512]{3,2,0,1:T(8,128)(2,1)S(1)}, bf16[2,2,64,512]{3,2,0,1:T(8,128)(2,1)S(1)}, u32[]{:S(2)}, u32[]{:S(2)}) collective-permute-start(bf16[2,2,64,512]{3,2,0,1:T(8,128)(2,1)S(1)} %get-tuple-element.156), channel_id=1, source_target_pairs={{0,1},{1,0},{2,3},{3,2},{4,5},{5,4},{6,7},{7,6},{8,9},{9,8},{10,11... | collective-permute-start | bytes 786440 | tf_op jit(solution)/shard_map/ppermute | solution.py:384
  182.4 9.3 %collective-permute-start.12 = (bf16[2,2,80,512]{3,2,0,1:T(8,128)(2,1)S(1)}, bf16[2,2,80,512]{3,2,0,1:T(8,128)(2,1)S(1)}, u32[]{:S(2)}, u32[]{:S(2)}) collective-permute-start(bf16[2,2,80,512]{3,2,0,1:T(8,128)(2,1)S(1)} %get-tuple-element.148), channel_id=1, source_target_pairs={{0,16},{8,24},{16,0},{24,8},{1,17},{9,25},{17,1},{25,9},{2,18},{10... | collective-permute-start | bytes 983048 | tf_op jit(solution)/shard_map/ppermute | solution.py:384
  192.0 9.6 %collective-permute-start.14 = (bf16[2,128,1536]{2,1,0:T(8,128)(2,1)S(1)}, bf16[2,128,1536]{2,1,0:T(8,128)(2,1)S(1)}, u32[]{:S(2)}, u32[]{:S(2)}) collective-permute-start(bf16[2,128,1536]{2,1,0:T(8,128)(2,1)S(1)} %get-tuple-element.146), channel_id=1, source_target_pairs={{0,8},{8,0},{16,24},{24,16},{1,9},{9,1},{17,25},{25,17},{2,10},{10... | collective-permute-start | bytes 2359304 | tf_op jit(solution)/shard_map/ppermute | solution.py:384
  192.1 9.5 %collective-permute-start.13 = (bf16[2,144,512]{2,1,0:T(8,128)(2,1)S(1)}, bf16[2,144,512]{2,1,0:T(8,128)(2,1)S(1)}, u32[]{:S(2)}, u32[]{:S(2)}) collective-permute-start(bf16[2,144,512]{2,1,0:T(8,128)(2,1)S(1)} %get-tuple-element.154), channel_id=1, source_target_pairs={{0,2},{1,3},{2,0},{3,1},{4,6},{5,7},{6,4},{7,5},{8,10},{9,11},{10,... | collective-permute-start | bytes 884744 | tf_op jit(solution)/shard_map/ppermute | solution.py:384
  202.7 32.0 %all-to-all-start = ((bf16[16,16,1536]{2,1,0:T(8,128)(2,1)}), bf16[16,16,1536]{2,1,0:T(8,128)(2,1)S(1)}, u32[]{:S(2)}, u32[]{:S(2)}) async-start(bf16[16,16,1536]{2,1,0:T(8,128)(2,1)} %bitcast.41), calls=%async_computation | async-start | bytes 1572864 | tf_op jit(solution)/shard_map/all_to_all | solution.py:467
  219.1 31.7 %copy-start.23 = (f32[16,2]{0,1:T(2,128)S(1)}, f32[16,2]{0,1:T(2,128)}, u32[]{:S(2)}) copy-start(f32[16,2]{0,1:T(2,128)} %param.38) | copy-start | bytes 388
  219.1 31.7 %copy-start.24 = (f32[16,2]{0,1:T(2,128)S(1)}, f32[16,2]{0,1:T(2,128)}, u32[]{:S(2)}) copy-start(f32[16,2]{0,1:T(2,128)} %param.37) | copy-start | bytes 388
  219.1 32.3 %copy-start.11 = (f32[64,512]{1,0:T(8,128)S(1)}, f32[64,512]{1,0:T(8,128)}, u32[]{:S(2)}) copy-start(f32[64,512]{1,0:T(8,128)} %param.36) | copy-start | bytes 393220
  219.1 32.3 %copy-start.12 = (f32[64,512]{1,0:T(8,128)S(1)}, f32[64,512]{1,0:T(8,128)}, u32[]{:S(2)}) copy-start(f32[64,512]{1,0:T(8,128)} %param.35) | copy-start | bytes 393220
  219.1 15.6 %collective-permute-start.15 = (bf16[144,512]{1,0:T(8,128)(2,1)S(1)}, bf16[144,512]{1,0:T(8,128)(2,1)S(1)}, u32[]{:S(2)}, u32[]{:S(2)}) collective-permute-start(bf16[144,512]{1,0:T(8,128)(2,1)S(1)} %get-tuple-element.161), channel_id=1, source_target_pairs={{0,4},{1,5},{2,6},{3,7},{4,0},{5,1},{6,2},{7,3},{8,12},{9,13},{10,... | collective-permute-start | bytes 442376 | tf_op jit(solution)/shard_map/ppermute | solution.py:384
  238.0 12.8 %copy-start.25 = (f32[2,16]{1,0:T(2,128)S(1)}, f32[2,16]{1,0:T(2,128)}, u32[]{:S(2)}) copy-start(f32[2,16]{1,0:T(2,128)} %get-tuple-element.122) | copy-start | bytes 388
  238.0 14.2 %copy-start.13 = (f32[16,2048]{1,0:T(8,128)S(1)}, f32[16,2048]{1,0:T(8,128)}, u32[]{:S(2)}) copy-start(f32[16,2048]{1,0:T(8,128)} %param.34) | copy-start | bytes 393220
  238.0 14.2 %copy-start.14 = (f32[16,2048]{1,0:T(8,128)S(1)}, f32[16,2048]{1,0:T(8,128)}, u32[]{:S(2)}) copy-start(f32[16,2048]{1,0:T(8,128)} %param.33) | copy-start | bytes 393220
  238.0 11.4 %all-to-all-start.1 = ((f32[32,8,128]{2,1,0:T(8,128)}), f32[32,8,128]{2,1,0:T(8,128)S(1)}, u32[]{:S(2)}, u32[]{:S(2)}) async-start(f32[32,8,128]{2,1,0:T(8,128)} %get-tuple-element.114), calls=%async_computation.1 | async-start | bytes 262144 | tf_op jit(solution)/shard_map/all_to_all | solution.py:473
  243.2 9.9 %copy-start.21 = (f32[16,512]{1,0:T(8,128)S(1)}, f32[16,512]{1,0:T(8,128)}, u32[]{:S(2)}) copy-start(f32[16,512]{1,0:T(8,128)} %param.31) | copy-start | bytes 98308
  (15 other events, 68.3 us)
Sparse Core Ops, SparseCore 0:
  16.0 65.3 all-gather.2

commit v4 on v3

--- a/solution.py
+++ b/solution.py
@@ -84,11 +84,6 @@
     rows = lax.broadcasted_iota(jnp.int32, (CHUNK, CHUNK), 0)
     cols = lax.broadcasted_iota(jnp.int32, (CHUNK, CHUNK), 1)
     return seg_col, flag((rows >= cols) & (seg_col == seg_row))
-
-
-def compacted(first, second):
-    ma, mb = half_masks(256)
-    return first * ma + second * mb
 
 
 def forward_kernel(
@@ -180,10 +175,10 @@
 
     @pl.when(step == 0)
     def _():
-        up_acc[...] = jnp.zeros_like(up_acc)
-        down_acc[...] = jnp.zeros_like(down_acc)
-        out_acc[...] = jnp.zeros_like(out_acc)
         back_acc[...] = jnp.zeros_like(back_acc)
+
+    def so_far(value):
+        return jnp.where(step == 0, 0.0, value)
 
     o = o_ref[...]
     g = g_ref[...]
@@ -204,8 +199,8 @@
         d_up = (d_act * (cdf + up * density)).astype(bf16)
         act_ref[:, fs] = act
         dup_ref[:, fs] = d_up
-        down_acc[fs, :] += dot(act, g, 0, 0)
-        up_acc[:, fs] += dot(h2, d_up, 0, 0)
+        down_acc[fs, :] = so_far(down_acc[fs, :]) + dot(act, g, 0, 0)
+        up_acc[:, fs] = so_far(up_acc[:, fs]) + dot(h2, d_up, 0, 0)
     out_ref[...] = (y1 + dot(act_ref[...], wd_ref[...].reshape(FF, D))).astype(bf16)
     d_h2 = dot(dup_ref[:, :cut], wu0_ref[...].reshape(D, cut), 1, 1)
     for f in range(1, FF // cut):
@@ -216,7 +211,7 @@
     dy1 = g.astype(f32) + r2 * (e2 - n2 * jnp.mean(e2 * n2, axis=-1, keepdims=True))
     dy1_ref[...] = dy1
     da = dy1.astype(bf16)
-    out_acc[...] += dot(da, o, 0, 0)
+    out_acc[...] = so_far(out_acc[...]) + dot(da, o, 0, 0)
     d_o = dot(da, wo)
     product = d_o * o.astype(f32)
     high = product.astype(bf16)
@@ -265,9 +260,19 @@
                     ups[here, 16 * f : 16 * (f + 1)] = piece.reshape(group, 16, cut)
                 others[here, :64] = down_acc[tall].astype(bf16).reshape(group, 64, D)
                 others[here, 64:] = out_acc[thin].astype(bf16).reshape(group, 16, D)
+        ma, mb = half_masks(128)
         for p in range(PAIRS):
-            back = back_acc[p].astype(bf16)
-            back_ref[p] = compacted(back[:FEATS], back[FEATS:])
+            first, second = back_acc[p, :FEATS], back_acc[p, FEATS:]
+            back_ref[p, :FEATS] = first[:, :128].astype(bf16) * ma + second[:, :128].astype(bf16) * mb
+            rows = []
+            for side, lane in ((first, 0), (second, HD)):
+                turned = side[:, 128:].T
+                total = turned[lane : lane + 1] + turned[lane + 1 : lane + 2]
+                high = total.astype(bf16).astype(f32)
+                for part in (high, total - high):
+                    rows += [part[:, :128], part[:, 128:]]
+            rows.append(jnp.zeros((8, 128), f32))
+            back_ref[p, FEATS:] = jnp.concatenate(rows, axis=0).astype(bf16)
 
 
 def backward_kernel(pairs, ends_ref, seg_ref, gather_ref, *refs):
@@ -280,13 +285,21 @@
     p_refs, pq_refs, pk_refs, qkv_refs, dn_refs, t_refs, back_refs = [
         refs[i * pairs : (i + 1) * pairs] for i in range(7)
     ]
-    ma2, mb2 = half_masks(256)
 
     @pl.when(step == 0)
     def _():
+        lane = lanes(128)
         for p in range(pairs):
-            state_ref[p, :FEATS] = (back_refs[p][0] * ma2).astype(f32)
-            state_ref[p, FEATS:] = (back_refs[p][0] * mb2).astype(f32)
+            extra = back_refs[p][0, FEATS:].astype(f32)
+            for i, mask in enumerate(half_masks(128)):
+                rows = slice(FEATS * i, FEATS * (i + 1))
+                state_ref[p, rows, :128] = (back_refs[p][0, :FEATS] * mask).astype(f32)
+                total = jnp.zeros((FEATS, 128), f32)
+                for t in range(2):
+                    at_row = 4 * i + 2 * t
+                    row = jnp.concatenate([extra[at_row : at_row + 1], extra[at_row + 1 : at_row + 2]], axis=1)
+                    total = jnp.where(lane == HD * i + t, as_column(row), total)
+                state_ref[p, rows, 128:] = total
 
     seg = seg_ref[0]
     seg_col = as_column(seg)
@@ -564,7 +577,7 @@
         ((ROWS, D), (length, D), f32),
         ((ROWS, PAIRS * 256), (length, PAIRS * 256), bf16),
     ]
-    sums = [(D // 32, 64, 512), (D // 32, 80, 512)] * 2 + [(PAIRS, FEATS, 256)]
+    sums = [(D // 32, 64, 512), (D // 32, 80, 512)] * 2 + [(PAIRS, FEATS + 16, 128)]
     return pl.pallas_call(
         partial(middle_kernel, group),
         grid_spec=pltpu.PrefetchScalarGridSpec(
@@ -607,7 +620,9 @@
         return pl.BlockSpec(shape, lambda c, *_: (steps - 1 - c, at) + rest)
 
     def state(at):
-        return pl.BlockSpec((1, FEATS, 256), lambda *_: (at, 0, 0), pipeline_mode=pl.Buffered(1))
+        return pl.BlockSpec(
+            (1, FEATS + 16, 128), lambda *_: (at, 0, 0), pipeline_mode=pl.Buffered(1)
+        )
 
     specs = [pl.BlockSpec((1, 1, ROWS), lambda c, *_: (steps + halo - 1 - c, 0, 0))]
     specs += [fixed(gather.shape)]
@@ -766,7 +781,7 @@
 
     def attention_back(at, back_in, *written):
         arrays = (scores, pq, pk, qkv, dn, states, back_in)
-        return backward_call(at, 2, ends, seg_rows, gather, arrays, *written)
+        return backward_call(at, 1, ends, seg_rows, gather, arrays, *written)
 
     lower = [(axis, bit, place - (place > core_bit[2])) for axis, bit, place in far_bits]
     first_order = lower + row_bits[:1]
@@ -775,12 +790,11 @@
     places = [place for _, _, place in first_order + last_order]
     cut = 4 * share
 
-    dqkv = attention_back(0, tied(back_in, sent_up, sent_rest))
-    kept_up, kept_rest = tied(kept_up, dqkv), tied(kept_rest, dqkv)
+    kept_up, kept_rest = tied(kept_up, back_in), tied(kept_rest, back_in)
     first = Halving(kept_up, came_up, places)
     second = Halving(kept_rest, came_rest, places)
     back_in = tied(back_in, first.send(*first_order[0]), second.send(*second_order[0]))
-    dqkv = attention_back(1, back_in, dqkv)
+    dqkv = attention_back(0, back_in)
 
     moved = []
     for i, (left, right) in enumerate(zip(first_order[1:], second_order[1:])):

time: 263 us -> 258 us (0.981)
  Pallas kernels: 126 us -> 122 us
    pallas_call x2 -> x1, Pallas kernels: 34.2 us -> 31 us  [backward_call(): pl.pallas_call(partial(backward_kernel, count), grid_spec=pltpu.PrefetchS...]
  transfers between devices with their start and end apart: 19 -> 19, of which waited for: 12 -> 12; matrix products, arithmetic and copies ran while one was open for 7% -> 8% of each run, Pallas kernels for 29% -> 28%
where the time goes in v4:
time: 258 us; the launch traced here: 257 us
  Pallas kernels  122 us (47%)
  waiting for transfers between devices  52.6 us (20%)
  starting transfers between devices  34.4 us (13%)
  between operations  17.3 us (7%)
  other arithmetic  13.2 us (5%)
  local copies, waits for them, and re-layouts  10.8 us (4%)
  matrix products  6.3 us (2%)
    pallas_call x1, Pallas kernels, middle_call(): pl.pallas_call(partial(middle_kernel, group), grid_spec=pltpu.PrefetchSca...  46.8 us
    ppermute x14, waiting for transfers between devices, swap(): return lax.ppermute(value, axis, [(i, i ^ 1 << bit) for i in range(size)])  44.9 us
    pallas_call x1, Pallas kernels, forward_call(): pl.pallas_call(forward_kernel, grid_spec=pltpu.PrefetchScalarGridSpec(num...  32.5 us
    pallas_call x1, Pallas kernels, backward_call(): pl.pallas_call(partial(backward_kernel, count), grid_spec=pltpu.PrefetchS...  31 us
    ppermute x14, starting transfers between devices, swap(): return lax.ppermute(value, axis, [(i, i ^ 1 << bit) for i in range(size)])  22.1 us
    pallas_call x1, Pallas kernels, input_call(): pl.pallas_call(input_kernel, grid=(length // ROWS,), in_specs=[by_step((R...  9.69 us
    dot_general x1, matrix products, dot(): lax.dot_general(a, b, (((ca,), (cb,)), ((), ())), preferred_element_type=...  6.3 us
    all_to_all x1, starting transfers between devices, exchange(): lax.all_to_all(blocks, AXES, split_axis=0, concat_axis=0, axis_index_grou...  5.87 us
  transfers between devices with their start and end apart: 19, of which 12 were waited for; matrix products, arithmetic and copies ran while one was open for 8% of the time, Pallas kernels for 28%

profile of v4, /device:TPU:0, one launch (start us, length us, event | category | flops | bytes accessed | tf_op | source)
XLA Modules:
  0.0 257.0 jit_solution(5398767368956913542)
XLA Ops:
  7.3 1.4 slice_bitcast_fusion
  9.1 4.0 %collective-permute-start = (bf16[16,1664]{1,0:T(8,128)(2,1)S(1)}, bf16[16,1664]{1,0:T(8,128)(2,1)S(1)}, u32[]{:S(2)}, u32[]{:S(2)}) collective-permute-start(bf16[16,1664]{1,0:T(8,128)(2,1)S(1)} %concatenate.81.packed_ref), channel_id=1, source_target_pairs={{0,4},{1,5},{2,6},{3,7},{4,0},{5,1},{6,2},{7,3},{8,12},{9,13},{10,... | collective-permute-start | bytes 159752 | tf_op jit(solution)/shard_map/ppermute | solution.py:397
  13.3 2.6 collective-permute-done
  15.9 1.4 collective-permute-start.1
  17.4 1.4 collective-permute-start.2
  20.0 2.2 collective-permute-done.2
  22.2 1.8 collective-permute-start.3
  25.6 5.6 %collective-permute-done.3 = bf16[2,2,16,1664]{3,2,0,1:T(8,128)(2,1)S(1)} collective-permute-done((bf16[2,2,16,1664]{3,2,0,1:T(8,128)(2,1)S(1)}, bf16[2,2,16,1664]{3,2,0,1:T(8,128)(2,1)S(1)}, u32[]{:S(2)}, u32[]{:S(2)}) %collective-permute-start.3) | collective-permute-done | bytes 213024 | tf_op jit(solution)/shard_map/ppermute | solution.py:397
  31.3 3.6 %collective-permute-start.4 = (bf16[2,2,2,16,1664]{4,3,0,1,2:T(8,128)(2,1)S(1)}, bf16[2,2,2,16,1664]{4,3,0,1,2:T(8,128)(2,1)S(1)}, u32[]{:S(2)}, u32[]{:S(2)}) collective-permute-start(bf16[2,2,2,16,1664]{4,3,0,1,2:T(8,128)(2,1)S(1)} %maximum_select_fusion.4), channel_id=1, source_target_pairs={{0,16},{8,24},{16,0},{24,8},{1,17},{9,25},{17,1},{25,9},{2,18},{10... | collective-permute-start | bytes 1277960 | tf_op jit(solution)/shard_map/ppermute | solution.py:397
  35.0 9.3 %collective-permute-done.4 = bf16[2,2,2,16,1664]{4,3,0,1,2:T(8,128)(2,1)S(1)} collective-permute-done((bf16[2,2,2,16,1664]{4,3,0,1,2:T(8,128)(2,1)S(1)}, bf16[2,2,2,16,1664]{4,3,0,1,2:T(8,128)(2,1)S(1)}, u32[]{:S(2)}, u32[]{:S(2)}) %collective-permute-start.4) | collective-permute-done | bytes 426016 | tf_op jit(solution)/shard_map/ppermute | solution.py:397
  44.8 2.1 collective-permute-done.5
  47.2 1.4 copy.67
  48.6 32.5 %forward.1 = (bf16[2048,512]{1,0:T(8,128)(2,1)}, bf16[2048,1536]{1,0:T(8,128)(2,1)}, bf16[2048,2048]{1,0:T(8,128)(2,1)}, bf16[2048,2048]{1,0:T(8,128)(2,1)}, bf1...) custom-call(s32[12]{0:T(128)} %slice.43.ends_ref, ...), custom_call_target="tpu_custom_call" | custom-call | flops 1750000000 | bytes 5250000 | tf_op jit(solution)/shard_map/forward/pallas_call | solution.py:542
  81.4 46.8 %middle.1 = (bf16[2048,512]{1,0:T(8,128)(2,1)}, f32[2048,512]{1,0:T(8,128)}, bf16[2048,1024]{1,0:T(8,128)(2,1)}, bf16[16,64,512]{2,1,0:T(8,128)(2,1)}, bf16[16,8...) custom-call(s32[12]{0:T(128)} %slice.43.ends_ref, ...), custom_call_target="tpu_custom_call" | custom-call | flops 2400000000 | bytes 7200000 | tf_op jit(solution)/shard_map/middle/pallas_call | solution.py:581
  130.2 3.3 %collective-permute-done.6.refs_24_.refs_25_.refs_26_.refs_27_ = bf16[4,272,128]{2,1,0:T(8,128)(2,1)S(1)} collective-permute-done((bf16[4,272,128]{2,1,0:T(8,128)(2,1)}, bf16[4,272,128]{2,1,0:T(8,128)(2,1)S(1)}, u32[]{:S(2)}, u32[]{:S(2)}) %collective-permute-start.6) | collective-permute-done | bytes 278560 | tf_op jit(solution)/shard_map/ppermute | solution.py:778
  133.5 1.4 constant_dynamic-slice_fusion.3
  135.0 1.3 constant_dynamic-slice_fusion.2
  137.2 3.5 %collective-permute-start.9 = (bf16[2,2,2,64,512]{4,3,0,1,2:T(8,128)(2,1)}, bf16[2,2,2,64,512]{4,3,0,1,2:T(8,128)(2,1)}, u32[]{:S(2)}, u32[]{:S(2)}) collective-permute-start(bf16[2,2,2,64,512]{4,3,0,1,2:T(8,128)(2,1)} %fusion.2), channel_id=1, source_target_pairs={{0,16},{8,24},{16,0},{24,8},{1,17},{9,25},{17,1},{25,9},{2,18},{10... | collective-permute-start | bytes 1572872 | tf_op jit(solution)/shard_map/ppermute | solution.py:397
  141.9 1.5 collective-permute-start.10
  143.5 31.0 %backward.1.dqkv_ref = bf16[2048,1536]{1,0:T(8,128)(2,1)} custom-call(s32[12]{0:T(128)} %slice.43.ends_ref, f32[6,1,512]{2,1,0:T(1,128)} %bitcast.112, bf16[512,256]{1,0:T(8,128)(2,1)} %maximum_maximum_fusion.gather_ref, bf16[2048,2048]{1,0:T(8,128)(2,1)} %get-tuple-element.83.refs_0_.refs_1_.refs_2_.refs_3_, ...), custom_call_target="tpu_custom_call" | custom-call | flops 1600000000 | bytes 4800000 | tf_op jit(solution)/shard_map/backward/pallas_call | solution.py:633
  174.7 1.3 fusion.9
  177.0 6.3 %convolution_convert_fusion = bf16[512,1536]{1,0:T(8,128)(2,1)S(1)} fusion(bf16[2048,512]{1,0:T(8,128)(2,1)S(1)} %copy-done.30, bf16[2048,1536]{1,0:T(8,128)(2,1)} %backward.1.dqkv_ref), kind=kOutput, calls=%fused_computation | convolution fusion | flops 3222011904 | bytes 9961472 | tf_op jit(solution)/shard_map/dot_general | solution.py:37
  184.3 1.9 collective-permute-done.12
  186.6 2.0 collective-permute-start.13
  188.6 7.6 %collective-permute-done.13 = bf16[2,144,512]{2,1,0:T(8,128)(2,1)S(1)} collective-permute-done((bf16[2,144,512]{2,1,0:T(8,128)(2,1)S(1)}, bf16[2,144,512]{2,1,0:T(8,128)(2,1)S(1)}, u32[]{:S(2)}, u32[]{:S(2)}) %collective-permute-start.13) | collective-permute-done | bytes 294944 | tf_op jit(solution)/shard_map/ppermute | solution.py:397
  197.2 5.9 %all-to-all-start = ((bf16[16,16,1536]{2,1,0:T(8,128)(2,1)}), bf16[16,16,1536]{2,1,0:T(8,128)(2,1)S(1)}, u32[]{:S(2)}, u32[]{:S(2)}) async-start(bf16[16,16,1536]{2,1,0:T(8,128)(2,1)} %bitcast.41), calls=%async_computation | async-start | bytes 1572864 | tf_op jit(solution)/shard_map/all_to_all | solution.py:480
  203.1 9.7 %input_grad.1 = f32[2048,512]{1,0:T(8,128)} custom-call(bf16[2048,1536]{1,0:T(8,128)(2,1)} %backward.1.dqkv_ref, bf16[512,1664]{1,0:T(8,128)(2,1)} %bitcast.87, bf16[2048,512]{1,0:T(8,128)(2,1)} %bitcast.85, f32[2048,512]{1,0:T(8,128)} %get-tuple-element.109.dy1_ref, f32[8,512]{1,0:T(8,128)} %get-tuple-element.80.gains_ref), custom_call_target="tpu_custom_call" | custom-call | flops 500000000 | bytes 1500000 | tf_op jit(solution)/shard_map/input_grad/pallas_call | solution.py:656
  213.6 2.9 %collective-permute-start.15 = (bf16[144,512]{1,0:T(8,128)(2,1)S(1)}, bf16[144,512]{1,0:T(8,128)(2,1)S(1)}, u32[]{:S(2)}, u32[]{:S(2)}) collective-permute-start(bf16[144,512]{1,0:T(8,128)(2,1)S(1)} %get-tuple-element.159), channel_id=1, source_target_pairs={{0,4},{1,5},{2,6},{3,7},{4,0},{5,1},{6,2},{7,3},{8,12},{9,13},{10,... | collective-permute-start | bytes 442376 | tf_op jit(solution)/shard_map/ppermute | solution.py:397
  216.5 12.7 %collective-permute-done.15.came_ref = bf16[144,512]{1,0:T(8,128)(2,1)S(1)} collective-permute-done((bf16[144,512]{1,0:T(8,128)(2,1)S(1)}, bf16[144,512]{1,0:T(8,128)(2,1)S(1)}, u32[]{:S(2)}, u32[]{:S(2)}) %collective-permute-start.15) | collective-permute-done | bytes 147488 | tf_op jit(solution)/shard_map/ppermute | solution.py:397
  230.1 2.3 finish.1
  232.5 3.7 %all-to-all-start.1 = ((f32[32,8,128]{2,1,0:T(8,128)}), f32[32,8,128]{2,1,0:T(8,128)S(1)}, u32[]{:S(2)}, u32[]{:S(2)}) async-start(f32[32,8,128]{2,1,0:T(8,128)} %get-tuple-element.112), calls=%async_computation.1 | async-start | bytes 262144 | tf_op jit(solution)/shard_map/all_to_all | solution.py:486
  239.8 4.0 %all-to-all-done.1 = f32[32,8,128]{2,1,0:T(8,128)S(1)} async-done(((f32[32,8,128]{2,1,0:T(8,128)}), f32[32,8,128]{2,1,0:T(8,128)S(1)}, u32[]{:S(2)}, u32[]{:S(2)}) %all-to-all-start.1) | async-done | bytes 131104 | tf_op jit(solution)/shard_map/all_to_all | solution.py:486
  (136 shorter events, 21.4 us)
Async XLA Ops:
  7.3 10.0 %copy-start.16 = (bf16[256,64]{0,1:T(8,128)(2,1)S(1)}, bf16[256,64]{0,1:T(8,128)(2,1)}, u32[]{:S(2)}) copy-start(bf16[256,64]{0,1:T(8,128)(2,1)} %param.23) | copy-start | bytes 98308
  7.3 11.5 %copy-start.21 = (s32[1,8192]{1,0:T(1,128)S(1)}, s32[1,8192]{1,0:T(1,128)}, u32[]{:S(2)}) copy-start(s32[1,8192]{1,0:T(1,128)} %param.22) | copy-start | bytes 98308
  7.3 74.2 %all-gather.3.cloned.1.call-start = ((), (), s32[]{:S(2)}) async-start(), calls=%async_computation.2 | async-start | bytes 4866048 | tf_op jit(solution)/shard_map/all_gather | solution.py:726
  9.1 13.1 %copy-start.8 = (bf16[16,1664]{1,0:T(8,128)(2,1)}, bf16[16,1664]{1,0:T(8,128)(2,1)S(1)}, u32[]{:S(2)}) copy-start(bf16[16,1664]{1,0:T(8,128)(2,1)S(1)} %concatenate.81.packed_ref) | copy-start | bytes 159748
  9.1 6.7 %collective-permute-start = (bf16[16,1664]{1,0:T(8,128)(2,1)S(1)}, bf16[16,1664]{1,0:T(8,128)(2,1)S(1)}, u32[]{:S(2)}, u32[]{:S(2)}) collective-permute-start(bf16[16,1664]{1,0:T(8,128)(2,1)S(1)} %concatenate.81.packed_ref), channel_id=1, source_target_pairs={{0,4},{1,5},{2,6},{3,7},{4,0},{5,1},{6,2},{7,3},{8,12},{9,13},{10,... | collective-permute-start | bytes 159752 | tf_op jit(solution)/shard_map/ppermute | solution.py:397
  15.9 9.7 %collective-permute-start.1 = (bf16[1024,512]{1,0:T(8,128)(2,1)S(1)}, bf16[1024,512]{1,0:T(8,128)(2,1)S(1)}, u32[]{:S(2)}, u32[]{:S(2)}) collective-permute-start(bf16[1024,512]{1,0:T(8,128)(2,1)S(1)} %slice_bitcast_fusion), channel_id=1, source_target_pairs={{0,8},{8,16},{16,24},{1,9},{9,17},{17,25},{2,10},{10,18},{18,26},{... | collective-permute-start | bytes 3145736 | tf_op jit(solution)/shard_map/ppermute | solution.py:722
  17.4 4.8 %collective-permute-start.2 = (bf16[2,16,1664]{2,1,0:T(8,128)(2,1)S(1)}, bf16[2,16,1664]{2,1,0:T(8,128)(2,1)S(1)}, u32[]{:S(2)}, u32[]{:S(2)}) collective-permute-start(bf16[2,16,1664]{2,1,0:T(8,128)(2,1)S(1)} %maximum_select_fusion.6), channel_id=1, source_target_pairs={{0,2},{1,3},{2,0},{3,1},{4,6},{5,7},{6,4},{7,5},{8,10},{9,11},{10,... | collective-permute-start | bytes 319496 | tf_op jit(solution)/shard_map/ppermute | solution.py:397
  22.2 9.0 %collective-permute-start.3 = (bf16[2,2,16,1664]{3,2,0,1:T(8,128)(2,1)S(1)}, bf16[2,2,16,1664]{3,2,0,1:T(8,128)(2,1)S(1)}, u32[]{:S(2)}, u32[]{:S(2)}) collective-permute-start(bf16[2,2,16,1664]{3,2,0,1:T(8,128)(2,1)S(1)} %maximum_select_fusion.5), channel_id=1, source_target_pairs={{0,1},{1,0},{2,3},{3,2},{4,5},{5,4},{6,7},{7,6},{8,9},{9,8},{10,11... | collective-permute-start | bytes 638984 | tf_op jit(solution)/shard_map/ppermute | solution.py:397
  31.3 13.0 %collective-permute-start.4 = (bf16[2,2,2,16,1664]{4,3,0,1,2:T(8,128)(2,1)S(1)}, bf16[2,2,2,16,1664]{4,3,0,1,2:T(8,128)(2,1)S(1)}, u32[]{:S(2)}, u32[]{:S(2)}) collective-permute-start(bf16[2,2,2,16,1664]{4,3,0,1,2:T(8,128)(2,1)S(1)} %maximum_select_fusion.4), channel_id=1, source_target_pairs={{0,16},{8,24},{16,0},{24,8},{1,17},{9,25},{17,1},{25,9},{2,18},{10... | collective-permute-start | bytes 1277960 | tf_op jit(solution)/shard_map/ppermute | solution.py:397
  44.4 2.4 collective-permute-start.5
  128.3 6.7 %collective-permute-start.7 = (bf16[16,64,512]{2,1,0:T(8,128)(2,1)}, bf16[16,64,512]{2,1,0:T(8,128)(2,1)}, u32[]{:S(2)}, u32[]{:S(2)}) collective-permute-start(bf16[16,64,512]{2,1,0:T(8,128)(2,1)} %get-tuple-element.91), channel_id=1, source_target_pairs={{0,8},{8,0},{16,24},{24,16},{1,9},{9,1},{17,25},{25,17},{2,10},{10... | collective-permute-start | bytes 3145736 | tf_op jit(solution)/shard_map/ppermute | solution.py:397
  128.6 12.2 %collective-permute-start.8 = (bf16[16,80,512]{2,1,0:T(8,128)(2,1)}, bf16[16,80,512]{2,1,0:T(8,128)(2,1)S(1)}, u32[]{:S(2)}, u32[]{:S(2)}) collective-permute-start(bf16[16,80,512]{2,1,0:T(8,128)(2,1)} %get-tuple-element.94), channel_id=1, source_target_pairs={{0,8},{8,0},{16,24},{24,16},{1,9},{9,1},{17,25},{25,17},{2,10},{10... | collective-permute-start | bytes 3932168 | tf_op jit(solution)/shard_map/ppermute | solution.py:397
  128.9 4.6 %collective-permute-start.6 = (bf16[4,272,128]{2,1,0:T(8,128)(2,1)}, bf16[4,272,128]{2,1,0:T(8,128)(2,1)S(1)}, u32[]{:S(2)}, u32[]{:S(2)}) collective-permute-start(bf16[4,272,128]{2,1,0:T(8,128)(2,1)} %get-tuple-element.88), channel_id=1, source_target_pairs={{8,0},{16,8},{24,16},{9,1},{17,9},{25,17},{10,2},{18,10},{26,18},{... | collective-permute-start | bytes 835592 | tf_op jit(solution)/shard_map/ppermute | solution.py:778
  137.2 37.5 %collective-permute-start.9 = (bf16[2,2,2,64,512]{4,3,0,1,2:T(8,128)(2,1)}, bf16[2,2,2,64,512]{4,3,0,1,2:T(8,128)(2,1)}, u32[]{:S(2)}, u32[]{:S(2)}) collective-permute-start(bf16[2,2,2,64,512]{4,3,0,1,2:T(8,128)(2,1)} %fusion.2), channel_id=1, source_target_pairs={{0,16},{8,24},{16,0},{24,8},{1,17},{9,25},{17,1},{25,9},{2,18},{10... | collective-permute-start | bytes 1572872 | tf_op jit(solution)/shard_map/ppermute | solution.py:397
  141.9 34.8 %collective-permute-start.10 = (bf16[2,2,2,80,512]{4,3,1,2,0:T(8,128)(2,1)}, bf16[2,2,2,80,512]{4,3,1,2,0:T(8,128)(2,1)S(1)}, u32[]{:S(2)}, u32[]{:S(2)}) collective-permute-start(bf16[2,2,2,80,512]{4,3,1,2,0:T(8,128)(2,1)} %fusion), channel_id=1, source_target_pairs={{0,1},{1,0},{2,3},{3,2},{4,5},{5,4},{6,7},{7,6},{8,9},{9,8},{10,11... | collective-permute-start | bytes 1966088 | tf_op jit(solution)/shard_map/ppermute | solution.py:397
  176.1 8.2 %collective-permute-start.11 = (bf16[2,2,64,512]{3,2,0,1:T(8,128)(2,1)S(1)}, bf16[2,2,64,512]{3,2,0,1:T(8,128)(2,1)S(1)}, u32[]{:S(2)}, u32[]{:S(2)}) collective-permute-start(bf16[2,2,64,512]{3,2,0,1:T(8,128)(2,1)S(1)} %get-tuple-element.154), channel_id=1, source_target_pairs={{0,1},{1,0},{2,3},{3,2},{4,5},{5,4},{6,7},{7,6},{8,9},{9,8},{10,11... | collective-permute-start | bytes 786440 | tf_op jit(solution)/shard_map/ppermute | solution.py:397
  176.9 9.3 %collective-permute-start.12 = (bf16[2,2,80,512]{3,2,0,1:T(8,128)(2,1)S(1)}, bf16[2,2,80,512]{3,2,0,1:T(8,128)(2,1)S(1)}, u32[]{:S(2)}, u32[]{:S(2)}) collective-permute-start(bf16[2,2,80,512]{3,2,0,1:T(8,128)(2,1)S(1)} %get-tuple-element.146), channel_id=1, source_target_pairs={{0,16},{8,24},{16,0},{24,8},{1,17},{9,25},{17,1},{25,9},{2,18},{10... | collective-permute-start | bytes 983048 | tf_op jit(solution)/shard_map/ppermute | solution.py:397
  186.5 9.6 %collective-permute-start.14 = (bf16[2,128,1536]{2,1,0:T(8,128)(2,1)S(1)}, bf16[2,128,1536]{2,1,0:T(8,128)(2,1)S(1)}, u32[]{:S(2)}, u32[]{:S(2)}) collective-permute-start(bf16[2,128,1536]{2,1,0:T(8,128)(2,1)S(1)} %get-tuple-element.144), channel_id=1, source_target_pairs={{0,8},{8,0},{16,24},{24,16},{1,9},{9,1},{17,25},{25,17},{2,10},{10... | collective-permute-start | bytes 2359304 | tf_op jit(solution)/shard_map/ppermute | solution.py:397
  186.6 9.6 %collective-permute-start.13 = (bf16[2,144,512]{2,1,0:T(8,128)(2,1)S(1)}, bf16[2,144,512]{2,1,0:T(8,128)(2,1)S(1)}, u32[]{:S(2)}, u32[]{:S(2)}) collective-permute-start(bf16[2,144,512]{2,1,0:T(8,128)(2,1)S(1)} %get-tuple-element.152), channel_id=1, source_target_pairs={{0,2},{1,3},{2,0},{3,1},{4,6},{5,7},{6,4},{7,5},{8,10},{9,11},{10,... | collective-permute-start | bytes 884744 | tf_op jit(solution)/shard_map/ppermute | solution.py:397
  197.2 31.9 %all-to-all-start = ((bf16[16,16,1536]{2,1,0:T(8,128)(2,1)}), bf16[16,16,1536]{2,1,0:T(8,128)(2,1)S(1)}, u32[]{:S(2)}, u32[]{:S(2)}) async-start(bf16[16,16,1536]{2,1,0:T(8,128)(2,1)} %bitcast.41), calls=%async_computation | async-start | bytes 1572864 | tf_op jit(solution)/shard_map/all_to_all | solution.py:480
  213.6 31.7 %copy-start.25 = (f32[16,2]{0,1:T(2,128)S(1)}, f32[16,2]{0,1:T(2,128)}, u32[]{:S(2)}) copy-start(f32[16,2]{0,1:T(2,128)} %param.28) | copy-start | bytes 388
  213.6 31.7 %copy-start.26 = (f32[16,2]{0,1:T(2,128)S(1)}, f32[16,2]{0,1:T(2,128)}, u32[]{:S(2)}) copy-start(f32[16,2]{0,1:T(2,128)} %param.38) | copy-start | bytes 388
  213.6 31.7 %copy-start.27 = (f32[16,2]{0,1:T(2,128)S(1)}, f32[16,2]{0,1:T(2,128)}, u32[]{:S(2)}) copy-start(f32[16,2]{0,1:T(2,128)} %param.37) | copy-start | bytes 388
  213.6 32.3 %copy-start.5 = (f32[64,512]{1,0:T(8,128)S(1)}, f32[64,512]{1,0:T(8,128)}, u32[]{:S(2)}) copy-start(f32[64,512]{1,0:T(8,128)} %param.27) | copy-start | bytes 393220
  213.6 32.3 %copy-start.12 = (f32[64,512]{1,0:T(8,128)S(1)}, f32[64,512]{1,0:T(8,128)}, u32[]{:S(2)}) copy-start(f32[64,512]{1,0:T(8,128)} %param.36) | copy-start | bytes 393220
  213.6 32.3 %copy-start.13 = (f32[64,512]{1,0:T(8,128)S(1)}, f32[64,512]{1,0:T(8,128)}, u32[]{:S(2)}) copy-start(f32[64,512]{1,0:T(8,128)} %param.35) | copy-start | bytes 393220
  213.6 15.6 %collective-permute-start.15 = (bf16[144,512]{1,0:T(8,128)(2,1)S(1)}, bf16[144,512]{1,0:T(8,128)(2,1)S(1)}, u32[]{:S(2)}, u32[]{:S(2)}) collective-permute-start(bf16[144,512]{1,0:T(8,128)(2,1)S(1)} %get-tuple-element.159), channel_id=1, source_target_pairs={{0,4},{1,5},{2,6},{3,7},{4,0},{5,1},{6,2},{7,3},{8,12},{9,13},{10,... | collective-permute-start | bytes 442376 | tf_op jit(solution)/shard_map/ppermute | solution.py:397
  232.4 12.8 %copy-start.28 = (f32[2,16]{1,0:T(2,128)S(1)}, f32[2,16]{1,0:T(2,128)}, u32[]{:S(2)}) copy-start(f32[2,16]{1,0:T(2,128)} %get-tuple-element.120) | copy-start | bytes 388
  232.4 14.3 %copy-start.7 = (f32[16,2048]{1,0:T(8,128)S(1)}, f32[16,2048]{1,0:T(8,128)}, u32[]{:S(2)}) copy-start(f32[16,2048]{1,0:T(8,128)} %param.26) | copy-start | bytes 393220
  232.5 14.3 %copy-start.14 = (f32[16,2048]{1,0:T(8,128)S(1)}, f32[16,2048]{1,0:T(8,128)}, u32[]{:S(2)}) copy-start(f32[16,2048]{1,0:T(8,128)} %param.34) | copy-start | bytes 393220
  232.5 14.3 %copy-start.15 = (f32[16,2048]{1,0:T(8,128)S(1)}, f32[16,2048]{1,0:T(8,128)}, u32[]{:S(2)}) copy-start(f32[16,2048]{1,0:T(8,128)} %param.33) | copy-start | bytes 393220
  232.5 11.4 %all-to-all-start.1 = ((f32[32,8,128]{2,1,0:T(8,128)}), f32[32,8,128]{2,1,0:T(8,128)S(1)}, u32[]{:S(2)}, u32[]{:S(2)}) async-start(f32[32,8,128]{2,1,0:T(8,128)} %get-tuple-element.112), calls=%async_computation.1 | async-start | bytes 262144 | tf_op jit(solution)/shard_map/all_to_all | solution.py:486
  (18 other events, 103.3 us)
Sparse Core Ops, SparseCore 0:
  16.0 65.3 all-gather.2
